TPU v7x, 32 devices: a whole 2x2x4 slice. The times are simulated.
32 devices in a mesh: groups: 2 (over y), gx: 4 (over z), samples: 2 (over x), gy: 2 (over core).
Axes of the slice: x: 2, y: 2, z: 4, core: 2. Of those that a mesh axis runs over, the one named last changes fastest.
Arguments:
- seeds: int32 [16], P(('groups', 'samples')), parts along dimension 0, may hold values from 0 to 63
- wind_profiles: float32 [64, 3, 128], replicated, may hold values from 0.04 to 0.16
- gust: float32 [32, 128, 128], P('gx', 'gy'), may hold values from 0.5 to 1.5
- reaction: float32 [32, 128, 128], P('gx', 'gy'), may hold values from 0.05 to 0.25
- flags: int32 [16, 32, 128, 128], P(('groups', 'samples'), 'gx', 'gy'), parts along dimension 0, may hold values from 0 to 7
- mask: int32 [32, 128], P('gx', 'gy'), may hold values 0 or 1
- kernel: float32 [128], replicated, may hold values from -0.5 to 0.5
- states: bfloat16 [5, 16, 32, 128, 128], P(None, ('groups', 'samples'), 'gx', 'gy'), parts along dimension 1, may hold values from -4 to 4
Outputs:
- risk_map: float32 [64, 128], P(('groups', 'gx'), 'gy'), parts along dimension 0
- source_gradient: float32 [64, 128, 128], P(('groups', 'gx', 'samples'), 'gy'), parts along dimension 0
- initial_adjoint: float32 [16, 32, 128, 128], P(('groups', 'samples'), 'gx', 'gy'), parts along dimension 0
There are 2 independent parts, one for each index of `groups`. A program takes and returns all parts, laid end to end along the dimension named above; an argument that names none is the same for every part. Nothing has to cross between parts.
Inputs may be any that keep to these rules, and one draw needn't show every extreme that they name: `seeds`: each seed names a row of wind_profiles. `flags`: bit d of a flag is 1 where the cell's outflow along dimension d goes toward higher indices.
All inputs are finite; a program needn't handle non-finite values. No bound on the sum of `mask` on one device may be relied on, other than what follows from the above.
Results may differ from a plain program's by a relative error of at most 0.0003.
Values may be sent and summed in bfloat16 or wider, within the bound.
No kernel may reach another device: no remote copies, remote signals or barrier semaphores. Data moves between devices by JAX's collectives and lax.ppermute only.
A program may use at most 64 MiB of HBM per device.

v0:
```python
import jax
import jax.numpy as jnp
from jax import lax
from jax.sharding import PartitionSpec as P

STEPS = 4


DIFFUSION = 0.05
KURTOSIS_WEIGHT = 1.0


def with_halo(block, sides, width, periodic):
    for axis, dim in sides:
        count = lax.axis_size(axis)
        forward = [(i, i + 1) for i in range(count - 1)]
        if periodic:
            forward.append((count - 1, 0))
        backward = [(target, source) for source, target in forward]
        low = lax.ppermute(
            lax.slice_in_dim(block, block.shape[dim] - width, None, axis=dim), axis, forward
        )
        high = lax.ppermute(lax.slice_in_dim(block, 0, width, axis=dim), axis, backward)
        block = jnp.concatenate([low, block, high], axis=dim)
    return block


def bit_value(outflow_bits, component):
    return (outflow_bits // 2**component % 2).astype(jnp.float32)


def outflow_rates(profile, outflow_bits, gust):
    rates = []
    for component in range(3):
        speeds = profile[:, component][:, None, None, :] * gust
        toward = bit_value(outflow_bits, component)
        rates.append(speeds * toward)
        rates.append(speeds * (1.0 - toward))
    return rates


def vertical(adjoint, upward, downward):
    zero_rim = jnp.zeros(adjoint.shape[:-1] + (1,), jnp.float32)
    above = jnp.concatenate([adjoint[..., 1:], zero_rim], -1)
    below = jnp.concatenate([zero_rim, adjoint[..., :-1]], -1)
    rising = jnp.concatenate([adjoint[..., 1:] - adjoint[..., :-1], zero_rim], -1)
    falling = jnp.concatenate([zero_rim, adjoint[..., :-1] - adjoint[..., 1:]], -1)
    return upward * above + downward * below + DIFFUSION * (rising + falling)


def adjoint_step(adjoint, stored, rates, leaving, reaction):
    east_out, west_out, north_out, south_out, upward, downward = rates
    padded_first = with_halo(adjoint, (("gx", 1),), 1, True)
    padded_second = with_halo(adjoint, (("gy", 2),), 1, False)
    mixed = (
        (1.0 - leaving) * adjoint + east_out * padded_first[:, 2:] + west_out * padded_first[:, :-2]
    )
    mixed = mixed + north_out * padded_second[:, :, 2:] + south_out * padded_second[:, :, :-2]
    return mixed + vertical(adjoint, upward, downward) - 2.0 * reaction * stored * adjoint


def on_device(seeds, wind_profiles, gust, reaction, flags, mask, kernel, states):
    local_count = seeds.shape[0]
    sample_count = local_count * lax.axis_size("samples")
    receptor = mask.astype(jnp.float32)
    surface = jnp.sum(states[STEPS].astype(jnp.float32) * kernel, axis=-1)
    average = lax.psum(jnp.sum(surface, axis=0), "samples") / sample_count
    spread = surface - average
    third_moment, fourth_moment = lax.psum(
        (jnp.sum(spread**3, axis=0), jnp.sum(spread**4, axis=0)), "samples"
    )
    third_moment = third_moment / sample_count
    fourth_moment = fourth_moment / sample_count
    risk_map = receptor * (average + KURTOSIS_WEIGHT * fourth_moment)
    sensitivity = receptor * (
        1.0 / sample_count + 4.0 * KURTOSIS_WEIGHT / sample_count * (spread**3 - third_moment)
    )
    profile_table = wind_profiles.reshape(wind_profiles.shape[0], -1)
    selector = (
        seeds[:, None] == jnp.arange(profile_table.shape[0], dtype=jnp.int32)[None, :]
    ).astype(jnp.float32)
    profile = jnp.dot(
        selector, profile_table, precision=lax.Precision.HIGHEST, preferred_element_type=jnp.float32
    ).reshape(local_count, 3, -1)
    final_adjoint = sensitivity[..., None] * kernel
    rates = outflow_rates(profile, flags, gust)
    leaving = rates[0] + rates[1] + rates[2] + rates[3] + rates[4] + rates[5]
    adjoint = final_adjoint
    running = adjoint
    for back_step in range(STEPS - 1, -1, -1):
        adjoint = adjoint_step(
            adjoint, states[back_step].astype(jnp.float32), rates, leaving, reaction
        )
        if back_step > 0:
            running = running + adjoint
    partial_sum = jnp.sum(running, axis=0)
    summed = lax.psum(partial_sum, "samples")
    share_rows = summed.shape[0] // lax.axis_size("samples")
    source_gradient = lax.dynamic_slice_in_dim(
        summed, lax.axis_index("samples") * share_rows, share_rows, 0
    )
    return (risk_map, source_gradient, adjoint)


def solution(mesh):
    return jax.shard_map(
        on_device,
        mesh=mesh,
        in_specs=(
            P(("groups", "samples")),
            P(),
            P("gx", "gy", None),
            P("gx", "gy", None),
            P(("groups", "samples"), "gx", "gy", None),
            P("gx", "gy"),
            P(),
            P(None, ("groups", "samples"), "gx", "gy", None),
        ),
        out_specs=(
            P(("groups", "gx"), "gy"),
            P(("groups", "gx", "samples"), "gy", None),
            P(("groups", "samples"), "gx", "gy", None),
        ),
        check_vma=False,
    )
```

profile of v0, /device:TPU:0, one launch (start us, length us, event | category | flops | bytes accessed | tf_op | source)
XLA Modules:
  0.0 120.8 jit_solution(11222084866204335115)
XLA Ops:
  7.2 1.5 %fusion.53 = (f32[8,64]{1,0:T(8,128)S(1)}, f32[4,8,64]{2,1,0:T(8,128)S(1)}) fusion(f32[128]{0:T(128)} %param.14, bf16[5,4,8,64,128]{4,3,2,1,0:T(8,128)(2,1)} %param.15), kind=kLoop, calls=%fused_computation.97 | loop fusion | flops 1046016 | bytes 535040 | tf_op jit(solution)/shard_map/reduce_sum | solution.py:67
  8.7 5.8 %psum.28 = f32[8,64]{1,0:T(8,128)S(1)} all-reduce(f32[8,64]{1,0:T(8,128)S(1)} %get-tuple-element.3), channel_id=1, replica_groups=mesh['groups'=2,'gx'=4,'samples'=2,'gy'=2] {'samples'}, use_global_device_ids=true, to_apply=%region_1.0 | all-reduce | flops 512 | bytes 4096 | tf_op jit(solution)/shard_map/psum | solution.py:67
  14.6 5.0 %all-reduce.16 = (f32[8,64]{1,0:T(8,128)S(1)}, f32[8,64]{1,0:T(8,128)S(1)}) all-reduce(f32[8,64]{1,0:T(8,128)S(1)} %get-tuple-element.6, f32[8,64]{1,0:T(8,128)S(1)} %get-tuple-element.5), channel_id=1, replica_groups=mesh['groups'=2,'gx'=4,'samples'=2,'gy'=2] {'samples'}, use_global_device_ids=true, to_apply=%region_4.0 | all-reduce | flops 1024 | bytes 8192 | tf_op jit(solution)/shard_map/psum | solution.py:69
  22.0 1.3 %collective-permute-start.3 = (f32[4,8,1,128]{3,2,1,0:T(1,128)}, f32[4,8,1,128]{3,2,1,0:T(1,128)S(1)}, u32[]{:S(2)}, u32[]{:S(2)}) collective-permute-start(f32[4,8,1,128]{3,2,1,0:T(1,128)} %get-tuple-element.42), channel_id=1, source_target_pairs={{0,1},{2,3},{4,5},{6,7},{8,9},{10,11},{12,13},{14,15},{16,17},{18,... | collective-permute-start | bytes 49160 | tf_op jit(solution)/shard_map/ppermute | solution.py:20
  23.3 1.3 %collective-permute-start.2 = (f32[4,8,1,128]{3,2,1,0:T(1,128)}, f32[4,8,1,128]{3,2,1,0:T(1,128)}, u32[]{:S(2)}, u32[]{:S(2)}) collective-permute-start(f32[4,8,1,128]{3,2,1,0:T(1,128)} %get-tuple-element.41), channel_id=1, source_target_pairs={{1,0},{3,2},{5,4},{7,6},{9,8},{11,10},{13,12},{15,14},{17,16},{19,... | collective-permute-start | bytes 49160 | tf_op jit(solution)/shard_map/ppermute | solution.py:23
  25.3 2.1 %collective-permute-start.1 = (f32[4,1,64,128]{3,2,1,0:T(8,128)}, f32[4,1,64,128]{3,2,1,0:T(8,128)}, u32[]{:S(2)}, u32[]{:S(2)}) collective-permute-start(f32[4,1,64,128]{3,2,1,0:T(8,128)} %get-tuple-element.40), channel_id=1, source_target_pairs={{0,4},{4,8},{8,12},{12,0},{1,5},{5,9},{9,13},{13,1},{2,6},{6,10},{... | collective-permute-start | bytes 393224 | tf_op jit(solution)/shard_map/ppermute | solution.py:20
  27.4 2.1 %collective-permute-start = (f32[4,1,64,128]{3,2,1,0:T(8,128)}, f32[4,1,64,128]{3,2,1,0:T(8,128)}, u32[]{:S(2)}, u32[]{:S(2)}) collective-permute-start(f32[4,1,64,128]{3,2,1,0:T(8,128)} %get-tuple-element.39), channel_id=1, source_target_pairs={{4,0},{8,4},{12,8},{0,12},{5,1},{9,5},{13,9},{1,13},{6,2},{10,6},{... | collective-permute-start | bytes 393224 | tf_op jit(solution)/shard_map/ppermute | solution.py:23
  29.5 2.1 %fusion.74 = (f32[4,8,64,127]{3,2,1,0:T(8,128)S(1)}, f32[4,8,64,127]{3,2,1,0:T(8,128)}, f32[4,8,64,127]{3,2,1,0:T(8,128)}, f32[4,8,64,127]{3,2,1,0:T(8,128)}) fusion(f32[4,8,64,128]{3,2,1,0:T(8,128)S(1)} %broadcast_multiply_fusion), kind=kLoop, calls=%fused_computation.140 | loop fusion | flops 520192 | bytes 6242304 | tf_op jit(solution)/shard_map/slice | solution.py:44
  33.2 3.7 %collective-permute-done = f32[4,1,64,128]{3,2,1,0:T(8,128)} collective-permute-done((f32[4,1,64,128]{3,2,1,0:T(8,128)}, f32[4,1,64,128]{3,2,1,0:T(8,128)}, u32[]{:S(2)}, u32[]{:S(2)}) %collective-permute-start) | collective-permute-done | bytes 131104 | tf_op jit(solution)/shard_map/ppermute | solution.py:23
  36.8 5.9 %fusion.5 = f32[4,8,64,128]{3,2,1,0:T(8,128)S(1)} fusion(f32[4,8,64,128]{3,2,1,0:T(8,128)S(1)} %broadcast_multiply_fusion, f32[4,8,1,128]{3,2,1,0:T(1,128)S(1)} %collective-permute-done.3, f32[4,8,1,128]{3,2,1,0:T(1,128)} %collective-permute-done.2, f32[4,1,64,128]{3,2,1,0:T(8,128)} %collective-permute-done.1, f32[4,1,64,128]{3,2,1,0:T(8,128)} %collective-permute-done, ...), kind=kLoop, calls=%fused_computation.28 | loop fusion | flops 25427968 | bytes 8665600 | tf_op jit(solution)/shard_map/sub | solution.py:59
  42.8 2.0 %collective-permute-start.7 = (f32[4,8,1,128]{3,2,1,0:T(1,128)S(1)}, f32[4,8,1,128]{3,2,1,0:T(1,128)S(1)}, u32[]{:S(2)}, u32[]{:S(2)}) collective-permute-start(f32[4,8,1,128]{3,2,1,0:T(1,128)S(1)} %get-tuple-element.34), channel_id=1, source_target_pairs={{0,1},{2,3},{4,5},{6,7},{8,9},{10,11},{12,13},{14,15},{16,17},{18,... | collective-permute-start | bytes 49160 | tf_op jit(solution)/shard_map/ppermute | solution.py:20
  44.8 1.3 %collective-permute-start.6 = (f32[4,8,1,128]{3,2,1,0:T(1,128)S(1)}, f32[4,8,1,128]{3,2,1,0:T(1,128)S(1)}, u32[]{:S(2)}, u32[]{:S(2)}) collective-permute-start(f32[4,8,1,128]{3,2,1,0:T(1,128)S(1)} %get-tuple-element.33), channel_id=1, source_target_pairs={{1,0},{3,2},{5,4},{7,6},{9,8},{11,10},{13,12},{15,14},{17,16},{19,... | collective-permute-start | bytes 49160 | tf_op jit(solution)/shard_map/ppermute | solution.py:23
  46.7 3.3 %collective-permute-start.4 = (f32[4,1,64,128]{3,2,1,0:T(8,128)S(1)}, f32[4,1,64,128]{3,2,1,0:T(8,128)S(1)}, u32[]{:S(2)}, u32[]{:S(2)}) collective-permute-start(f32[4,1,64,128]{3,2,1,0:T(8,128)S(1)} %get-tuple-element.31), channel_id=1, source_target_pairs={{4,0},{8,4},{12,8},{0,12},{5,1},{9,5},{13,9},{1,13},{6,2},{10,6},{... | collective-permute-start | bytes 393224 | tf_op jit(solution)/shard_map/ppermute | solution.py:23
  50.5 3.8 %collective-permute-done.5 = f32[4,1,64,128]{3,2,1,0:T(8,128)S(1)} collective-permute-done((f32[4,1,64,128]{3,2,1,0:T(8,128)S(1)}, f32[4,1,64,128]{3,2,1,0:T(8,128)S(1)}, u32[]{:S(2)}, u32[]{:S(2)}) %collective-permute-start.5) | collective-permute-done | bytes 131104 | tf_op jit(solution)/shard_map/ppermute | solution.py:20
  54.3 1.4 %collective-permute-done.4 = f32[4,1,64,128]{3,2,1,0:T(8,128)S(1)} collective-permute-done((f32[4,1,64,128]{3,2,1,0:T(8,128)S(1)}, f32[4,1,64,128]{3,2,1,0:T(8,128)S(1)}, u32[]{:S(2)}, u32[]{:S(2)}) %collective-permute-start.4) | collective-permute-done | bytes 131104 | tf_op jit(solution)/shard_map/ppermute | solution.py:23
  55.8 5.1 %fusion.38 = f32[4,8,64,128]{3,2,1,0:T(8,128)S(1)} fusion(f32[4,8,64,128]{3,2,1,0:T(8,128)S(1)} %fusion.5, f32[4,8,1,128]{3,2,1,0:T(1,128)S(1)} %collective-permute-done.7, f32[4,8,1,128]{3,2,1,0:T(1,128)S(1)} %collective-permute-done.6, f32[4,1,64,128]{3,2,1,0:T(8,128)S(1)} %collective-permute-done.5, f32[4,1,64,128]{3,2,1,0:T(8,128)S(1)} %collective-permute-done.4, ...), kind=kLoop, calls=%fused_computation.70 | loop fusion | flops 25165824 | bytes 8656896 | tf_op jit(solution)/shard_map/sub | solution.py:59
  60.9 1.9 %collective-permute-start.11 = (f32[4,8,1,128]{3,2,1,0:T(1,128)S(1)}, f32[4,8,1,128]{3,2,1,0:T(1,128)S(1)}, u32[]{:S(2)}, u32[]{:S(2)}) collective-permute-start(f32[4,8,1,128]{3,2,1,0:T(1,128)S(1)} %get-tuple-element.22), channel_id=1, source_target_pairs={{0,1},{2,3},{4,5},{6,7},{8,9},{10,11},{12,13},{14,15},{16,17},{18,... | collective-permute-start | bytes 49160 | tf_op jit(solution)/shard_map/ppermute | solution.py:20
  62.8 1.3 %collective-permute-start.10 = (f32[4,8,1,128]{3,2,1,0:T(1,128)S(1)}, f32[4,8,1,128]{3,2,1,0:T(1,128)S(1)}, u32[]{:S(2)}, u32[]{:S(2)}) collective-permute-start(f32[4,8,1,128]{3,2,1,0:T(1,128)S(1)} %get-tuple-element.21), channel_id=1, source_target_pairs={{1,0},{3,2},{5,4},{7,6},{9,8},{11,10},{13,12},{15,14},{17,16},{19,... | collective-permute-start | bytes 49160 | tf_op jit(solution)/shard_map/ppermute | solution.py:23
  65.0 3.0 %collective-permute-start.8 = (f32[4,1,64,128]{3,2,1,0:T(8,128)S(1)}, f32[4,1,64,128]{3,2,1,0:T(8,128)S(1)}, u32[]{:S(2)}, u32[]{:S(2)}) collective-permute-start(f32[4,1,64,128]{3,2,1,0:T(8,128)S(1)} %get-tuple-element.19), channel_id=1, source_target_pairs={{4,0},{8,4},{12,8},{0,12},{5,1},{9,5},{13,9},{1,13},{6,2},{10,6},{... | collective-permute-start | bytes 393224 | tf_op jit(solution)/shard_map/ppermute | solution.py:23
  68.6 3.8 %collective-permute-done.9 = f32[4,1,64,128]{3,2,1,0:T(8,128)S(1)} collective-permute-done((f32[4,1,64,128]{3,2,1,0:T(8,128)S(1)}, f32[4,1,64,128]{3,2,1,0:T(8,128)S(1)}, u32[]{:S(2)}, u32[]{:S(2)}) %collective-permute-start.9) | collective-permute-done | bytes 131104 | tf_op jit(solution)/shard_map/ppermute | solution.py:20
  72.3 1.7 %collective-permute-done.8 = f32[4,1,64,128]{3,2,1,0:T(8,128)S(1)} collective-permute-done((f32[4,1,64,128]{3,2,1,0:T(8,128)S(1)}, f32[4,1,64,128]{3,2,1,0:T(8,128)S(1)}, u32[]{:S(2)}, u32[]{:S(2)}) %collective-permute-start.8) | collective-permute-done | bytes 131104 | tf_op jit(solution)/shard_map/ppermute | solution.py:23
  74.0 6.1 %fusion.8 = (f32[8,64,128]{2,1,0:T(8,128)}, f32[4,8,64,128]{3,2,1,0:T(8,128)S(1)}) fusion(f32[4,8,64,128]{3,2,1,0:T(8,128)S(1)} %fusion.38, f32[4,8,64,128]{3,2,1,0:T(8,128)S(1)} %fusion.5, f32[4,8,64]{2,1,0:T(8,128)S(1)} %add_multiply_fusion, f32[128]{0:T(128)S(1)} %copy-done.5, bf16[5,4,8,64,128]{4,3,2,1,0:T(8,128)(2,1)} %param.15, ...), kind=kLoop, calls=%fused_computation.31 | loop fusion | flops 26411008 | bytes 9976320 | tf_op jit(solution)/shard_map/reduce_sum | solution.py:96
  81.4 1.9 %collective-permute-start.15 = (f32[4,8,1,128]{3,2,1,0:T(1,128)}, f32[4,8,1,128]{3,2,1,0:T(1,128)S(1)}, u32[]{:S(2)}, u32[]{:S(2)}) collective-permute-start(f32[4,8,1,128]{3,2,1,0:T(1,128)} %get-tuple-element.18), channel_id=1, source_target_pairs={{0,1},{2,3},{4,5},{6,7},{8,9},{10,11},{12,13},{14,15},{16,17},{18,... | collective-permute-start | bytes 49160 | tf_op jit(solution)/shard_map/ppermute | solution.py:20
  83.3 1.3 %collective-permute-start.14 = (f32[4,8,1,128]{3,2,1,0:T(1,128)}, f32[4,8,1,128]{3,2,1,0:T(1,128)S(1)}, u32[]{:S(2)}, u32[]{:S(2)}) collective-permute-start(f32[4,8,1,128]{3,2,1,0:T(1,128)} %get-tuple-element.17), channel_id=1, source_target_pairs={{1,0},{3,2},{5,4},{7,6},{9,8},{11,10},{13,12},{15,14},{17,16},{19,... | collective-permute-start | bytes 49160 | tf_op jit(solution)/shard_map/ppermute | solution.py:23
  84.6 1.9 %collective-permute-start.13 = (f32[4,1,64,128]{3,2,1,0:T(8,128)}, f32[4,1,64,128]{3,2,1,0:T(8,128)}, u32[]{:S(2)}, u32[]{:S(2)}) collective-permute-start(f32[4,1,64,128]{3,2,1,0:T(8,128)} %get-tuple-element.16), channel_id=1, source_target_pairs={{0,4},{4,8},{8,12},{12,0},{1,5},{5,9},{9,13},{13,1},{2,6},{6,10},{... | collective-permute-start | bytes 393224 | tf_op jit(solution)/shard_map/ppermute | solution.py:20
  86.5 2.0 %collective-permute-start.12 = (f32[4,1,64,128]{3,2,1,0:T(8,128)}, f32[4,1,64,128]{3,2,1,0:T(8,128)}, u32[]{:S(2)}, u32[]{:S(2)}) collective-permute-start(f32[4,1,64,128]{3,2,1,0:T(8,128)} %get-tuple-element.15), channel_id=1, source_target_pairs={{4,0},{8,4},{12,8},{0,12},{5,1},{9,5},{13,9},{1,13},{6,2},{10,6},{... | collective-permute-start | bytes 393224 | tf_op jit(solution)/shard_map/ppermute | solution.py:23
  88.5 2.0 %fusion.65 = (f32[4,8,64,127]{3,2,1,0:T(8,128)S(1)}, f32[4,8,64,127]{3,2,1,0:T(8,128)}, f32[4,8,64,127]{3,2,1,0:T(8,128)}, f32[4,8,64,127]{3,2,1,0:T(8,128)}) fusion(f32[4,8,64,128]{3,2,1,0:T(8,128)S(1)} %get-tuple-element.10), kind=kLoop, calls=%fused_computation.131 | loop fusion | flops 520192 | bytes 6242304 | tf_op jit(solution)/shard_map/slice | solution.py:44
  90.6 2.6 %collective-permute-done.13 = f32[4,1,64,128]{3,2,1,0:T(8,128)} collective-permute-done((f32[4,1,64,128]{3,2,1,0:T(8,128)}, f32[4,1,64,128]{3,2,1,0:T(8,128)}, u32[]{:S(2)}, u32[]{:S(2)}) %collective-permute-start.13) | collective-permute-done | bytes 131104 | tf_op jit(solution)/shard_map/ppermute | solution.py:20
  93.1 2.7 %collective-permute-done.12 = f32[4,1,64,128]{3,2,1,0:T(8,128)} collective-permute-done((f32[4,1,64,128]{3,2,1,0:T(8,128)}, f32[4,1,64,128]{3,2,1,0:T(8,128)}, u32[]{:S(2)}, u32[]{:S(2)}) %collective-permute-start.12) | collective-permute-done | bytes 131104 | tf_op jit(solution)/shard_map/ppermute | solution.py:23
  95.9 6.5 %fusion.18 = f32[4,8,64,128]{3,2,1,0:T(8,128)} fusion(f32[4,8,64,128]{3,2,1,0:T(8,128)S(1)} %get-tuple-element.10, f32[4,8,1,128]{3,2,1,0:T(1,128)S(1)} %collective-permute-done.15, f32[4,8,1,128]{3,2,1,0:T(1,128)S(1)} %collective-permute-done.14, f32[4,1,64,128]{3,2,1,0:T(8,128)} %collective-permute-done.13, f32[4,1,64,128]{3,2,1,0:T(8,128)} %collective-permute-done.12, ...), kind=kLoop, calls=%fused_computation.42 | loop fusion | flops 25165824 | bytes 8656896 | tf_op jit(solution)/shard_map/sub | solution.py:59
  102.4 10.0 %all-reduce.19.cloned.1.call-done = f32[8,64,128]{2,1,0:T(8,128)} async-done(((f32[8,64,128]{2,1,0:T(8,128)}), f32[8,64,128]{2,1,0:T(8,128)}) %all-reduce.19.cloned.1.call-update) | async-done | bytes 262160 | tf_op jit(solution)/shard_map/psum | solution.py:97
  112.3 1.6 %constant_dynamic-slice_fusion = f32[4,64,128]{2,1,0:T(8,128)} fusion(f32[8,64,128]{2,1,0:T(8,128)} %all-reduce.19.cloned.1.call-done, s32[]{:T(128)S(6)} %select_n.32), kind=kLoop, calls=%fused_computation.122 | loop fusion | bytes 262148 | tf_op jit(solution)/shard_map/dynamic_slice | solution.py:99
  (47 shorter events, 8.7 us)
Async XLA Ops:
  7.2 25.0 %copy-start = (f32[64,3,128]{2,0,1:T(8,128)S(1)}, f32[64,3,128]{2,0,1:T(8,128)}, u32[]{:S(2)}) copy-start(f32[64,3,128]{2,0,1:T(8,128)} %param.9) | copy-start | bytes 294916
  7.2 105.2 %all-reduce.19.cloned.1.call-start = ((), (), s32[]{:S(2)}) async-start(), calls=%async_computation | async-start | bytes 524288 | tf_op jit(solution)/shard_map/psum | solution.py:97
  22.0 10.4 %collective-permute-start.3 = (f32[4,8,1,128]{3,2,1,0:T(1,128)}, f32[4,8,1,128]{3,2,1,0:T(1,128)S(1)}, u32[]{:S(2)}, u32[]{:S(2)}) collective-permute-start(f32[4,8,1,128]{3,2,1,0:T(1,128)} %get-tuple-element.42), channel_id=1, source_target_pairs={{0,1},{2,3},{4,5},{6,7},{8,9},{10,11},{12,13},{14,15},{16,17},{18,... | collective-permute-start | bytes 49160 | tf_op jit(solution)/shard_map/ppermute | solution.py:20
  23.3 9.2 %collective-permute-start.2 = (f32[4,8,1,128]{3,2,1,0:T(1,128)}, f32[4,8,1,128]{3,2,1,0:T(1,128)}, u32[]{:S(2)}, u32[]{:S(2)}) collective-permute-start(f32[4,8,1,128]{3,2,1,0:T(1,128)} %get-tuple-element.41), channel_id=1, source_target_pairs={{1,0},{3,2},{5,4},{7,6},{9,8},{11,10},{13,12},{15,14},{17,16},{19,... | collective-permute-start | bytes 49160 | tf_op jit(solution)/shard_map/ppermute | solution.py:23
  25.3 7.9 %collective-permute-start.1 = (f32[4,1,64,128]{3,2,1,0:T(8,128)}, f32[4,1,64,128]{3,2,1,0:T(8,128)}, u32[]{:S(2)}, u32[]{:S(2)}) collective-permute-start(f32[4,1,64,128]{3,2,1,0:T(8,128)} %get-tuple-element.40), channel_id=1, source_target_pairs={{0,4},{4,8},{8,12},{12,0},{1,5},{5,9},{9,13},{13,1},{2,6},{6,10},{... | collective-permute-start | bytes 393224 | tf_op jit(solution)/shard_map/ppermute | solution.py:20
  27.4 4.2 %copy-start.4 = (s32[8,64]{1,0:T(8,128)S(1)}, s32[8,64]{1,0:T(8,128)}, u32[]{:S(2)}) copy-start(s32[8,64]{1,0:T(8,128)} %param.13) | copy-start | bytes 6148
  27.4 4.8 %copy-start.3 = (f32[8,64,128]{2,1,0:T(8,128)S(1)}, f32[8,64,128]{2,1,0:T(8,128)}, u32[]{:S(2)}) copy-start(f32[8,64,128]{2,1,0:T(8,128)} %param.11) | copy-start | bytes 786436
  27.4 4.8 %copy-start.6 = (s32[4]{0:T(128)S(1)}, s32[4]{0:T(128)}, u32[]{:S(2)}) copy-start(s32[4]{0:T(128)} %param.8) | copy-start | bytes 52
  27.4 9.5 %copy-start.1 = (s32[4,8,64,128]{3,2,1,0:T(8,128)S(1)}, s32[4,8,64,128]{3,2,1,0:T(8,128)}, u32[]{:S(2)}) copy-start(s32[4,8,64,128]{3,2,1,0:T(8,128)} %param.12) | copy-start | bytes 3145732
  27.4 9.4 %copy-start.5 = (f32[128]{0:T(128)S(1)}, f32[128]{0:T(128)}, u32[]{:S(2)}) copy-start(f32[128]{0:T(128)} %param.14) | copy-start | bytes 1540
  27.4 9.4 %collective-permute-start = (f32[4,1,64,128]{3,2,1,0:T(8,128)}, f32[4,1,64,128]{3,2,1,0:T(8,128)}, u32[]{:S(2)}, u32[]{:S(2)}) collective-permute-start(f32[4,1,64,128]{3,2,1,0:T(8,128)} %get-tuple-element.39), channel_id=1, source_target_pairs={{4,0},{8,4},{12,8},{0,12},{5,1},{9,5},{13,9},{1,13},{6,2},{10,6},{... | collective-permute-start | bytes 393224 | tf_op jit(solution)/shard_map/ppermute | solution.py:23
  42.8 7.7 %collective-permute-start.7 = (f32[4,8,1,128]{3,2,1,0:T(1,128)S(1)}, f32[4,8,1,128]{3,2,1,0:T(1,128)S(1)}, u32[]{:S(2)}, u32[]{:S(2)}) collective-permute-start(f32[4,8,1,128]{3,2,1,0:T(1,128)S(1)} %get-tuple-element.34), channel_id=1, source_target_pairs={{0,1},{2,3},{4,5},{6,7},{8,9},{10,11},{12,13},{14,15},{16,17},{18,... | collective-permute-start | bytes 49160 | tf_op jit(solution)/shard_map/ppermute | solution.py:20
  44.8 5.7 %collective-permute-start.6 = (f32[4,8,1,128]{3,2,1,0:T(1,128)S(1)}, f32[4,8,1,128]{3,2,1,0:T(1,128)S(1)}, u32[]{:S(2)}, u32[]{:S(2)}) collective-permute-start(f32[4,8,1,128]{3,2,1,0:T(1,128)S(1)} %get-tuple-element.33), channel_id=1, source_target_pairs={{1,0},{3,2},{5,4},{7,6},{9,8},{11,10},{13,12},{15,14},{17,16},{19,... | collective-permute-start | bytes 49160 | tf_op jit(solution)/shard_map/ppermute | solution.py:23
  46.1 8.2 %collective-permute-start.5 = (f32[4,1,64,128]{3,2,1,0:T(8,128)S(1)}, f32[4,1,64,128]{3,2,1,0:T(8,128)S(1)}, u32[]{:S(2)}, u32[]{:S(2)}) collective-permute-start(f32[4,1,64,128]{3,2,1,0:T(8,128)S(1)} %get-tuple-element.32), channel_id=1, source_target_pairs={{0,4},{4,8},{8,12},{12,0},{1,5},{5,9},{9,13},{13,1},{2,6},{6,10},{... | collective-permute-start | bytes 393224 | tf_op jit(solution)/shard_map/ppermute | solution.py:20
  46.7 9.1 %copy-start.2 = (f32[8,64,128]{2,1,0:T(8,128)S(1)}, f32[8,64,128]{2,1,0:T(8,128)}, u32[]{:S(2)}) copy-start(f32[8,64,128]{2,1,0:T(8,128)} %param.10) | copy-start | bytes 786436
  46.7 9.1 %collective-permute-start.4 = (f32[4,1,64,128]{3,2,1,0:T(8,128)S(1)}, f32[4,1,64,128]{3,2,1,0:T(8,128)S(1)}, u32[]{:S(2)}, u32[]{:S(2)}) collective-permute-start(f32[4,1,64,128]{3,2,1,0:T(8,128)S(1)} %get-tuple-element.31), channel_id=1, source_target_pairs={{4,0},{8,4},{12,8},{0,12},{5,1},{9,5},{13,9},{1,13},{6,2},{10,6},{... | collective-permute-start | bytes 393224 | tf_op jit(solution)/shard_map/ppermute | solution.py:23
  60.9 7.6 %collective-permute-start.11 = (f32[4,8,1,128]{3,2,1,0:T(1,128)S(1)}, f32[4,8,1,128]{3,2,1,0:T(1,128)S(1)}, u32[]{:S(2)}, u32[]{:S(2)}) collective-permute-start(f32[4,8,1,128]{3,2,1,0:T(1,128)S(1)} %get-tuple-element.22), channel_id=1, source_target_pairs={{0,1},{2,3},{4,5},{6,7},{8,9},{10,11},{12,13},{14,15},{16,17},{18,... | collective-permute-start | bytes 49160 | tf_op jit(solution)/shard_map/ppermute | solution.py:20
  62.8 5.8 %collective-permute-start.10 = (f32[4,8,1,128]{3,2,1,0:T(1,128)S(1)}, f32[4,8,1,128]{3,2,1,0:T(1,128)S(1)}, u32[]{:S(2)}, u32[]{:S(2)}) collective-permute-start(f32[4,8,1,128]{3,2,1,0:T(1,128)S(1)} %get-tuple-element.21), channel_id=1, source_target_pairs={{1,0},{3,2},{5,4},{7,6},{9,8},{11,10},{13,12},{15,14},{17,16},{19,... | collective-permute-start | bytes 49160 | tf_op jit(solution)/shard_map/ppermute | solution.py:23
  64.1 8.2 %collective-permute-start.9 = (f32[4,1,64,128]{3,2,1,0:T(8,128)S(1)}, f32[4,1,64,128]{3,2,1,0:T(8,128)S(1)}, u32[]{:S(2)}, u32[]{:S(2)}) collective-permute-start(f32[4,1,64,128]{3,2,1,0:T(8,128)S(1)} %get-tuple-element.20), channel_id=1, source_target_pairs={{0,4},{4,8},{8,12},{12,0},{1,5},{5,9},{9,13},{13,1},{2,6},{6,10},{... | collective-permute-start | bytes 393224 | tf_op jit(solution)/shard_map/ppermute | solution.py:20
  65.0 9.1 %collective-permute-start.8 = (f32[4,1,64,128]{3,2,1,0:T(8,128)S(1)}, f32[4,1,64,128]{3,2,1,0:T(8,128)S(1)}, u32[]{:S(2)}, u32[]{:S(2)}) collective-permute-start(f32[4,1,64,128]{3,2,1,0:T(8,128)S(1)} %get-tuple-element.19), channel_id=1, source_target_pairs={{4,0},{8,4},{12,8},{0,12},{5,1},{9,5},{13,9},{1,13},{6,2},{10,6},{... | collective-permute-start | bytes 393224 | tf_op jit(solution)/shard_map/ppermute | solution.py:23
  81.4 9.1 %collective-permute-start.15 = (f32[4,8,1,128]{3,2,1,0:T(1,128)}, f32[4,8,1,128]{3,2,1,0:T(1,128)S(1)}, u32[]{:S(2)}, u32[]{:S(2)}) collective-permute-start(f32[4,8,1,128]{3,2,1,0:T(1,128)} %get-tuple-element.18), channel_id=1, source_target_pairs={{0,1},{2,3},{4,5},{6,7},{8,9},{10,11},{12,13},{14,15},{16,17},{18,... | collective-permute-start | bytes 49160 | tf_op jit(solution)/shard_map/ppermute | solution.py:20
  83.3 7.3 %collective-permute-start.14 = (f32[4,8,1,128]{3,2,1,0:T(1,128)}, f32[4,8,1,128]{3,2,1,0:T(1,128)S(1)}, u32[]{:S(2)}, u32[]{:S(2)}) collective-permute-start(f32[4,8,1,128]{3,2,1,0:T(1,128)} %get-tuple-element.17), channel_id=1, source_target_pairs={{1,0},{3,2},{5,4},{7,6},{9,8},{11,10},{13,12},{15,14},{17,16},{19,... | collective-permute-start | bytes 49160 | tf_op jit(solution)/shard_map/ppermute | solution.py:23
  84.6 8.5 %collective-permute-start.13 = (f32[4,1,64,128]{3,2,1,0:T(8,128)}, f32[4,1,64,128]{3,2,1,0:T(8,128)}, u32[]{:S(2)}, u32[]{:S(2)}) collective-permute-start(f32[4,1,64,128]{3,2,1,0:T(8,128)} %get-tuple-element.16), channel_id=1, source_target_pairs={{0,4},{4,8},{8,12},{12,0},{1,5},{5,9},{9,13},{13,1},{2,6},{6,10},{... | collective-permute-start | bytes 393224 | tf_op jit(solution)/shard_map/ppermute | solution.py:20
  86.5 9.4 %collective-permute-start.12 = (f32[4,1,64,128]{3,2,1,0:T(8,128)}, f32[4,1,64,128]{3,2,1,0:T(8,128)}, u32[]{:S(2)}, u32[]{:S(2)}) collective-permute-start(f32[4,1,64,128]{3,2,1,0:T(8,128)} %get-tuple-element.15), channel_id=1, source_target_pairs={{4,0},{8,4},{12,8},{0,12},{5,1},{9,5},{13,9},{1,13},{6,2},{10,6},{... | collective-permute-start | bytes 393224 | tf_op jit(solution)/shard_map/ppermute | solution.py:23
Sparse Core Ops, SparseCore 0:
  90.7 21.6 all-reduce.18
where the time goes:
time: 121 us
  other arithmetic  32.5 us (27%)
  waiting for transfers between devices  30.4 us (25%)
  starting transfers between devices  28.1 us (23%)
  between operations  14.3 us (12%)
  blocking collectives  10.9 us (9%)
  local copies, waits for them, and re-layouts  4.39 us (4%)
    sub x3, other arithmetic, adjoint_step(): mixed + vertical(adjoint, upward, downward)  17.5 us
    ppermute x8, starting transfers between devices, with_halo(): lax.ppermute(lax.slice_in_dim(block, 0, width, axis=dim), axis, backward)  15.6 us
    ppermute x8, starting transfers between devices, with_halo(): lax.ppermute(lax.slice_in_dim(block, block.shape[dim] - width, None, axis...  12.5 us
    ppermute x8, waiting for transfers between devices, with_halo(): lax.ppermute(lax.slice_in_dim(block, block.shape[dim] - width, None, axis...  10.9 us
    psum x1, waiting for transfers between devices, on_device(): summed = lax.psum(partial_sum, 'samples')  9.96 us
    ppermute x8, waiting for transfers between devices, with_halo(): lax.ppermute(lax.slice_in_dim(block, 0, width, axis=dim), axis, backward)  9.5 us
    reduce_sum x1, other arithmetic, on_device(): partial_sum = jnp.sum(running, axis=0)  6.06 us
    psum x1, blocking collectives, on_device(): average = lax.psum(jnp.sum(surface, axis=0), 'samples') / sample_count  5.85 us
  transfers between devices with their start and end apart: 17, of which 9 were waited for; matrix products, arithmetic and copies ran while one was open for 11% of the time, Pallas kernels for 0%

commit v1 on v0

v1 whole, which is shorter than its diff:
```python
import functools

import jax
import jax.numpy as jnp
from jax import lax
from jax.experimental import pallas as pl
from jax.experimental.pallas import tpu as pltpu
from jax.sharding import PartitionSpec as P

STEPS = 4
DIFFUSION = 0.05
KURTOSIS_WEIGHT = 1.0

F32 = jnp.float32
BF16 = jnp.bfloat16
VMEM = pl.BlockSpec(memory_space=pltpu.VMEM)
ANY = pl.BlockSpec(memory_space=pl.ANY)


def call(body, outs, args, name, out_specs=None, in_specs=None, scratch=(), aliases=None, micros=1.0):
    return pl.pallas_call(
        body,
        name=name,
        out_shape=outs,
        in_specs=in_specs or [VMEM] * len(args),
        out_specs=out_specs or jax.tree.map(lambda _: VMEM, outs),
        scratch_shapes=scratch,
        input_output_aliases=aliases or {},
        compiler_params=pltpu.CompilerParams(vmem_limit_bytes=4 << 20),
        cost_estimate=pl.CostEstimate(
            flops=int(1e6 * micros), bytes_accessed=int(3e6 * micros), transcendentals=0
        ),
    )(*args)


def shape(*dims, dtype=F32):
    return jax.ShapeDtypeStruct(dims, dtype)


def three_parts(value):
    first = value.astype(BF16).astype(F32)
    second = (value - first).astype(BF16).astype(F32)
    third = value - first - second
    return first, second, third


def stack_rows(rows, width):
    index = lax.broadcasted_iota(jnp.int32, (16, width), 0)
    block = jnp.zeros((16, width), F32)
    for position, row in enumerate(rows):
        block = jnp.where(index == position, row, block)
    return block.astype(BF16)


def surface_body(states_ref, kernel_ref, out_ref):
    samples, rows, width, levels = states_ref.shape
    parts = stack_rows(three_parts(kernel_ref[...]), levels)
    for k in range(samples):
        flat = states_ref[k].reshape(rows * width, levels)
        product = lax.dot_general(
            parts, flat, (((1,), (1,)), ((), ())), preferred_element_type=F32
        )
        out_ref[k : k + 1] = product[0:1] + product[1:2] + product[2:3]


def outer_rows(row, kernel_rows):
    first, second, third = three_parts(row)
    left = stack_rows((first, first, first, second, second, third), row.shape[1])
    return lax.dot_general(
        left, kernel_rows, (((0,), (0,)), ((), ())), preferred_element_type=F32
    )


def kernel_rows_of(kernel_ref):
    first, second, third = three_parts(kernel_ref[...])
    return stack_rows((first, second, third, first, second, first), kernel_ref.shape[1])


def final_body(sens_ref, beside_ref, kernel_ref, side_ref, edge_ref, inner_ref, beside_out, run_edge_ref, run_inner_ref):
    samples, _, width, levels = edge_ref.shape
    rows = inner_ref.shape[1] + 2
    right = kernel_rows_of(kernel_ref)
    total = [jnp.zeros((width, levels), F32)] * rows
    lanes = lax.broadcasted_iota(jnp.int32, (rows, rows * width), 1)
    starts = lax.broadcasted_iota(jnp.int32, (rows, rows * width), 0) * width
    wanted = lanes == starts + jnp.where(side_ref[0, 0] > 0.5, width - 1, 0)
    for k in range(samples):
        block = outer_rows(sens_ref[k : k + 1], right)
        for x in range(rows):
            piece = block[x * width : (x + 1) * width]
            if x == 0:
                edge_ref[k, 0] = piece
            elif x == rows - 1:
                edge_ref[k, 1] = piece
            else:
                inner_ref[k, x - 1] = piece
            total[x] = total[x] + piece
        column = jnp.sum(jnp.where(wanted, beside_ref[k : k + 1], 0.0), axis=1, keepdims=True)
        beside_out[k] = column * kernel_ref[...]
    run_edge_ref[0] = total[0]
    run_edge_ref[1] = total[rows - 1]
    for x in range(1, rows - 1):
        run_inner_ref[x - 1] = total[x]


def halo_body(low_ref, high_ref, kernel_ref, low_out, high_out):
    right = kernel_rows_of(kernel_ref)
    for source, target in ((low_ref, low_out), (high_ref, high_out)):
        for k in range(target.shape[0]):
            target[k] = outer_rows(source[k : k + 1], right)


class Plan:
    def __init__(self, levels):
        lane = lax.broadcasted_iota(jnp.int32, (8, levels), 1)
        row = lax.broadcasted_iota(jnp.int32, (8, levels), 0)
        self.below_top = lane < levels - 1
        self.above_base = lane > 0
        self.top_row = row == 7
        self.base_row = row == 0
        self.loss = 1.0 - (
            jnp.where(self.below_top, DIFFUSION, 0.0) + jnp.where(self.above_base, DIFFUSION, 0.0)
        )


def step_row(plan, centre, west, east, low_row, high_row, bits, gust, twice, stored, speeds):
    width, levels = centre.shape
    tiles = width // 8
    first, second, third, whole = speeds
    piece = lambda value, t: value[8 * t : 8 * t + 8]
    parts = [piece(centre, t) for t in range(tiles)]
    up = [pltpu.roll(part, 7, 0) for part in parts] + [jnp.broadcast_to(high_row, (8, levels))]
    down = [jnp.broadcast_to(low_row, (8, levels))] + [pltpu.roll(part, 1, 0) for part in parts]
    result = []
    for t in range(tiles):
        here = parts[t]
        north = jnp.where(plan.top_row, up[t + 1], up[t])
        south = jnp.where(plan.base_row, down[t], down[t + 1])
        above = jnp.where(plan.below_top, pltpu.roll(here, levels - 1, 1), 0.0)
        below = jnp.where(plan.above_base, pltpu.roll(here, 1, 1), 0.0)
        flag = piece(bits, t)
        moved = (
            first * jnp.where((flag & 1) != 0, piece(east, t), piece(west, t))
            + second * jnp.where((flag & 2) != 0, north, south)
            + third * jnp.where((flag & 4) != 0, above, below)
            - whole * here
        )
        result.append(
            here * (plan.loss - piece(twice, t) * piece(stored, t))
            + piece(gust, t) * moved
            + DIFFUSION * (above + below)
        )
    return result


def speeds_of(profile_ref, k, levels):
    rows = [profile_ref[k, d : d + 1] for d in range(3)]
    rows.append(rows[0] + rows[1] + rows[2])
    return [jnp.broadcast_to(row, (8, levels)) for row in rows]


def inner_body(
    step, last, edge_ref, inner_ref, beside_ref, side_ref, run_ref, flags_ref, gust_ref, reaction_ref,
    states_ref, profile_ref, *outs
):
    samples, inside, width, levels = inner_ref.shape
    plan = Plan(levels)
    if last:
        target, buffer, semaphore = outs
    else:
        buffer, run_out = outs

    def at(k, x):
        return edge_ref[k, x // (inside + 1)] if x in (0, inside + 1) else inner_ref[k, x - 1]

    for x in range(1, inside + 1):
        gust = gust_ref[x]
        twice = 2.0 * reaction_ref[x]
        total = None if last else [run_ref[x - 1, 8 * t : 8 * t + 8] for t in range(width // 8)]
        for k in range(samples):
            halo = beside_ref[k, x : x + 1]
            tiles = step_row(
                plan, at(k, x), at(k, x - 1), at(k, x + 1), halo * side_ref[0:1], halo * side_ref[1:2],
                flags_ref[k, x], gust, twice, states_ref[step, k, x].astype(F32),
                speeds_of(profile_ref, k, levels),
            )
            for t, tile in enumerate(tiles):
                buffer[k, x - 1, 8 * t : 8 * t + 8] = tile
                if not last:
                    total[t] = total[t] + tile
        if not last:
            for t, tile in enumerate(total):
                run_out[x - 1, 8 * t : 8 * t + 8] = tile
    if last:
        copy = pltpu.make_async_copy(buffer, target.at[:, 1 : inside + 1], semaphore)
        copy.start()
        copy.wait()


def edge_body(
    step, last, edge_ref, inner_ref, low_ref, high_ref, beside_ref, side_ref, run_ref, flags_ref, gust_ref,
    reaction_ref, states_ref, profile_ref, now_ref, *outs
):
    samples, inside, width, levels = inner_ref.shape
    plan = Plan(levels)
    if last:
        target, buffer, semaphore = outs
    else:
        buffer, low_out, high_out, beside_out, run_out = outs
    for side, x in enumerate((0, inside + 1)):
        gust = gust_ref[x]
        twice = 2.0 * reaction_ref[x]
        total = None if last else [run_ref[side, 8 * t : 8 * t + 8] for t in range(width // 8)]
        for k in range(samples):
            halo = beside_ref[k, x : x + 1]
            if side == 0:
                west, east = low_ref[k].astype(F32), inner_ref[k, 0]
            else:
                west, east = inner_ref[k, inside - 1], high_ref[k].astype(F32)
            tiles = step_row(
                plan, edge_ref[k, side], west, east, halo * side_ref[0:1], halo * side_ref[1:2],
                flags_ref[k, x], gust, twice, states_ref[step, k, x].astype(F32),
                speeds_of(profile_ref, k, levels),
            )
            for t, tile in enumerate(tiles):
                buffer[k, side, 8 * t : 8 * t + 8] = tile
                if not last:
                    total[t] = total[t] + tile
            if not last:
                whole = jnp.concatenate(tiles, axis=0).astype(BF16)
                (low_out if side == 0 else high_out)[k] = whole
                rim = jnp.where(side_ref[0:1] > 0.5, tiles[0][0:1], tiles[-1][7:8])
                beside_out[k, x : x + 1] = rim
        if not last:
            for t, tile in enumerate(total):
                run_out[side, 8 * t : 8 * t + 8] = tile
    if last:
        copies = [
            pltpu.make_async_copy(buffer.at[:, 0], target.at[:, 0], semaphore.at[0]),
            pltpu.make_async_copy(buffer.at[:, 1], target.at[:, inside + 1], semaphore.at[1]),
        ]
        for copy in copies:
            copy.start()
        for copy in copies:
            copy.wait()
    else:
        for k in range(samples):
            for x in range(1, inside + 1):
                rim = jnp.where(side_ref[0:1] > 0.5, now_ref[k, x - 1, 0:1], now_ref[k, x - 1, width - 1 : width])
                beside_out[k, x : x + 1] = rim


def exchange_x(to_low, to_high):
    count = lax.axis_size("gx")
    forward = [(i, (i + 1) % count) for i in range(count)]
    backward = [(target, source) for source, target in forward]
    return lax.ppermute(to_high, "gx", forward), lax.ppermute(to_low, "gx", backward)


def swap_y(block):
    return lax.ppermute(block, "gy", [(0, 1), (1, 0)])


def on_device(seeds, wind_profiles, gust, reaction, flags, mask, kernel, states):
    local_count, rows, width, levels = flags.shape
    shards = lax.axis_size("samples")
    sample_count = local_count * shards
    inside = rows - 2
    kernel_row = kernel[None, :]
    side = jnp.broadcast_to(
        jnp.stack([lax.axis_index("gy") == 1, lax.axis_index("gy") == 0]).astype(F32)[:, None], (2, levels)
    )

    surface = call(
        surface_body, shape(local_count, rows * width), (states[STEPS], kernel_row), "surface"
    )
    others = [
        lax.ppermute(surface, "samples", [(i, (i + hop) % shards) for i in range(shards)])
        for hop in range(1, shards)
    ]
    every = jnp.concatenate([surface] + others, axis=0)
    receptor = mask.reshape(1, rows * width).astype(F32)
    average = jnp.sum(every, axis=0, keepdims=True) / sample_count
    spread = every - average
    cubed = spread * spread * spread
    third_moment = jnp.sum(cubed, axis=0, keepdims=True) / sample_count
    fourth_moment = jnp.sum(cubed * spread, axis=0, keepdims=True) / sample_count
    risk_map = (receptor * (average + KURTOSIS_WEIGHT * fourth_moment)).reshape(rows, width)
    sensitivity = receptor * (
        1.0 / sample_count
        + 4.0 * KURTOSIS_WEIGHT / sample_count * (cubed[:local_count] - third_moment)
    )

    profile_table = wind_profiles.reshape(wind_profiles.shape[0], -1)
    selector = (seeds[:, None] == jnp.arange(profile_table.shape[0], dtype=jnp.int32)[None, :]).astype(F32)
    profile = jnp.dot(
        selector, profile_table, precision=lax.Precision.HIGHEST, preferred_element_type=F32
    ).reshape(local_count, 3, levels)

    low_sens, high_sens = exchange_x(sensitivity[:, :width], sensitivity[:, (rows - 1) * width :])
    beside_sens = swap_y(sensitivity)
    edge, inner, beside, run_edge, run_inner = call(
        final_body,
        (
            shape(local_count, 2, width, levels),
            shape(local_count, inside, width, levels),
            shape(local_count, rows, levels),
            shape(2, width, levels),
            shape(inside, width, levels),
        ),
        (sensitivity, beside_sens, kernel_row, side),
        "final",
    )
    low, high = call(
        halo_body, (shape(local_count, width, levels),) * 2, (low_sens, high_sens, kernel_row), "halo"
    )
    fixed = (flags, gust, reaction, states, profile)
    for step in range(STEPS - 1, 0, -1):
        inner_now, run_inner = call(
            functools.partial(inner_body, step, False),
            (shape(local_count, inside, width, levels), shape(inside, width, levels)),
            (edge, inner, beside, side, run_inner) + fixed,
            f"inner{step}",
        )
        edge_now, to_low, to_high, to_beside, run_edge = call(
            functools.partial(edge_body, step, False),
            (
                shape(local_count, 2, width, levels),
                shape(local_count, width, levels, dtype=BF16),
                shape(local_count, width, levels, dtype=BF16),
                shape(local_count, rows, levels),
                shape(2, width, levels),
            ),
            (edge, inner, low, high, beside, side, run_edge) + fixed + (inner_now,),
            f"edge{step}",
            micros=0.4,
        )
        edge, inner = edge_now, inner_now
        low, high = exchange_x(to_low, to_high)
        beside = swap_y(to_beside)

    target = call(
        functools.partial(inner_body, 0, True),
        shape(*flags.shape),
        (edge, inner, beside, side, run_inner) + fixed,
        "inner0",
        out_specs=ANY,
        scratch=[pltpu.VMEM((local_count, inside, width, levels), F32), pltpu.SemaphoreType.DMA],
    )
    running = jnp.concatenate([run_edge[:1], run_inner, run_edge[1:]], axis=0)
    share_rows = rows // shards
    me = lax.axis_index("samples")
    source_gradient = lax.dynamic_slice_in_dim(running, me * share_rows, share_rows, 0)
    for hop in range(1, shards):
        to = (me + hop) % shards
        piece = lax.dynamic_slice_in_dim(running, to * share_rows, share_rows, 0)
        source_gradient = source_gradient + lax.ppermute(
            piece, "samples", [(i, (i + hop) % shards) for i in range(shards)]
        )
    args = (edge, inner, low, high, beside, side, run_edge) + fixed + (target,)
    initial_adjoint = call(
        functools.partial(edge_body, 0, True),
        shape(*flags.shape),
        args,
        "edge0",
        out_specs=ANY,
        in_specs=[VMEM] * (len(args) - 1) + [ANY],
        scratch=[pltpu.VMEM((local_count, 2, width, levels), F32), pltpu.SemaphoreType.DMA((2,))],
        aliases={len(args) - 1: 0},
        micros=0.4,
    )
    return risk_map, source_gradient, initial_adjoint


def solution(mesh):
    return jax.shard_map(
        on_device,
        mesh=mesh,
        in_specs=(
            P(("groups", "samples")),
            P(),
            P("gx", "gy", None),
            P("gx", "gy", None),
            P(("groups", "samples"), "gx", "gy", None),
            P("gx", "gy"),
            P(),
            P(None, ("groups", "samples"), "gx", "gy", None),
        ),
        out_specs=(
            P(("groups", "gx"), "gy"),
            P(("groups", "gx", "samples"), "gy", None),
            P(("groups", "samples"), "gx", "gy", None),
        ),
        check_vma=False,
    )
```

time: 121 us -> 56.2 us (0.46)
  other arithmetic: 32.5 us -> 2.73 us
  waiting for transfers between devices: 30.4 us -> 7.18 us
  between operations: 14.3 us -> 0.85 us
  blocking collectives: 10.9 us -> 0 us
  local copies, waits for them, and re-layouts: 4.39 us -> 14.6 us
  Pallas kernels: 0 us -> 9 us
  starting transfers between devices: 28.1 us -> 20.5 us
    sub x3 -> x0, other arithmetic: 17.5 us -> none  [adjoint_step(): mixed + vertical(adjoint, upward, downward)]
    ppermute x16 -> x14, waiting for transfers between devices: 20.4 us -> 7.18 us  [the longest x4 4.08 us: exchange_x(): lax.ppermute(to_high, 'gx', forward)]
    unnamed x14 -> x42, local copies, waits for them, and re-layouts: 0.03 us -> 12.5 us
    psum x2 -> x0, blocking collectives: 10.9 us -> none  [the longest x1 5.85 us: on_device(): average = lax.psum(jnp.sum(surface, axis=0), 'samples') / sample_count]
    psum x1 -> x0, waiting for transfers between devices: 9.96 us -> none  [on_device(): summed = lax.psum(partial_sum, 'samples')]
    pallas_call x0 -> x11, Pallas kernels: none -> 9 us  [call(): pl.pallas_call(body, name=name, out_shape=outs, in_specs=in_specs or [VME...]
    ppermute x16 -> x14, starting transfers between devices: 28.1 us -> 20.5 us  [the longest x4 15.6 us: exchange_x(): lax.ppermute(to_low, 'gx', backward)]
    reduce_sum x3, other arithmetic: 7.57 us -> 0.07 us  [the longest x2 0.04 us: on_device(): average = jnp.sum(every, axis=0, keepdims=True) / sample_count]
  transfers between devices with their start and end apart: 17 -> 14, of which waited for: 9 -> 5; matrix products, arithmetic and copies ran while one was open for 11% -> 6% of each run, Pallas kernels for 0% -> 9%
where the time goes in v1:
time: 56.2 us; the launch traced here: 55.7 us
  starting transfers between devices  20.5 us (36%)
  local copies, waits for them, and re-layouts  14.6 us (26%)
  Pallas kernels  9 us (16%)
  waiting for transfers between devices  7.18 us (13%)
  other arithmetic  2.73 us (5%)
  matrix products  0.85 us (2%)
  between operations  0.85 us (2%)
    ppermute x4, starting transfers between devices, exchange_x(): lax.ppermute(to_low, 'gx', backward)  15.6 us
    unnamed x42, local copies, waits for them, and re-layouts  12.5 us
    pallas_call x11, Pallas kernels, call(): pl.pallas_call(body, name=name, out_shape=outs, in_specs=in_specs or [VME...  9 us
    ppermute x4, waiting for transfers between devices, exchange_x(): lax.ppermute(to_high, 'gx', forward)  4.08 us
    ppermute x1, starting transfers between devices, on_device(): lax.ppermute(surface, 'samples', [(i, (i + hop) % shards) for i in range(...  3 us
    ppermute x4, waiting for transfers between devices, swap_y(): return lax.ppermute(block, 'gy', [(0, 1), (1, 0)])  1.61 us
    ppermute x1, starting transfers between devices, on_device(): lax.ppermute(piece, 'samples', [(i, (i + hop) % shards) for i in range(sh...  1.55 us
    ppermute x4, waiting for transfers between devices, exchange_x(): lax.ppermute(to_low, 'gx', backward)  1.23 us
  transfers between devices with their start and end apart: 14, of which 5 were waited for; matrix products, arithmetic and copies ran while one was open for 6% of the time, Pallas kernels for 9%

profile of v1, /device:TPU:0, one launch (start us, length us, event | category | flops | bytes accessed | tf_op | source)
XLA Modules:
  0.0 55.7 jit_solution(13535127902576791539)
XLA Ops:
  0.6 1.1 %slice_bitcast_fusion.states_ref = bf16[4,8,64,128]{3,2,1,0:T(8,128)(2,1)S(1)} fusion(bf16[5,4,8,64,128]{4,3,2,1,0:T(8,128)(2,1)} %states_ref.15), kind=kLoop, calls=%fused_computation | loop fusion | bytes 1048576 | tf_op jit(solution)/shard_map/squeeze | solution.py:275
  2.7 3.0 %collective-permute-start = (f32[4,512]{1,0:T(4,128)S(1)}, f32[4,512]{1,0:T(4,128)S(1)}, u32[]{:S(2)}, u32[]{:S(2)}) collective-permute-start(f32[4,512]{1,0:T(4,128)S(1)} %surface.1), channel_id=1, source_target_pairs={{0,2},{2,0},{1,3},{3,1},{4,6},{6,4},{5,7},{7,5},{8,10},{10,8},{9,1... | collective-permute-start | bytes 24584 | tf_op jit(solution)/shard_map/ppermute | solution.py:278
  5.7 0.9 %fusion = f32[4,3,128]{2,0,1:T(4,128)S(1)} fusion(s32[4]{0:T(128)} %param.8, f32[64,3,128]{2,0,1:T(8,128)S(1)} %copy-done), kind=kOutput, calls=%fused_computation.4 | convolution fusion | flops 1179904 | bytes 104464 | tf_op jit(solution)/shard_map/dot_general | solution.py:296
  6.5 0.7 %convert_element_type.21 = f32[8,64]{1,0:T(8,128)S(1)} convert(s32[8,64]{1,0:T(8,128)} %param.13) | non-fusion elementwise | flops 512 | bytes 4096 | tf_op jit(solution)/shard_map/convert_element_type | solution.py:282
  8.1 4.2 %collective-permute-start.3 = (f32[4,64]{1,0:T(4,128)S(1)}, f32[4,64]{1,0:T(4,128)S(1)}, u32[]{:S(2)}, u32[]{:S(2)}) collective-permute-start(f32[4,64]{1,0:T(4,128)S(1)} %get-tuple-element.66), channel_id=1, source_target_pairs={{4,0},{8,4},{12,8},{0,12},{5,1},{9,5},{13,9},{1,13},{6,2},{10,6},{... | collective-permute-start | bytes 3080 | tf_op jit(solution)/shard_map/ppermute | solution.py:257
  12.3 1.2 %collective-permute-done.3.high_ref = f32[4,64]{1,0:T(4,128)S(1)} collective-permute-done((f32[4,64]{1,0:T(4,128)S(1)}, f32[4,64]{1,0:T(4,128)S(1)}, u32[]{:S(2)}, u32[]{:S(2)}) %collective-permute-start.3) | collective-permute-done | bytes 1056 | tf_op jit(solution)/shard_map/ppermute | solution.py:257
  13.5 4.1 %collective-permute-done.2.low_ref = f32[4,64]{1,0:T(4,128)S(1)} collective-permute-done((f32[4,64]{1,0:T(4,128)S(1)}, f32[4,64]{1,0:T(4,128)S(1)}, u32[]{:S(2)}, u32[]{:S(2)}) %collective-permute-start.2) | collective-permute-done | bytes 1056 | tf_op jit(solution)/shard_map/ppermute | solution.py:257
  17.6 0.7 %copy-done.18 = f32[128]{0:T(128)S(1)} copy-done((f32[128]{0:T(128)S(1)}, f32[128]{0:T(128)}, u32[]{:S(2)}) %copy-start.18) | copy-done | bytes 536
  18.6 0.7 %copy-done.19 = f32[128]{0:T(128)S(1)} copy-done((f32[128]{0:T(128)S(1)}, f32[128]{0:T(128)}, u32[]{:S(2)}) %copy-start.19) | copy-done | bytes 536
  19.6 1.7 %copy-done.1 = bf16[5,4,8,64,128]{4,3,2,1,0:T(8,128)(2,1)S(1)} copy-done((bf16[5,4,8,64,128]{4,3,2,1,0:T(8,128)(2,1)S(1)}, bf16[5,4,8,64,128]{4,3,2,1,0:T(8,128)(2,1)}, u32[]{:S(2)}) %copy-start.1) | copy-done | bytes 2621464
  21.3 1.2 %copy-done.3 = s32[4,8,64,128]{3,2,1,0:T(8,128)S(1)} copy-done((s32[4,8,64,128]{3,2,1,0:T(8,128)S(1)}, s32[4,8,64,128]{3,2,1,0:T(8,128)}, u32[]{:S(2)}) %copy-start.3) | copy-done | bytes 1048600
  22.5 0.9 %copy-done.7 = f32[8,64,128]{2,1,0:T(8,128)S(1)} copy-done((f32[8,64,128]{2,1,0:T(8,128)S(1)}, f32[8,64,128]{2,1,0:T(8,128)}, u32[]{:S(2)}) %copy-start.7) | copy-done | bytes 262168
  23.5 0.9 %copy-done.9 = f32[8,64,128]{2,1,0:T(8,128)S(1)} copy-done((f32[8,64,128]{2,1,0:T(8,128)S(1)}, f32[8,64,128]{2,1,0:T(8,128)}, u32[]{:S(2)}) %copy-start.9) | copy-done | bytes 262168
  24.5 0.9 %inner3.1 = (f32[4,6,64,128]{3,2,1,0:T(8,128)S(1)}, f32[6,64,128]{2,1,0:T(8,128)S(1)}) custom-call(f32[4,2,64,128]{3,2,1,0:T(8,128)S(1)} %get-tuple-element.31.edge_ref, f32[4,6,64,128]{3,2,1,0:T(8,128)S(1)} %get-tuple-element.32.inner_ref, f32[4,8,128]{2,1,0:T(8,128)S(1)} %get-tuple-element.35.beside_ref, f32[2,128]{1,0:T(2,128)S(1)} %broadcast_in_dim.5.side_ref, ...), custom_call_target="tpu_custom_call" | custom-call | flops 1000000 | bytes 3000000 | tf_op jit(solution)/shard_map/inner3/pallas_call | solution.py:21
  25.4 0.8 %copy-done.2 = bf16[5,4,8,64,128]{4,3,2,1,0:T(8,128)(2,1)S(1)} copy-done((bf16[5,4,8,64,128]{4,3,2,1,0:T(8,128)(2,1)S(1)}, bf16[5,4,8,64,128]{4,3,2,1,0:T(8,128)(2,1)}, u32[]{:S(2)}) %copy-start.2) | copy-done | bytes 2621464
  26.9 3.8 %collective-permute-start.5 = (bf16[4,64,128]{2,1,0:T(8,128)(2,1)S(1)}, bf16[4,64,128]{2,1,0:T(8,128)(2,1)S(1)}, u32[]{:S(2)}, u32[]{:S(2)}) collective-permute-start(bf16[4,64,128]{2,1,0:T(8,128)(2,1)S(1)} %get-tuple-element.41), channel_id=1, source_target_pairs={{4,0},{8,4},{12,8},{0,12},{5,1},{9,5},{13,9},{1,13},{6,2},{10,6},{... | collective-permute-start | bytes 196616 | tf_op jit(solution)/shard_map/ppermute | solution.py:257
  30.7 1.2 %collective-permute-done.6.beside_ref = f32[4,8,128]{2,1,0:T(8,128)S(1)} collective-permute-done((f32[4,8,128]{2,1,0:T(8,128)S(1)}, f32[4,8,128]{2,1,0:T(8,128)S(1)}, u32[]{:S(2)}, u32[]{:S(2)}) %collective-permute-start.6) | collective-permute-done | bytes 16416 | tf_op jit(solution)/shard_map/ppermute | solution.py:261
  31.9 0.9 %inner2.1 = (f32[4,6,64,128]{3,2,1,0:T(8,128)S(1)}, f32[6,64,128]{2,1,0:T(8,128)S(1)}) custom-call(f32[4,2,64,128]{3,2,1,0:T(8,128)S(1)} %get-tuple-element.39.edge_ref, f32[4,6,64,128]{3,2,1,0:T(8,128)S(1)} %get-tuple-element.38.now_ref.inner_ref, f32[4,8,128]{2,1,0:T(8,128)S(1)} %collective-permute-done.6.beside_ref, ...), custom_call_target="tpu_custom_call" | custom-call | flops 1000000 | bytes 3000000 | tf_op jit(solution)/shard_map/inner2/pallas_call | solution.py:21
  32.8 0.7 %copy-done.13 = f32[6,64,128]{2,1,0:T(8,128)} copy-done((f32[6,64,128]{2,1,0:T(8,128)}, f32[6,64,128]{2,1,0:T(8,128)S(1)}, u32[]{:S(2)}) %copy-start.13) | copy-done | bytes 196632
  33.5 1.0 %edge2.1 = (f32[4,2,64,128]{3,2,1,0:T(8,128)S(1)}, bf16[4,64,128]{2,1,0:T(8,128)(2,1)}, bf16[4,64,128]{2,1,0:T(8,128)(2,1)}, f32[4,8,128]{2,1,0:T(8,128)S(1)}, f32[2,64,128]{2,1,0:T(8,128)S(1)}) custom-call(f32[4,2,64,128]{3,2,1,0:T(8,128)S(1)} %get-tuple-element.39.edge_ref, f32[4,6,64,128]{3,2,1,0:T(8,128)S(1)} %get-tuple-element.38.now_ref.inner_ref, ...), custom_call_target="tpu_custom_call" | custom-call | flops 400000 | bytes 1200000 | tf_op jit(solution)/shard_map/edge2/pallas_call | solution.py:21
  35.1 3.8 %collective-permute-start.8 = (bf16[4,64,128]{2,1,0:T(8,128)(2,1)}, bf16[4,64,128]{2,1,0:T(8,128)(2,1)}, u32[]{:S(2)}, u32[]{:S(2)}) collective-permute-start(bf16[4,64,128]{2,1,0:T(8,128)(2,1)} %get-tuple-element.48), channel_id=1, source_target_pairs={{4,0},{8,4},{12,8},{0,12},{5,1},{9,5},{13,9},{1,13},{6,2},{10,6},{... | collective-permute-start | bytes 196616 | tf_op jit(solution)/shard_map/ppermute | solution.py:257
  38.9 0.8 %add.33 = f32[8,64]{1,0:T(8,128)S(1)} reshape(f32[512]{0:T(512)} %get-tuple-element.68) | data formatting | bytes 4096 | tf_op jit(solution)/shard_map/add | solution.py:288
  40.1 1.2 %copy-done.5 = s32[4,8,64,128]{3,2,1,0:T(8,128)S(1)} copy-done((s32[4,8,64,128]{3,2,1,0:T(8,128)S(1)}, s32[4,8,64,128]{3,2,1,0:T(8,128)}, u32[]{:S(2)}) %copy-start.5) | copy-done | bytes 1048600
  41.3 1.1 %copy-done.12 = f32[4,6,64,128]{3,2,1,0:T(8,128)S(1)} copy-done((f32[4,6,64,128]{3,2,1,0:T(8,128)S(1)}, f32[4,6,64,128]{3,2,1,0:T(8,128)}, u32[]{:S(2)}) %copy-start.12) | copy-done | bytes 786456
  42.5 0.9 %copy-done.14 = f32[6,64,128]{2,1,0:T(8,128)S(1)} copy-done((f32[6,64,128]{2,1,0:T(8,128)S(1)}, f32[6,64,128]{2,1,0:T(8,128)}, u32[]{:S(2)}) %copy-start.14) | copy-done | bytes 196632
  43.4 0.9 %inner1.1 = (f32[4,6,64,128]{3,2,1,0:T(8,128)S(1)}, f32[6,64,128]{2,1,0:T(8,128)S(1)}) custom-call(f32[4,2,64,128]{3,2,1,0:T(8,128)S(1)} %get-tuple-element.46.edge_ref, f32[4,6,64,128]{3,2,1,0:T(8,128)S(1)} %copy-done.12, f32[4,8,128]{2,1,0:T(8,128)S(1)} %collective-permute-done.9.beside_ref, f32[2,128]{1,0:T(2,128)S(1)} %broadcast_in_dim.5.side_ref, ...), custom_call_target="tpu_custom_call" | custom-call | flops 1000000 | bytes 3000000 | tf_op jit(solution)/shard_map/inner1/pallas_call | solution.py:21
  44.4 1.3 %edge1.1 = (f32[4,2,64,128]{3,2,1,0:T(8,128)S(1)}, bf16[4,64,128]{2,1,0:T(8,128)(2,1)S(1)}, bf16[4,64,128]{2,1,0:T(8,128)(2,1)S(1)}, f32[4,8,128]{2,1,0:T(8,128)S(1)}, f32[2,64,128]{2,1,0:T(8,128)S(1)}) custom-call(f32[4,2,64,128]{3,2,1,0:T(8,128)S(1)} %get-tuple-element.46.edge_ref, f32[4,6,64,128]{3,2,1,0:T(8,128)S(1)} %copy-done.12, ...), custom_call_target="tpu_custom_call" | custom-call | flops 400000 | bytes 1200000 | tf_op jit(solution)/shard_map/edge1/pallas_call | solution.py:21
  45.9 3.8 %collective-permute-start.12 = (bf16[4,64,128]{2,1,0:T(8,128)(2,1)S(1)}, bf16[4,64,128]{2,1,0:T(8,128)(2,1)S(1)}, u32[]{:S(2)}, u32[]{:S(2)}) collective-permute-start(bf16[4,64,128]{2,1,0:T(8,128)(2,1)S(1)} %get-tuple-element.57), channel_id=1, source_target_pairs={{4,0},{8,4},{12,8},{0,12},{5,1},{9,5},{13,9},{1,13},{6,2},{10,6},{... | collective-permute-start | bytes 196616 | tf_op jit(solution)/shard_map/ppermute | solution.py:257
  49.8 1.6 %collective-permute-start.10 = (f32[4,64,128]{2,1,0:T(8,128)S(1)}, f32[4,64,128]{2,1,0:T(8,128)S(1)}, u32[]{:S(2)}, u32[]{:S(2)}) collective-permute-start(f32[4,64,128]{2,1,0:T(8,128)S(1)} %constant_dynamic-slice_fusion), channel_id=1, source_target_pairs={{0,2},{2,0},{1,3},{3,1},{4,6},{6,4},{5,7},{7,5},{8,10},{10,8},{9,1... | collective-permute-start | bytes 393224 | tf_op jit(solution)/shard_map/ppermute | solution.py:357
  51.9 1.8 %inner0.1.now_ref = f32[4,8,64,128]{3,2,1,0:T(8,128)} custom-call(f32[4,2,64,128]{3,2,1,0:T(8,128)S(1)} %get-tuple-element.55.edge_ref, f32[4,6,64,128]{3,2,1,0:T(8,128)S(1)} %get-tuple-element.52.now_ref.inner_ref, f32[4,8,128]{2,1,0:T(8,128)S(1)} %collective-permute-done.13.beside_ref, f32[2,128]{1,0:T(2,128)S(1)} %broadcast_in_dim.5.side_ref, ...), custom_call_target="tpu_custom_call" | custom-call | flops 1000000 | bytes 3000000 | tf_op jit(solution)/shard_map/inner0/pallas_call | solution.py:21
  53.8 1.0 %edge0.1 = f32[4,8,64,128]{3,2,1,0:T(8,128)} custom-call(f32[4,2,64,128]{3,2,1,0:T(8,128)S(1)} %get-tuple-element.55.edge_ref, f32[4,6,64,128]{3,2,1,0:T(8,128)S(1)} %get-tuple-element.52.now_ref.inner_ref, bf16[4,64,128]{2,1,0:T(8,128)(2,1)S(1)} %collective-permute-done.11.low_ref, ...), custom_call_target="tpu_custom_call", output_to_operand_aliasing={{}: (12, {})} | custom-call | flops 400000 | bytes 1200000 | tf_op jit(solution)/shard_map/edge0/pallas_call | solution.py:21
  55.0 0.7 %dynamic-slice_add_fusion = f32[4,64,128]{2,1,0:T(8,128)} fusion(f32[4,64,128]{2,1,0:T(8,128)S(1)} %collective-permute-done.10, f32[8,64,128]{2,1,0:T(8,128)S(1)} %pad_maximum_fusion, s32[]{:T(128)S(6)} %select_n.13), kind=kLoop, calls=%fused_computation.2 | loop fusion | flops 32768 | bytes 393220 | tf_op jit(solution)/shard_map/add | solution.py:357
  (69 shorter events, 5.4 us)
Async XLA Ops:
  0.6 5.0 %copy-start = (f32[64,3,128]{2,0,1:T(8,128)S(1)}, f32[64,3,128]{2,0,1:T(8,128)}, u32[]{:S(2)}) copy-start(f32[64,3,128]{2,0,1:T(8,128)} %param.9) | copy-start | bytes 294916
  1.8 0.7 %copy-start.17 = (f32[128]{0:T(128)S(1)}, f32[128]{0:T(128)}, u32[]{:S(2)}) copy-start(f32[128]{0:T(128)} %param.14) | copy-start | bytes 1540
  2.7 4.7 %collective-permute-start = (f32[4,512]{1,0:T(4,128)S(1)}, f32[4,512]{1,0:T(4,128)S(1)}, u32[]{:S(2)}, u32[]{:S(2)}) collective-permute-start(f32[4,512]{1,0:T(4,128)S(1)} %surface.1), channel_id=1, source_target_pairs={{0,2},{2,0},{1,3},{3,1},{4,6},{6,4},{5,7},{7,5},{8,10},{10,8},{9,1... | collective-permute-start | bytes 24584 | tf_op jit(solution)/shard_map/ppermute | solution.py:278
  8.0 10.4 %collective-permute-start.1 = (f32[4,512]{1,0:T(4,128)S(1)}, f32[4,512]{1,0:T(4,128)S(1)}, u32[]{:S(2)}, u32[]{:S(2)}) collective-permute-start(f32[4,512]{1,0:T(4,128)S(1)} %fusion.5.sens_ref), channel_id=1, source_target_pairs={{0,1},{1,0},{2,3},{3,2},{4,5},{5,4},{6,7},{7,6},{8,9},{9,8},{10,11... | collective-permute-start | bytes 24584 | tf_op jit(solution)/shard_map/ppermute | solution.py:261
  8.1 5.5 %collective-permute-start.3 = (f32[4,64]{1,0:T(4,128)S(1)}, f32[4,64]{1,0:T(4,128)S(1)}, u32[]{:S(2)}, u32[]{:S(2)}) collective-permute-start(f32[4,64]{1,0:T(4,128)S(1)} %get-tuple-element.66), channel_id=1, source_target_pairs={{4,0},{8,4},{12,8},{0,12},{5,1},{9,5},{13,9},{1,13},{6,2},{10,6},{... | collective-permute-start | bytes 3080 | tf_op jit(solution)/shard_map/ppermute | solution.py:257
  12.2 5.4 %collective-permute-start.2 = (f32[4,64]{1,0:T(4,128)S(1)}, f32[4,64]{1,0:T(4,128)S(1)}, u32[]{:S(2)}, u32[]{:S(2)}) collective-permute-start(f32[4,64]{1,0:T(4,128)S(1)} %get-tuple-element.67), channel_id=1, source_target_pairs={{0,4},{4,8},{8,12},{12,0},{1,5},{5,9},{9,13},{13,1},{2,6},{6,10},{... | collective-permute-start | bytes 3080 | tf_op jit(solution)/shard_map/ppermute | solution.py:257
  19.6 1.7 %copy-start.1 = (bf16[5,4,8,64,128]{4,3,2,1,0:T(8,128)(2,1)S(1)}, bf16[5,4,8,64,128]{4,3,2,1,0:T(8,128)(2,1)}, u32[]{:S(2)}) copy-start(bf16[5,4,8,64,128]{4,3,2,1,0:T(8,128)(2,1)} %states_ref.15) | copy-start | bytes 7864324
  21.3 1.2 %copy-start.3 = (s32[4,8,64,128]{3,2,1,0:T(8,128)S(1)}, s32[4,8,64,128]{3,2,1,0:T(8,128)}, u32[]{:S(2)}) copy-start(s32[4,8,64,128]{3,2,1,0:T(8,128)} %flags_ref.15) | copy-start | bytes 3145732
  22.5 0.9 %copy-start.7 = (f32[8,64,128]{2,1,0:T(8,128)S(1)}, f32[8,64,128]{2,1,0:T(8,128)}, u32[]{:S(2)}) copy-start(f32[8,64,128]{2,1,0:T(8,128)} %gust_ref.15) | copy-start | bytes 786436
  23.5 0.9 %copy-start.9 = (f32[8,64,128]{2,1,0:T(8,128)S(1)}, f32[8,64,128]{2,1,0:T(8,128)}, u32[]{:S(2)}) copy-start(f32[8,64,128]{2,1,0:T(8,128)} %reaction_ref.15) | copy-start | bytes 786436
  24.4 1.7 %copy-start.2 = (bf16[5,4,8,64,128]{4,3,2,1,0:T(8,128)(2,1)S(1)}, bf16[5,4,8,64,128]{4,3,2,1,0:T(8,128)(2,1)}, u32[]{:S(2)}) copy-start(bf16[5,4,8,64,128]{4,3,2,1,0:T(8,128)(2,1)} %states_ref.15) | copy-start | bytes 7864324
  24.4 2.0 %copy-start.4 = (s32[4,8,64,128]{3,2,1,0:T(8,128)S(1)}, s32[4,8,64,128]{3,2,1,0:T(8,128)}, u32[]{:S(2)}) copy-start(s32[4,8,64,128]{3,2,1,0:T(8,128)} %flags_ref.15) | copy-start | bytes 3145732
  26.8 6.7 %collective-permute-start.4 = (bf16[4,64,128]{2,1,0:T(8,128)(2,1)S(1)}, bf16[4,64,128]{2,1,0:T(8,128)(2,1)S(1)}, u32[]{:S(2)}, u32[]{:S(2)}) collective-permute-start(bf16[4,64,128]{2,1,0:T(8,128)(2,1)S(1)} %get-tuple-element.40), channel_id=1, source_target_pairs={{0,4},{4,8},{8,12},{12,0},{1,5},{5,9},{9,13},{13,1},{2,6},{6,10},{... | collective-permute-start | bytes 196616 | tf_op jit(solution)/shard_map/ppermute | solution.py:257
  26.9 6.6 %collective-permute-start.5 = (bf16[4,64,128]{2,1,0:T(8,128)(2,1)S(1)}, bf16[4,64,128]{2,1,0:T(8,128)(2,1)S(1)}, u32[]{:S(2)}, u32[]{:S(2)}) collective-permute-start(bf16[4,64,128]{2,1,0:T(8,128)(2,1)S(1)} %get-tuple-element.41), channel_id=1, source_target_pairs={{4,0},{8,4},{12,8},{0,12},{5,1},{9,5},{13,9},{1,13},{6,2},{10,6},{... | collective-permute-start | bytes 196616 | tf_op jit(solution)/shard_map/ppermute | solution.py:257
  30.7 1.2 %collective-permute-start.6 = (f32[4,8,128]{2,1,0:T(8,128)S(1)}, f32[4,8,128]{2,1,0:T(8,128)S(1)}, u32[]{:S(2)}, u32[]{:S(2)}) collective-permute-start(f32[4,8,128]{2,1,0:T(8,128)S(1)} %get-tuple-element.42), channel_id=1, source_target_pairs={{0,1},{1,0},{2,3},{3,2},{4,5},{5,4},{6,7},{7,6},{8,9},{9,8},{10,11... | collective-permute-start | bytes 49160 | tf_op jit(solution)/shard_map/ppermute | solution.py:261
  32.8 0.7 %copy-start.13 = (f32[6,64,128]{2,1,0:T(8,128)}, f32[6,64,128]{2,1,0:T(8,128)S(1)}, u32[]{:S(2)}) copy-start(f32[6,64,128]{2,1,0:T(8,128)S(1)} %get-tuple-element.51.run_ref) | copy-start | bytes 589828
  33.5 1.0 %copy-start.11 = (f32[4,6,64,128]{3,2,1,0:T(8,128)}, f32[4,6,64,128]{3,2,1,0:T(8,128)S(1)}, u32[]{:S(2)}) copy-start(f32[4,6,64,128]{3,2,1,0:T(8,128)S(1)} %get-tuple-element.45.now_ref.inner_ref) | copy-start | bytes 2359300
  33.5 6.6 %copy-start.8 = (f32[8,64,128]{2,1,0:T(8,128)S(1)}, f32[8,64,128]{2,1,0:T(8,128)}, u32[]{:S(2)}) copy-start(f32[8,64,128]{2,1,0:T(8,128)} %gust_ref.15) | copy-start | bytes 786436
  33.5 6.6 %copy-start.10 = (f32[8,64,128]{2,1,0:T(8,128)S(1)}, f32[8,64,128]{2,1,0:T(8,128)}, u32[]{:S(2)}) copy-start(f32[8,64,128]{2,1,0:T(8,128)} %reaction_ref.15) | copy-start | bytes 786436
  35.1 9.2 %collective-permute-start.7 = (bf16[4,64,128]{2,1,0:T(8,128)(2,1)}, bf16[4,64,128]{2,1,0:T(8,128)(2,1)}, u32[]{:S(2)}, u32[]{:S(2)}) collective-permute-start(bf16[4,64,128]{2,1,0:T(8,128)(2,1)} %get-tuple-element.47), channel_id=1, source_target_pairs={{0,4},{4,8},{8,12},{12,0},{1,5},{5,9},{9,13},{13,1},{2,6},{6,10},{... | collective-permute-start | bytes 196616 | tf_op jit(solution)/shard_map/ppermute | solution.py:257
  35.1 9.2 %collective-permute-start.8 = (bf16[4,64,128]{2,1,0:T(8,128)(2,1)}, bf16[4,64,128]{2,1,0:T(8,128)(2,1)}, u32[]{:S(2)}, u32[]{:S(2)}) collective-permute-start(bf16[4,64,128]{2,1,0:T(8,128)(2,1)} %get-tuple-element.48), channel_id=1, source_target_pairs={{4,0},{8,4},{12,8},{0,12},{5,1},{9,5},{13,9},{1,13},{6,2},{10,6},{... | collective-permute-start | bytes 196616 | tf_op jit(solution)/shard_map/ppermute | solution.py:257
  38.9 1.2 %collective-permute-start.9 = (f32[4,8,128]{2,1,0:T(8,128)S(1)}, f32[4,8,128]{2,1,0:T(8,128)S(1)}, u32[]{:S(2)}, u32[]{:S(2)}) collective-permute-start(f32[4,8,128]{2,1,0:T(8,128)S(1)} %get-tuple-element.49), channel_id=1, source_target_pairs={{0,1},{1,0},{2,3},{3,2},{4,5},{5,4},{6,7},{7,6},{8,9},{9,8},{10,11... | collective-permute-start | bytes 49160 | tf_op jit(solution)/shard_map/ppermute | solution.py:261
  40.1 1.2 %copy-start.5 = (s32[4,8,64,128]{3,2,1,0:T(8,128)S(1)}, s32[4,8,64,128]{3,2,1,0:T(8,128)}, u32[]{:S(2)}) copy-start(s32[4,8,64,128]{3,2,1,0:T(8,128)} %flags_ref.15) | copy-start | bytes 3145732
  41.3 1.1 %copy-start.12 = (f32[4,6,64,128]{3,2,1,0:T(8,128)S(1)}, f32[4,6,64,128]{3,2,1,0:T(8,128)}, u32[]{:S(2)}) copy-start(f32[4,6,64,128]{3,2,1,0:T(8,128)} %copy-done.11) | copy-start | bytes 2359300
  42.5 0.9 %copy-start.14 = (f32[6,64,128]{2,1,0:T(8,128)S(1)}, f32[6,64,128]{2,1,0:T(8,128)}, u32[]{:S(2)}) copy-start(f32[6,64,128]{2,1,0:T(8,128)} %copy-done.13) | copy-start | bytes 589828
  43.4 0.9 %copy-start.16 = (f32[2,64,128]{2,1,0:T(8,128)S(1)}, f32[2,64,128]{2,1,0:T(8,128)}, u32[]{:S(2)}) copy-start(f32[2,64,128]{2,1,0:T(8,128)} %copy-done.15) | copy-start | bytes 196612
  44.3 7.0 %copy-start.20 = (s32[8,64]{1,0:T(8,128)S(1)}, s32[8,64]{1,0:T(8,128)}, u32[]{:S(2)}) copy-start(s32[8,64]{1,0:T(8,128)} %param.13) | copy-start | bytes 6148
  44.4 7.6 %copy-start.6 = (s32[4,8,64,128]{3,2,1,0:T(8,128)S(1)}, s32[4,8,64,128]{3,2,1,0:T(8,128)}, u32[]{:S(2)}) copy-start(s32[4,8,64,128]{3,2,1,0:T(8,128)} %flags_ref.15) | copy-start | bytes 3145732
  45.7 6.3 %collective-permute-start.13 = (f32[4,8,128]{2,1,0:T(8,128)S(1)}, f32[4,8,128]{2,1,0:T(8,128)S(1)}, u32[]{:S(2)}, u32[]{:S(2)}) collective-permute-start(f32[4,8,128]{2,1,0:T(8,128)S(1)} %get-tuple-element.58), channel_id=1, source_target_pairs={{0,1},{1,0},{2,3},{3,2},{4,5},{5,4},{6,7},{7,6},{8,9},{9,8},{10,11... | collective-permute-start | bytes 49160 | tf_op jit(solution)/shard_map/ppermute | solution.py:261
  45.9 7.8 %collective-permute-start.11 = (bf16[4,64,128]{2,1,0:T(8,128)(2,1)S(1)}, bf16[4,64,128]{2,1,0:T(8,128)(2,1)S(1)}, u32[]{:S(2)}, u32[]{:S(2)}) collective-permute-start(bf16[4,64,128]{2,1,0:T(8,128)(2,1)S(1)} %get-tuple-element.56), channel_id=1, source_target_pairs={{0,4},{4,8},{8,12},{12,0},{1,5},{5,9},{9,13},{13,1},{2,6},{6,10},{... | collective-permute-start | bytes 196616 | tf_op jit(solution)/shard_map/ppermute | solution.py:257
  45.9 7.8 %collective-permute-start.12 = (bf16[4,64,128]{2,1,0:T(8,128)(2,1)S(1)}, bf16[4,64,128]{2,1,0:T(8,128)(2,1)S(1)}, u32[]{:S(2)}, u32[]{:S(2)}) collective-permute-start(bf16[4,64,128]{2,1,0:T(8,128)(2,1)S(1)} %get-tuple-element.57), channel_id=1, source_target_pairs={{4,0},{8,4},{12,8},{0,12},{5,1},{9,5},{13,9},{1,13},{6,2},{10,6},{... | collective-permute-start | bytes 196616 | tf_op jit(solution)/shard_map/ppermute | solution.py:257
  49.8 5.3 %collective-permute-start.10 = (f32[4,64,128]{2,1,0:T(8,128)S(1)}, f32[4,64,128]{2,1,0:T(8,128)S(1)}, u32[]{:S(2)}, u32[]{:S(2)}) collective-permute-start(f32[4,64,128]{2,1,0:T(8,128)S(1)} %constant_dynamic-slice_fusion), channel_id=1, source_target_pairs={{0,2},{2,0},{1,3},{3,1},{4,6},{6,4},{5,7},{7,5},{8,10},{10,8},{9,1... | collective-permute-start | bytes 393224 | tf_op jit(solution)/shard_map/ppermute | solution.py:357
  (3 other events, 1.9 us)

commit v2 on v1

v2 whole, which is shorter than its diff:
```python
import functools

import jax
import jax.numpy as jnp
from jax import lax
from jax.experimental import pallas as pl
from jax.experimental.pallas import tpu as pltpu
from jax.sharding import PartitionSpec as P

STEPS = 4
DIFFUSION = 0.05
KURTOSIS_WEIGHT = 1.0

F32 = jnp.float32
BF16 = jnp.bfloat16
VMEM = pl.BlockSpec(memory_space=pltpu.VMEM)
ANY = pl.BlockSpec(memory_space=pl.ANY)
HBM = pl.BlockSpec(memory_space=pltpu.HBM)


def call(body, outs, args, name, out_specs=None, in_specs=None, scratch=(), aliases=None, micros=1.0):
    return pl.pallas_call(
        body,
        name=name,
        out_shape=outs,
        in_specs=in_specs or [VMEM] * len(args),
        out_specs=out_specs or jax.tree.map(lambda _: VMEM, outs),
        scratch_shapes=scratch,
        input_output_aliases=aliases or {},
        compiler_params=pltpu.CompilerParams(vmem_limit_bytes=4 << 20),
        cost_estimate=pl.CostEstimate(
            flops=int(1e6 * micros), bytes_accessed=int(3e6 * micros), transcendentals=0
        ),
    )(*args)


def shape(*dims, dtype=F32):
    return jax.ShapeDtypeStruct(dims, dtype)


def three_parts(value):
    first = value.astype(BF16).astype(F32)
    second = (value - first).astype(BF16).astype(F32)
    third = value - first - second
    return first, second, third


def stack_rows(rows, width):
    index = lax.broadcasted_iota(jnp.int32, (16, width), 0)
    block = jnp.zeros((16, width), F32)
    for position, row in enumerate(rows):
        block = jnp.where(index == position, row, block)
    return block.astype(BF16)


def surface_body(states_ref, kernel_ref, mask_ref, surface_ref, kernel_out, mask_out, buffer, semaphores):
    samples, rows, width, levels = buffer.shape
    head = [
        pltpu.make_async_copy(kernel_ref, kernel_out, semaphores.at[samples]),
        pltpu.make_async_copy(mask_ref, mask_out, semaphores.at[samples + 1]),
    ]
    copies = [
        pltpu.make_async_copy(states_ref.at[STEPS, k], buffer.at[k], semaphores.at[k])
        for k in range(samples)
    ]
    for copy in head + copies:
        copy.start()
    head[0].wait()
    parts = stack_rows(three_parts(kernel_out[...]), levels)
    for k in range(samples):
        copies[k].wait()
        for x in range(rows):
            product = lax.dot_general(
                parts, buffer[k, x], (((1,), (1,)), ((), ())), preferred_element_type=F32
            )
            surface_ref[k, x : x + 1] = product[0:1] + product[1:2] + product[2:3]
    head[1].wait()


def moments_body(count, *refs):
    parts, mask_ref = refs[:count], refs[count]
    risk_ref, sens_ref, low_ref, high_ref = refs[count + 1 :]
    samples, rows, _ = sens_ref.shape
    total = samples * count
    every = [part[k] for part in parts for k in range(samples)]
    average = sum(every) / total
    spread = [value - average for value in every]
    cubed = [value * value * value for value in spread]
    third_moment = sum(cubed) / total
    fourth_moment = sum(cube * value for cube, value in zip(cubed, spread)) / total
    receptor = mask_ref[...].astype(F32)
    risk_ref[...] = receptor * (average + KURTOSIS_WEIGHT * fourth_moment)
    for k in range(samples):
        sens = receptor * (
            1.0 / total + 4.0 * KURTOSIS_WEIGHT / total * (cubed[k] - third_moment)
        )
        sens_ref[k] = sens
        low_ref[k : k + 1] = sens[0:1]
        high_ref[k : k + 1] = sens[rows - 1 : rows]


def outer_rows(row, kernel_rows):
    first, second, third = three_parts(row)
    left = stack_rows((first, first, first, second, second, third), row.shape[1])
    return lax.dot_general(
        left, kernel_rows, (((0,), (0,)), ((), ())), preferred_element_type=F32
    )


def kernel_rows_of(kernel_ref):
    first, second, third = three_parts(kernel_ref[...])
    return stack_rows((first, second, third, first, second, first), kernel_ref.shape[1])


def final_body(sens_ref, beside_ref, kernel_ref, edge_ref, inner_ref, beside_out, run_edge_ref, run_inner_ref):
    samples, rows, width = sens_ref.shape
    levels = kernel_ref.shape[1]
    right = kernel_rows_of(kernel_ref)
    lanes = lax.broadcasted_iota(jnp.int32, (rows, width), 1)
    wanted = lanes == jnp.where(lax.axis_index("gy") == 1, width - 1, 0)
    for k in range(samples):
        column = jnp.sum(jnp.where(wanted, beside_ref[k], 0.0), axis=1, keepdims=True)
        beside_out[k] = column * kernel_ref[...]
    for x in range(rows):
        total = jnp.zeros((width, levels), F32)
        for k in range(samples):
            piece = outer_rows(sens_ref[k, x : x + 1], right)
            if x in (0, rows - 1):
                edge_ref[k, x // (rows - 1)] = piece
            else:
                inner_ref[k, x - 1] = piece
            total = total + piece
        if x in (0, rows - 1):
            run_edge_ref[x // (rows - 1)] = total
        else:
            run_inner_ref[x - 1] = total


def halo_body(low_ref, high_ref, kernel_ref, low_out, high_out):
    right = kernel_rows_of(kernel_ref)
    for source, target in ((low_ref, low_out), (high_ref, high_out)):
        for k in range(target.shape[0]):
            target[k] = outer_rows(source[k : k + 1], right)


def load_body(
    seeds_ref, table_ref, flags_ref, gust_ref, reaction_ref, states_ref,
    profile_out, flags_out, gust_out, reaction_out, states_out, table, semaphores
):
    samples = flags_out.shape[0]
    copies = [(table_ref, table), (gust_ref, gust_out), (reaction_ref, reaction_out)]
    for k in range(samples):
        copies.append((flags_ref.at[k], flags_out.at[k]))
    for step in reversed(range(STEPS)):
        copies.append((states_ref.at[step], states_out.at[step]))
    copies = [
        pltpu.make_async_copy(source, target, semaphores.at[i])
        for i, (source, target) in enumerate(copies)
    ]
    for copy in copies:
        copy.start()
    copies[0].wait()
    for k in range(samples):
        for d in range(3):
            profile_out[k, d : d + 1] = table[d, pl.ds(seeds_ref[k], 1)]
    for copy in copies[1:]:
        copy.wait()


class Plan:
    def __init__(self, levels):
        lane = lax.broadcasted_iota(jnp.int32, (8, levels), 1)
        row = lax.broadcasted_iota(jnp.int32, (8, levels), 0)
        self.below_top = lane < levels - 1
        self.above_base = lane > 0
        self.top_row = row == 7
        self.base_row = row == 0
        self.loss = 1.0 - (
            jnp.where(self.below_top, DIFFUSION, 0.0) + jnp.where(self.above_base, DIFFUSION, 0.0)
        )


def step_row(plan, centre, west, east, low_row, high_row, bits, gust, twice, stored, speeds):
    width, levels = centre.shape
    tiles = width // 8
    first, second, third, whole = speeds
    piece = lambda value, t: value[8 * t : 8 * t + 8]
    parts = [piece(centre, t) for t in range(tiles)]
    up = [pltpu.roll(part, 7, 0) for part in parts] + [jnp.broadcast_to(high_row, (8, levels))]
    down = [jnp.broadcast_to(low_row, (8, levels))] + [pltpu.roll(part, 1, 0) for part in parts]
    result = []
    for t in range(tiles):
        here = parts[t]
        north = jnp.where(plan.top_row, up[t + 1], up[t])
        south = jnp.where(plan.base_row, down[t], down[t + 1])
        above = jnp.where(plan.below_top, pltpu.roll(here, levels - 1, 1), 0.0)
        below = jnp.where(plan.above_base, pltpu.roll(here, 1, 1), 0.0)
        flag = piece(bits, t)
        moved = (
            first * jnp.where((flag & 1) != 0, piece(east, t), piece(west, t))
            + second * jnp.where((flag & 2) != 0, north, south)
            + third * jnp.where((flag & 4) != 0, above, below)
            - whole * here
        )
        result.append(
            here * (plan.loss - piece(twice, t) * piece(stored, t))
            + piece(gust, t) * moved
            + DIFFUSION * (above + below)
        )
    return result


def speeds_of(profile_ref, k, levels):
    rows = [profile_ref[k, d : d + 1] for d in range(3)]
    rows.append(rows[0] + rows[1] + rows[2])
    return [jnp.broadcast_to(row, (8, levels)) for row in rows]


def side_flags(levels):
    side = lax.axis_index("gy")
    ones = jnp.full((1, levels), 1.0, F32)
    return jnp.where(side == 1, ones, 0.0), jnp.where(side == 0, ones, 0.0), side == 1


def inner_body(
    step, last, edge_ref, inner_ref, beside_ref, run_ref, profile_ref, flags_ref, gust_ref, reaction_ref,
    states_ref, *outs
):
    samples, inside, width, levels = inner_ref.shape
    plan = Plan(levels)
    if last:
        target, buffer, semaphores = outs
    else:
        buffer, rim_out, run_out = outs
    low_side, high_side, upper = side_flags(levels)
    copies = []

    def at(k, x):
        return edge_ref[k, x // (inside + 1)] if x in (0, inside + 1) else inner_ref[k, x - 1]

    for x in range(1, inside + 1):
        gust = gust_ref[x]
        twice = 2.0 * reaction_ref[x]
        total = None if last else [run_ref[x - 1, 8 * t : 8 * t + 8] for t in range(width // 8)]
        for k in range(samples):
            halo = beside_ref[k, x : x + 1]
            tiles = step_row(
                plan, at(k, x), at(k, x - 1), at(k, x + 1), halo * low_side, halo * high_side,
                flags_ref[k, x], gust, twice, states_ref[step, k, x].astype(F32),
                speeds_of(profile_ref, k, levels),
            )
            for t, tile in enumerate(tiles):
                buffer[k, x - 1, 8 * t : 8 * t + 8] = tile
                if not last:
                    total[t] = total[t] + tile
            if not last:
                rim_out[k, x : x + 1] = jnp.where(upper, tiles[0][0:1], tiles[-1][7:8])
        if last:
            copies.append(
                pltpu.make_async_copy(buffer.at[:, x - 1], target.at[:, x], semaphores.at[x - 1])
            )
            copies[-1].start()
        else:
            for t, tile in enumerate(total):
                run_out[x - 1, 8 * t : 8 * t + 8] = tile
    for copy in copies:
        copy.wait()


def edge_body(
    step, last, rims, edge_ref, inner_ref, low_ref, high_ref, beside_ref, run_ref, profile_ref, flags_ref,
    gust_ref, reaction_ref, states_ref, *outs
):
    samples, inside, width, levels = inner_ref.shape
    plan = Plan(levels)
    copies = []
    if last:
        pieces, (_, target, source_out, buffer, source, semaphores) = outs[:rims], outs[rims:]
        source[...] = sum(piece[...] for piece in pieces)
        copies.append(pltpu.make_async_copy(source, source_out, semaphores.at[2]))
        copies[-1].start()
    else:
        buffer, low_out, high_out, rim_out, run_out = outs
    low_side, high_side, upper = side_flags(levels)
    for side, x in enumerate((0, inside + 1)):
        gust = gust_ref[x]
        twice = 2.0 * reaction_ref[x]
        total = None if last else [run_ref[side, 8 * t : 8 * t + 8] for t in range(width // 8)]
        for k in range(samples):
            row = side if beside_ref.shape[1] == 2 else x
            halo = beside_ref[k, row : row + 1]
            if side == 0:
                west, east = low_ref[k].astype(F32), inner_ref[k, 0]
            else:
                west, east = inner_ref[k, inside - 1], high_ref[k].astype(F32)
            tiles = step_row(
                plan, edge_ref[k, side], west, east, halo * low_side, halo * high_side,
                flags_ref[k, x], gust, twice, states_ref[step, k, x].astype(F32),
                speeds_of(profile_ref, k, levels),
            )
            for t, tile in enumerate(tiles):
                buffer[k, side, 8 * t : 8 * t + 8] = tile
                if not last:
                    total[t] = total[t] + tile
            if not last:
                whole = jnp.concatenate(tiles, axis=0).astype(BF16)
                (low_out if side == 0 else high_out)[k] = whole
                rim_out[k, side : side + 1] = jnp.where(upper, tiles[0][0:1], tiles[-1][7:8])
        if last:
            copies.append(
                pltpu.make_async_copy(buffer.at[:, side], target.at[:, x], semaphores.at[side])
            )
            copies[-1].start()
        else:
            for t, tile in enumerate(total):
                run_out[side, 8 * t : 8 * t + 8] = tile
    for copy in copies:
        copy.wait()


def share_body(shards, edge_ref, inner_ref, *outs):
    pieces, full = outs[:shards], outs[shards]
    rows = full.shape[0]
    full[0] = edge_ref[0]
    full[1 : rows - 1] = inner_ref[...]
    full[rows - 1] = edge_ref[1]
    me = lax.axis_index("samples")
    share = rows // shards
    for hop in range(shards):
        owner = lax.rem(me + hop, shards)
        pieces[hop][...] = full[pl.ds(owner * share, share)]


def exchange_x(to_low, to_high):
    count = lax.axis_size("gx")
    forward = [(i, (i + 1) % count) for i in range(count)]
    backward = [(target, source) for source, target in forward]
    return lax.ppermute(to_high, "gx", forward), lax.ppermute(to_low, "gx", backward)


def swap_y(block):
    return lax.ppermute(block, "gy", [(0, 1), (1, 0)])


def rotate(block, axis, hop):
    count = lax.axis_size(axis)
    return lax.ppermute(block, axis, [(i, (i + hop) % count) for i in range(count)])


def on_device(seeds, wind_profiles, gust, reaction, flags, mask, kernel, states):
    local_count, rows, width, levels = flags.shape
    shards = lax.axis_size("samples")
    inside = rows - 2
    slab = shape(local_count, width, levels)
    hold = lambda value: pltpu.with_memory_space_constraint(value, pltpu.HBM)
    flags, gust, reaction, states, mask = map(hold, (flags, gust, reaction, states, mask))
    kernel = hold(kernel[None, :])
    table = hold(jnp.swapaxes(wind_profiles, 0, 1))

    surface, kernel_row, mask_here = call(
        surface_body,
        (shape(local_count, rows, width), shape(1, levels), shape(rows, width, dtype=jnp.int32)),
        (states, kernel, mask),
        "surface",
        in_specs=[HBM] * 3,
        scratch=[
            pltpu.VMEM((local_count, rows, width, levels), BF16),
            pltpu.SemaphoreType.DMA((local_count + 2,)),
        ],
    )
    others = [rotate(surface, "samples", hop) for hop in range(1, shards)]
    risk_map, sensitivity, low_sens, high_sens = call(
        functools.partial(moments_body, shards),
        (shape(rows, width), shape(local_count, rows, width)) + (shape(local_count, width),) * 2,
        (surface, *others, mask_here),
        "moments",
        micros=0.1,
    )
    low, high = exchange_x(low_sens, high_sens)
    beside_sens = swap_y(sensitivity)
    fixed = call(
        load_body,
        (
            shape(local_count, 3, levels),
            shape(*flags.shape, dtype=flags.dtype),
            shape(*gust.shape),
            shape(*reaction.shape),
            shape(STEPS, *flags.shape, dtype=states.dtype),
        ),
        (seeds, table, flags, gust, reaction, states),
        "load",
        in_specs=[pl.BlockSpec(memory_space=pltpu.SMEM)] + [HBM] * 5,
        scratch=[
            pltpu.VMEM((3, wind_profiles.shape[0], levels), F32),
            pltpu.SemaphoreType.DMA((local_count + 3 + STEPS,)),
        ],
    )
    edge, inner, beside, run_edge, run_inner = call(
        final_body,
        (
            shape(local_count, 2, width, levels),
            shape(local_count, inside, width, levels),
            shape(local_count, rows, levels),
            shape(2, width, levels),
            shape(inside, width, levels),
        ),
        (sensitivity, beside_sens, kernel_row),
        "final",
        micros=0.3,
    )
    beside_edge = beside
    low, high = call(halo_body, (slab,) * 2, (low, high, kernel_row), "halo", micros=0.1)
    for step in range(STEPS - 1, 0, -1):
        inner_now, rim_inner, run_inner = call(
            functools.partial(inner_body, step, False),
            (
                shape(local_count, inside, width, levels),
                shape(local_count, rows, levels),
                shape(inside, width, levels),
            ),
            (edge, inner, beside, run_inner) + fixed,
            f"inner{step}",
        )
        edge, to_low, to_high, rim_edge, run_edge = call(
            functools.partial(edge_body, step, False, 0),
            (
                shape(local_count, 2, width, levels),
                shape(local_count, width, levels, dtype=BF16),
                shape(local_count, width, levels, dtype=BF16),
                shape(local_count, 2, levels),
                shape(2, width, levels),
            ),
            (edge, inner, low, high, beside_edge, run_edge) + fixed,
            f"edge{step}",
            micros=0.4,
        )
        inner = inner_now
        low, high = exchange_x(to_low, to_high)
        beside, beside_edge = swap_y(rim_inner), swap_y(rim_edge)

    target = call(
        functools.partial(inner_body, 0, True),
        shape(*flags.shape),
        (edge, inner, beside, run_inner) + fixed,
        "inner0",
        out_specs=ANY,
        scratch=[pltpu.VMEM((local_count, inside, width, levels), F32), pltpu.SemaphoreType.DMA((inside,))],
    )
    share = shape(rows // shards, width, levels)
    pieces = call(
        functools.partial(share_body, shards),
        (share,) * shards,
        (run_edge, run_inner),
        "share",
        scratch=[pltpu.VMEM((rows, width, levels), F32)],
        micros=0.1,
    )
    pieces = [pieces[0]] + [rotate(pieces[hop], "samples", hop) for hop in range(1, shards)]
    args = (edge, inner, low, high, beside_edge, run_edge) + fixed + (*pieces, target)
    initial_adjoint, source_gradient = call(
        functools.partial(edge_body, 0, True, shards),
        (shape(*flags.shape), share),
        args,
        "edge0",
        out_specs=(ANY, ANY),
        in_specs=[VMEM] * (len(args) - 1) + [ANY],
        scratch=[
            pltpu.VMEM((local_count, 2, width, levels), F32),
            pltpu.VMEM(share.shape, F32),
            pltpu.SemaphoreType.DMA((3,)),
        ],
        aliases={len(args) - 1: 0},
        micros=0.4,
    )
    return risk_map, source_gradient, initial_adjoint


def solution(mesh):
    return jax.shard_map(
        on_device,
        mesh=mesh,
        in_specs=(
            P(("groups", "samples")),
            P(),
            P("gx", "gy", None),
            P("gx", "gy", None),
            P(("groups", "samples"), "gx", "gy", None),
            P("gx", "gy"),
            P(),
            P(None, ("groups", "samples"), "gx", "gy", None),
        ),
        out_specs=(
            P(("groups", "gx"), "gy"),
            P(("groups", "gx", "samples"), "gy", None),
            P(("groups", "samples"), "gx", "gy", None),
        ),
        check_vma=False,
    )
```

time: 56.2 us -> 40.6 us (0.72)
  local copies, waits for them, and re-layouts: 14.6 us -> 0.01 us
  Pallas kernels: 9 us -> 12.1 us
  other arithmetic: 2.73 us -> 0 us
  waiting for transfers between devices: 7.18 us -> 6.24 us
  starting transfers between devices: 20.5 us -> 21.4 us
  matrix products: 0.85 us -> 0 us
    unnamed x42 -> x2, local copies, waits for them, and re-layouts: 12.5 us -> 0.01 us
    ppermute x4, starting transfers between devices: 0.07 us -> 3.2 us  [exchange_x(): lax.ppermute(to_high, 'gx', forward)]
    ppermute x4, starting transfers between devices: 15.6 us -> 12.5 us  [exchange_x(): lax.ppermute(to_low, 'gx', backward)]
    pallas_call x11 -> x14, Pallas kernels: 9 us -> 12.1 us  [call(): pl.pallas_call(body, name=name, out_shape=outs, in_specs=in_specs or [VME...]
    ppermute x4, waiting for transfers between devices: 4.08 us -> 1.74 us  [exchange_x(): lax.ppermute(to_high, 'gx', forward)]
    ppermute x2, waiting for transfers between devices: 0.25 us -> 1.72 us  [rotate(): lax.ppermute(block, axis, [(i, (i + hop) % count) for i in range(count)])]
    add x2 -> x0, other arithmetic: 1.26 us -> none  [the longest x1 0.67 us: on_device(): source_gradient + lax.ppermute(piece, 'samples', [(i, (i + hop) % shards)...]
    ppermute x4, waiting for transfers between devices: 1.23 us -> 0.01 us  [exchange_x(): lax.ppermute(to_low, 'gx', backward)]
  transfers between devices with their start and end apart: 14 -> 17, of which waited for: 5 -> 6; matrix products, arithmetic and copies ran while one was open for 6% -> 0% of each run, Pallas kernels for 9% -> 18%
where the time goes in v2:
time: 40.6 us; the launch traced here: 40.5 us
  starting transfers between devices  21.4 us (53%)
  Pallas kernels  12.1 us (30%)
  waiting for transfers between devices  6.24 us (15%)
  between operations  0.79 us (2%)
    ppermute x4, starting transfers between devices, exchange_x(): lax.ppermute(to_low, 'gx', backward)  12.5 us
    pallas_call x14, Pallas kernels, call(): pl.pallas_call(body, name=name, out_shape=outs, in_specs=in_specs or [VME...  12.1 us
    ppermute x2, starting transfers between devices, rotate(): lax.ppermute(block, axis, [(i, (i + hop) % count) for i in range(count)])  4.56 us
    ppermute x4, starting transfers between devices, exchange_x(): lax.ppermute(to_high, 'gx', forward)  3.2 us
    ppermute x7, waiting for transfers between devices, swap_y(): return lax.ppermute(block, 'gy', [(0, 1), (1, 0)])  2.77 us
    ppermute x4, waiting for transfers between devices, exchange_x(): lax.ppermute(to_high, 'gx', forward)  1.74 us
    ppermute x2, waiting for transfers between devices, rotate(): lax.ppermute(block, axis, [(i, (i + hop) % count) for i in range(count)])  1.72 us
    ppermute x7, starting transfers between devices, swap_y(): return lax.ppermute(block, 'gy', [(0, 1), (1, 0)])  1.09 us
  transfers between devices with their start and end apart: 17, of which 6 were waited for; matrix products, arithmetic and copies ran while one was open for 0% of the time, Pallas kernels for 18%

profile of v2, /device:TPU:0, one launch (start us, length us, event | category | flops | bytes accessed | tf_op | source)
XLA Modules:
  0.0 40.5 jit_solution(17167002960200113035)
XLA Ops:
  0.6 1.7 %surface.1 = (f32[4,8,64]{2,1,0:T(8,128)S(1)}, f32[1,128]{1,0:T(1,128)S(1)}, s32[8,64]{1,0:T(8,128)S(1)}) custom-call(bf16[5,4,8,64,128]{4,3,2,1,0:T(8,128)(2,1)} %states_ref.3, f32[1,128]{1,0:T(1,128)} %bitcast.3, s32[8,64]{1,0:T(8,128)} %mask_ref.1), custom_call_target="tpu_custom_call" | custom-call | flops 1000000 | bytes 3000000 | tf_op jit(solution)/shard_map/surface/pallas_call | solution.py:22
  2.4 3.0 %collective-permute-start = (f32[4,8,64]{2,1,0:T(8,128)S(1)}, f32[4,8,64]{2,1,0:T(8,128)S(1)}, u32[]{:S(2)}, u32[]{:S(2)}) collective-permute-start(f32[4,8,64]{2,1,0:T(8,128)S(1)} %get-tuple-element.50.refs_0_), channel_id=1, source_target_pairs={{0,2},{2,0},{1,3},{3,1},{4,6},{6,4},{5,7},{7,5},{8,10},{10,8},{9,1... | collective-permute-start | bytes 24584 | tf_op jit(solution)/shard_map/ppermute | solution.py:347
  5.4 1.7 %collective-permute-done.refs_1_ = f32[4,8,64]{2,1,0:T(8,128)S(1)} collective-permute-done((f32[4,8,64]{2,1,0:T(8,128)S(1)}, f32[4,8,64]{2,1,0:T(8,128)S(1)}, u32[]{:S(2)}, u32[]{:S(2)}) %collective-permute-start) | collective-permute-done | bytes 8224 | tf_op jit(solution)/shard_map/ppermute | solution.py:347
  7.1 0.6 %moments.1 = (f32[8,64]{1,0:T(8,128)}, f32[4,8,64]{2,1,0:T(8,128)S(1)}, f32[4,64]{1,0:T(4,128)S(1)}, f32[4,64]{1,0:T(4,128)S(1)}) custom-call(f32[4,8,64]{2,1,0:T(8,128)S(1)} %get-tuple-element.50.refs_0_, f32[4,8,64]{2,1,0:T(8,128)S(1)} %collective-permute-done.refs_1_, s32[8,64]{1,0:T(8,128)S(1)} %get-tuple-element.51.refs_2_), custom_call_target="tpu_custom_call" | custom-call | flops 100000 | bytes 300000 | tf_op jit(solution)/shard_map/moments/pallas_call | solution.py:22
  7.7 0.0 collective-permute-start.1
  7.7 2.1 %collective-permute-start.2 = (f32[4,64]{1,0:T(4,128)S(1)}, f32[4,64]{1,0:T(4,128)S(1)}, u32[]{:S(2)}, u32[]{:S(2)}) collective-permute-start(f32[4,64]{1,0:T(4,128)S(1)} %get-tuple-element.57), channel_id=1, source_target_pairs={{0,4},{4,8},{8,12},{12,0},{1,5},{5,9},{9,13},{13,1},{2,6},{6,10},{... | collective-permute-start | bytes 3080 | tf_op jit(solution)/shard_map/ppermute | solution.py:338
  9.8 2.0 %collective-permute-start.3 = (f32[4,64]{1,0:T(4,128)S(1)}, f32[4,64]{1,0:T(4,128)S(1)}, u32[]{:S(2)}, u32[]{:S(2)}) collective-permute-start(f32[4,64]{1,0:T(4,128)S(1)} %get-tuple-element.58), channel_id=1, source_target_pairs={{4,0},{8,4},{12,8},{0,12},{5,1},{9,5},{13,9},{1,13},{6,2},{10,6},{... | collective-permute-start | bytes 3080 | tf_op jit(solution)/shard_map/ppermute | solution.py:338
  11.9 2.7 %load.1 = (f32[4,3,128]{2,1,0:T(4,128)S(1)}, s32[4,8,64,128]{3,2,1,0:T(8,128)S(1)}, f32[8,64,128]{2,1,0:T(8,128)S(1)}, f32[8,64,128]{2,1,0:T(8,128)S(1)}, bf16[4,4,8,64,128]{4,3,2,1,0:T(8,128)(2,1)S(1)}) custom-call(s32[4]{0:T(128)S(1)} %copy-done, f32[3,64,128]{2,1,0:T(8,128)} %bitcast.2, s32[4,8,64,128]{3,2,1,0:T(8,128)} %flags_ref.1, ...), custom_call_target="tpu_custom_call" | custom-call | flops 1000000 | bytes 3000000 | tf_op jit(solution)/shard_map/load/pallas_call | solution.py:22
  14.6 0.2 halo.1
  14.8 0.4 final.1
  15.2 0.3 edge3.1
  15.5 0.5 %collective-permute-start.4 = (bf16[4,64,128]{2,1,0:T(8,128)(2,1)S(1)}, bf16[4,64,128]{2,1,0:T(8,128)(2,1)S(1)}, u32[]{:S(2)}, u32[]{:S(2)}) collective-permute-start(bf16[4,64,128]{2,1,0:T(8,128)(2,1)S(1)} %get-tuple-element.71), channel_id=1, source_target_pairs={{0,4},{4,8},{8,12},{12,0},{1,5},{5,9},{9,13},{13,1},{2,6},{6,10},{... | collective-permute-start | bytes 196616 | tf_op jit(solution)/shard_map/ppermute | solution.py:338
  16.0 3.4 %collective-permute-start.5 = (bf16[4,64,128]{2,1,0:T(8,128)(2,1)S(1)}, bf16[4,64,128]{2,1,0:T(8,128)(2,1)S(1)}, u32[]{:S(2)}, u32[]{:S(2)}) collective-permute-start(bf16[4,64,128]{2,1,0:T(8,128)(2,1)S(1)} %get-tuple-element.72), channel_id=1, source_target_pairs={{4,0},{8,4},{12,8},{0,12},{5,1},{9,5},{13,9},{1,13},{6,2},{10,6},{... | collective-permute-start | bytes 196616 | tf_op jit(solution)/shard_map/ppermute | solution.py:338
  19.4 0.9 %inner3.1 = (f32[4,6,64,128]{3,2,1,0:T(8,128)S(1)}, f32[4,8,128]{2,1,0:T(8,128)S(1)}, f32[6,64,128]{2,1,0:T(8,128)S(1)}) custom-call(f32[4,2,64,128]{3,2,1,0:T(8,128)S(1)} %get-tuple-element.55.edge_ref, f32[4,6,64,128]{3,2,1,0:T(8,128)S(1)} %get-tuple-element.56.inner_ref, f32[4,8,128]{2,1,0:T(8,128)S(1)} %get-tuple-element.61.beside_ref, ...), custom_call_target="tpu_custom_call" | custom-call | flops 1000000 | bytes 3000000 | tf_op jit(solution)/shard_map/inner3/pallas_call | solution.py:22
  20.3 0.2 collective-permute-done.6.beside_ref
  20.6 1.7 %collective-permute-done.4.low_ref = bf16[4,64,128]{2,1,0:T(8,128)(2,1)S(1)} collective-permute-done((bf16[4,64,128]{2,1,0:T(8,128)(2,1)S(1)}, bf16[4,64,128]{2,1,0:T(8,128)(2,1)S(1)}, u32[]{:S(2)}, u32[]{:S(2)}) %collective-permute-start.4) | collective-permute-done | bytes 65568 | tf_op jit(solution)/shard_map/ppermute | solution.py:338
  22.3 0.3 edge2.1
  22.6 0.6 %collective-permute-start.8 = (bf16[4,64,128]{2,1,0:T(8,128)(2,1)S(1)}, bf16[4,64,128]{2,1,0:T(8,128)(2,1)S(1)}, u32[]{:S(2)}, u32[]{:S(2)}) collective-permute-start(bf16[4,64,128]{2,1,0:T(8,128)(2,1)S(1)} %get-tuple-element.79), channel_id=1, source_target_pairs={{0,4},{4,8},{8,12},{12,0},{1,5},{5,9},{9,13},{13,1},{2,6},{6,10},{... | collective-permute-start | bytes 196616 | tf_op jit(solution)/shard_map/ppermute | solution.py:338
  23.2 3.3 %collective-permute-start.9 = (bf16[4,64,128]{2,1,0:T(8,128)(2,1)S(1)}, bf16[4,64,128]{2,1,0:T(8,128)(2,1)S(1)}, u32[]{:S(2)}, u32[]{:S(2)}) collective-permute-start(bf16[4,64,128]{2,1,0:T(8,128)(2,1)S(1)} %get-tuple-element.80), channel_id=1, source_target_pairs={{4,0},{8,4},{12,8},{0,12},{5,1},{9,5},{13,9},{1,13},{6,2},{10,6},{... | collective-permute-start | bytes 196616 | tf_op jit(solution)/shard_map/ppermute | solution.py:338
  26.5 1.2 %collective-permute-done.7.beside_ref = f32[4,8,128]{2,1,0:T(8,128)S(1)} collective-permute-done((f32[4,8,128]{2,1,0:T(8,128)S(1)}, f32[4,8,128]{2,1,0:T(8,128)S(1)}, u32[]{:S(2)}, u32[]{:S(2)}) %collective-permute-start.7) | collective-permute-done | bytes 16416 | tf_op jit(solution)/shard_map/ppermute | solution.py:342
  27.7 0.9 %inner2.1 = (f32[4,6,64,128]{3,2,1,0:T(8,128)S(1)}, f32[4,8,128]{2,1,0:T(8,128)S(1)}, f32[6,64,128]{2,1,0:T(8,128)S(1)}) custom-call(f32[4,2,64,128]{3,2,1,0:T(8,128)S(1)} %get-tuple-element.68.edge_ref, f32[4,6,64,128]{3,2,1,0:T(8,128)S(1)} %get-tuple-element.70.inner_ref, f32[4,8,128]{2,1,0:T(8,128)S(1)} %collective-permute-done.7.beside_ref, ...), custom_call_target="tpu_custom_call" | custom-call | flops 1000000 | bytes 3000000 | tf_op jit(solution)/shard_map/inner2/pallas_call | solution.py:22
  28.6 0.2 collective-permute-start.11
  28.9 0.3 collective-permute-start.10
  29.2 0.7 %collective-permute-done.11.beside_ref = f32[4,8,128]{2,1,0:T(8,128)S(1)} collective-permute-done((f32[4,8,128]{2,1,0:T(8,128)S(1)}, f32[4,8,128]{2,1,0:T(8,128)S(1)}, u32[]{:S(2)}, u32[]{:S(2)}) %collective-permute-start.11) | collective-permute-done | bytes 16416 | tf_op jit(solution)/shard_map/ppermute | solution.py:342
  29.9 0.9 %inner1.1 = (f32[4,6,64,128]{3,2,1,0:T(8,128)S(1)}, f32[4,8,128]{2,1,0:T(8,128)S(1)}, f32[6,64,128]{2,1,0:T(8,128)S(1)}) custom-call(f32[4,2,64,128]{3,2,1,0:T(8,128)S(1)} %get-tuple-element.75.edge_ref, f32[4,6,64,128]{3,2,1,0:T(8,128)S(1)} %get-tuple-element.78.inner_ref, f32[4,8,128]{2,1,0:T(8,128)S(1)} %collective-permute-done.11.beside_ref, ...), custom_call_target="tpu_custom_call" | custom-call | flops 1000000 | bytes 3000000 | tf_op jit(solution)/shard_map/inner1/pallas_call | solution.py:22
  30.9 0.3 edge1.1
  31.2 1.6 %collective-permute-start.15 = (f32[4,64,128]{2,1,0:T(8,128)S(1)}, f32[4,64,128]{2,1,0:T(8,128)S(1)}, u32[]{:S(2)}, u32[]{:S(2)}) collective-permute-start(f32[4,64,128]{2,1,0:T(8,128)S(1)} %get-tuple-element.93), channel_id=1, source_target_pairs={{0,2},{2,0},{1,3},{3,1},{4,6},{6,4},{5,7},{7,5},{8,10},{10,8},{9,1... | collective-permute-start | bytes 393224 | tf_op jit(solution)/shard_map/ppermute | solution.py:347
  32.8 3.8 %collective-permute-start.13 = (bf16[4,64,128]{2,1,0:T(8,128)(2,1)S(1)}, bf16[4,64,128]{2,1,0:T(8,128)(2,1)S(1)}, u32[]{:S(2)}, u32[]{:S(2)}) collective-permute-start(bf16[4,64,128]{2,1,0:T(8,128)(2,1)S(1)} %get-tuple-element.88), channel_id=1, source_target_pairs={{4,0},{8,4},{12,8},{0,12},{5,1},{9,5},{13,9},{1,13},{6,2},{10,6},{... | collective-permute-start | bytes 196616 | tf_op jit(solution)/shard_map/ppermute | solution.py:338
  36.6 0.5 %collective-permute-start.14 = (f32[4,2,128]{2,1,0:T(2,128)S(1)}, f32[4,2,128]{2,1,0:T(2,128)S(1)}, u32[]{:S(2)}, u32[]{:S(2)}) collective-permute-start(f32[4,2,128]{2,1,0:T(2,128)S(1)} %get-tuple-element.89), channel_id=1, source_target_pairs={{0,1},{1,0},{2,3},{3,2},{4,5},{5,4},{6,7},{7,6},{8,9},{9,8},{10,11... | collective-permute-start | bytes 12296 | tf_op jit(solution)/shard_map/ppermute | solution.py:342
  37.1 0.7 %collective-permute-done.16.beside_ref = f32[4,8,128]{2,1,0:T(8,128)S(1)} collective-permute-done((f32[4,8,128]{2,1,0:T(8,128)S(1)}, f32[4,8,128]{2,1,0:T(8,128)S(1)}, u32[]{:S(2)}, u32[]{:S(2)}) %collective-permute-start.16) | collective-permute-done | bytes 16416 | tf_op jit(solution)/shard_map/ppermute | solution.py:342
  37.8 1.6 %inner0.1.outs_2_ = f32[4,8,64,128]{3,2,1,0:T(8,128)} custom-call(f32[4,2,64,128]{3,2,1,0:T(8,128)S(1)} %get-tuple-element.83.edge_ref, f32[4,6,64,128]{3,2,1,0:T(8,128)S(1)} %get-tuple-element.86.inner_ref, f32[4,8,128]{2,1,0:T(8,128)S(1)} %collective-permute-done.16.beside_ref, f32[6,64,128]{2,1,0:T(8,128)S(1)} %get-tuple-element.91.inner_ref.run_ref, ...), custom_call_target="tpu_custom_call" | custom-call | flops 1000000 | bytes 3000000 | tf_op jit(solution)/shard_map/inner0/pallas_call | solution.py:22
  39.5 1.0 %edge0.1 = (f32[4,8,64,128]{3,2,1,0:T(8,128)}, f32[4,64,128]{2,1,0:T(8,128)}) custom-call(f32[4,2,64,128]{3,2,1,0:T(8,128)S(1)} %get-tuple-element.83.edge_ref, f32[4,6,64,128]{3,2,1,0:T(8,128)S(1)} %get-tuple-element.86.inner_ref, bf16[4,64,128]{2,1,0:T(8,128)(2,1)S(1)} %collective-permute-done.12.low_ref, ...), custom_call_target="tpu_custom_call", output_to_operand_aliasing={{0}: (13, {})} | custom-call | flops 400000 | bytes 1200000 | tf_op jit(solution)/shard_map/edge0/pallas_call | solution.py:22
  (18 shorter events, 0.1 us)
Async XLA Ops:
  0.6 11.2 %copy-start = (s32[4]{0:T(128)S(1)}, s32[4]{0:T(128)}, u32[]{:S(2)}) copy-start(s32[4]{0:T(128)} %seeds_ref.1) | copy-start | bytes 52
  2.4 4.7 %collective-permute-start = (f32[4,8,64]{2,1,0:T(8,128)S(1)}, f32[4,8,64]{2,1,0:T(8,128)S(1)}, u32[]{:S(2)}, u32[]{:S(2)}) collective-permute-start(f32[4,8,64]{2,1,0:T(8,128)S(1)} %get-tuple-element.50.refs_0_), channel_id=1, source_target_pairs={{0,2},{2,0},{1,3},{3,1},{4,6},{6,4},{5,7},{7,5},{8,10},{10,8},{9,1... | collective-permute-start | bytes 24584 | tf_op jit(solution)/shard_map/ppermute | solution.py:347
  7.7 7.1 %collective-permute-start.1 = (f32[4,8,64]{2,1,0:T(8,128)S(1)}, f32[4,8,64]{2,1,0:T(8,128)S(1)}, u32[]{:S(2)}, u32[]{:S(2)}) collective-permute-start(f32[4,8,64]{2,1,0:T(8,128)S(1)} %get-tuple-element.53.sens_ref), channel_id=1, source_target_pairs={{0,1},{1,0},{2,3},{3,2},{4,5},{5,4},{6,7},{7,6},{8,9},{9,8},{10,11... | collective-permute-start | bytes 24584 | tf_op jit(solution)/shard_map/ppermute | solution.py:342
  7.7 6.8 %collective-permute-start.2 = (f32[4,64]{1,0:T(4,128)S(1)}, f32[4,64]{1,0:T(4,128)S(1)}, u32[]{:S(2)}, u32[]{:S(2)}) collective-permute-start(f32[4,64]{1,0:T(4,128)S(1)} %get-tuple-element.57), channel_id=1, source_target_pairs={{0,4},{4,8},{8,12},{12,0},{1,5},{5,9},{9,13},{13,1},{2,6},{6,10},{... | collective-permute-start | bytes 3080 | tf_op jit(solution)/shard_map/ppermute | solution.py:338
  9.8 4.7 %collective-permute-start.3 = (f32[4,64]{1,0:T(4,128)S(1)}, f32[4,64]{1,0:T(4,128)S(1)}, u32[]{:S(2)}, u32[]{:S(2)}) collective-permute-start(f32[4,64]{1,0:T(4,128)S(1)} %get-tuple-element.58), channel_id=1, source_target_pairs={{4,0},{8,4},{12,8},{0,12},{5,1},{9,5},{13,9},{1,13},{6,2},{10,6},{... | collective-permute-start | bytes 3080 | tf_op jit(solution)/shard_map/ppermute | solution.py:338
  15.5 6.8 %collective-permute-start.4 = (bf16[4,64,128]{2,1,0:T(8,128)(2,1)S(1)}, bf16[4,64,128]{2,1,0:T(8,128)(2,1)S(1)}, u32[]{:S(2)}, u32[]{:S(2)}) collective-permute-start(bf16[4,64,128]{2,1,0:T(8,128)(2,1)S(1)} %get-tuple-element.71), channel_id=1, source_target_pairs={{0,4},{4,8},{8,12},{12,0},{1,5},{5,9},{9,13},{13,1},{2,6},{6,10},{... | collective-permute-start | bytes 196616 | tf_op jit(solution)/shard_map/ppermute | solution.py:338
  16.0 6.3 %collective-permute-start.5 = (bf16[4,64,128]{2,1,0:T(8,128)(2,1)S(1)}, bf16[4,64,128]{2,1,0:T(8,128)(2,1)S(1)}, u32[]{:S(2)}, u32[]{:S(2)}) collective-permute-start(bf16[4,64,128]{2,1,0:T(8,128)(2,1)S(1)} %get-tuple-element.72), channel_id=1, source_target_pairs={{4,0},{8,4},{12,8},{0,12},{5,1},{9,5},{13,9},{1,13},{6,2},{10,6},{... | collective-permute-start | bytes 196616 | tf_op jit(solution)/shard_map/ppermute | solution.py:338
  19.4 1.2 %collective-permute-start.6 = (f32[4,2,128]{2,1,0:T(2,128)S(1)}, f32[4,2,128]{2,1,0:T(2,128)S(1)}, u32[]{:S(2)}, u32[]{:S(2)}) collective-permute-start(f32[4,2,128]{2,1,0:T(2,128)S(1)} %get-tuple-element.73), channel_id=1, source_target_pairs={{0,1},{1,0},{2,3},{3,2},{4,5},{5,4},{6,7},{7,6},{8,9},{9,8},{10,11... | collective-permute-start | bytes 12296 | tf_op jit(solution)/shard_map/ppermute | solution.py:342
  22.6 8.2 %collective-permute-start.8 = (bf16[4,64,128]{2,1,0:T(8,128)(2,1)S(1)}, bf16[4,64,128]{2,1,0:T(8,128)(2,1)S(1)}, u32[]{:S(2)}, u32[]{:S(2)}) collective-permute-start(bf16[4,64,128]{2,1,0:T(8,128)(2,1)S(1)} %get-tuple-element.79), channel_id=1, source_target_pairs={{0,4},{4,8},{8,12},{12,0},{1,5},{5,9},{9,13},{13,1},{2,6},{6,10},{... | collective-permute-start | bytes 196616 | tf_op jit(solution)/shard_map/ppermute | solution.py:338
  23.2 7.6 %collective-permute-start.9 = (bf16[4,64,128]{2,1,0:T(8,128)(2,1)S(1)}, bf16[4,64,128]{2,1,0:T(8,128)(2,1)S(1)}, u32[]{:S(2)}, u32[]{:S(2)}) collective-permute-start(bf16[4,64,128]{2,1,0:T(8,128)(2,1)S(1)} %get-tuple-element.80), channel_id=1, source_target_pairs={{4,0},{8,4},{12,8},{0,12},{5,1},{9,5},{13,9},{1,13},{6,2},{10,6},{... | collective-permute-start | bytes 196616 | tf_op jit(solution)/shard_map/ppermute | solution.py:338
  26.5 1.2 %collective-permute-start.7 = (f32[4,8,128]{2,1,0:T(8,128)S(1)}, f32[4,8,128]{2,1,0:T(8,128)S(1)}, u32[]{:S(2)}, u32[]{:S(2)}) collective-permute-start(f32[4,8,128]{2,1,0:T(8,128)S(1)} %get-tuple-element.76), channel_id=1, source_target_pairs={{0,1},{1,0},{2,3},{3,2},{4,5},{5,4},{6,7},{7,6},{8,9},{9,8},{10,11... | collective-permute-start | bytes 49160 | tf_op jit(solution)/shard_map/ppermute | solution.py:342
  28.6 1.2 %collective-permute-start.11 = (f32[4,8,128]{2,1,0:T(8,128)S(1)}, f32[4,8,128]{2,1,0:T(8,128)S(1)}, u32[]{:S(2)}, u32[]{:S(2)}) collective-permute-start(f32[4,8,128]{2,1,0:T(8,128)S(1)} %get-tuple-element.84), channel_id=1, source_target_pairs={{0,1},{1,0},{2,3},{3,2},{4,5},{5,4},{6,7},{7,6},{8,9},{9,8},{10,11... | collective-permute-start | bytes 49160 | tf_op jit(solution)/shard_map/ppermute | solution.py:342
  28.9 2.0 %collective-permute-start.10 = (f32[4,2,128]{2,1,0:T(2,128)S(1)}, f32[4,2,128]{2,1,0:T(2,128)S(1)}, u32[]{:S(2)}, u32[]{:S(2)}) collective-permute-start(f32[4,2,128]{2,1,0:T(2,128)S(1)} %get-tuple-element.81), channel_id=1, source_target_pairs={{0,1},{1,0},{2,3},{3,2},{4,5},{5,4},{6,7},{7,6},{8,9},{9,8},{10,11... | collective-permute-start | bytes 12296 | tf_op jit(solution)/shard_map/ppermute | solution.py:342
  31.2 8.2 %collective-permute-start.15 = (f32[4,64,128]{2,1,0:T(8,128)S(1)}, f32[4,64,128]{2,1,0:T(8,128)S(1)}, u32[]{:S(2)}, u32[]{:S(2)}) collective-permute-start(f32[4,64,128]{2,1,0:T(8,128)S(1)} %get-tuple-element.93), channel_id=1, source_target_pairs={{0,2},{2,0},{1,3},{3,1},{4,6},{6,4},{5,7},{7,5},{8,10},{10,8},{9,1... | collective-permute-start | bytes 393224 | tf_op jit(solution)/shard_map/ppermute | solution.py:347
  32.8 6.6 %collective-permute-start.12 = (bf16[4,64,128]{2,1,0:T(8,128)(2,1)S(1)}, bf16[4,64,128]{2,1,0:T(8,128)(2,1)S(1)}, u32[]{:S(2)}, u32[]{:S(2)}) collective-permute-start(bf16[4,64,128]{2,1,0:T(8,128)(2,1)S(1)} %get-tuple-element.87), channel_id=1, source_target_pairs={{0,4},{4,8},{8,12},{12,0},{1,5},{5,9},{9,13},{13,1},{2,6},{6,10},{... | collective-permute-start | bytes 196616 | tf_op jit(solution)/shard_map/ppermute | solution.py:338
  32.8 6.6 %collective-permute-start.13 = (bf16[4,64,128]{2,1,0:T(8,128)(2,1)S(1)}, bf16[4,64,128]{2,1,0:T(8,128)(2,1)S(1)}, u32[]{:S(2)}, u32[]{:S(2)}) collective-permute-start(bf16[4,64,128]{2,1,0:T(8,128)(2,1)S(1)} %get-tuple-element.88), channel_id=1, source_target_pairs={{4,0},{8,4},{12,8},{0,12},{5,1},{9,5},{13,9},{1,13},{6,2},{10,6},{... | collective-permute-start | bytes 196616 | tf_op jit(solution)/shard_map/ppermute | solution.py:338
  36.6 1.2 %collective-permute-start.16 = (f32[4,8,128]{2,1,0:T(8,128)S(1)}, f32[4,8,128]{2,1,0:T(8,128)S(1)}, u32[]{:S(2)}, u32[]{:S(2)}) collective-permute-start(f32[4,8,128]{2,1,0:T(8,128)S(1)} %get-tuple-element.94), channel_id=1, source_target_pairs={{0,1},{1,0},{2,3},{3,2},{4,5},{5,4},{6,7},{7,6},{8,9},{9,8},{10,11... | collective-permute-start | bytes 49160 | tf_op jit(solution)/shard_map/ppermute | solution.py:342
  36.6 2.8 %collective-permute-start.14 = (f32[4,2,128]{2,1,0:T(2,128)S(1)}, f32[4,2,128]{2,1,0:T(2,128)S(1)}, u32[]{:S(2)}, u32[]{:S(2)}) collective-permute-start(f32[4,2,128]{2,1,0:T(2,128)S(1)} %get-tuple-element.89), channel_id=1, source_target_pairs={{0,1},{1,0},{2,3},{3,2},{4,5},{5,4},{6,7},{7,6},{8,9},{9,8},{10,11... | collective-permute-start | bytes 12296 | tf_op jit(solution)/shard_map/ppermute | solution.py:342

commit v3 on v2

v3 whole, which is shorter than its diff:
```python
import functools

import jax
import jax.numpy as jnp
from jax import lax
from jax.experimental import pallas as pl
from jax.experimental.pallas import tpu as pltpu
from jax.sharding import PartitionSpec as P

STEPS = 4
DIFFUSION = 0.05
KURTOSIS_WEIGHT = 1.0
INNER_COST = 1.0

F32 = jnp.float32
BF16 = jnp.bfloat16
VMEM = pl.BlockSpec(memory_space=pltpu.VMEM)
ANY = pl.BlockSpec(memory_space=pl.ANY)
HBM = pl.BlockSpec(memory_space=pltpu.HBM)


def call(body, outs, args, name, out_specs=None, in_specs=None, scratch=(), aliases=None, micros=1.0):
    return pl.pallas_call(
        body,
        name=name,
        out_shape=outs,
        in_specs=in_specs or [VMEM] * len(args),
        out_specs=out_specs or jax.tree.map(lambda _: VMEM, outs),
        scratch_shapes=scratch,
        input_output_aliases=aliases or {},
        compiler_params=pltpu.CompilerParams(vmem_limit_bytes=4 << 20),
        cost_estimate=pl.CostEstimate(
            flops=int(1e6 * micros), bytes_accessed=int(3e6 * micros), transcendentals=0
        ),
    )(*args)


def shape(*dims, dtype=F32):
    return jax.ShapeDtypeStruct(dims, dtype)


def three_parts(value):
    first = value.astype(BF16).astype(F32)
    second = (value - first).astype(BF16).astype(F32)
    third = value - first - second
    return first, second, third


def stack_rows(rows, width):
    index = lax.broadcasted_iota(jnp.int32, (16, width), 0)
    block = jnp.zeros((16, width), F32)
    for position, row in enumerate(rows):
        block = jnp.where(index == position, row, block)
    return block.astype(BF16)


def surface_body(states_ref, kernel_ref, surface_ref, kernel_out, buffer, semaphores):
    samples, rows, width, levels = buffer.shape
    copies = [
        pltpu.make_async_copy(states_ref.at[STEPS, k], buffer.at[k], semaphores.at[k])
        for k in range(samples)
    ]
    copies.append(pltpu.make_async_copy(kernel_ref, kernel_out, semaphores.at[samples]))
    for copy in copies:
        copy.start()
    copies[-1].wait()
    parts = stack_rows(three_parts(kernel_out[...]), levels)
    for k in range(samples):
        copies[k].wait()
        flat = buffer[k].reshape(rows * width, levels)
        product = lax.dot_general(
            parts, flat, (((1,), (1,)), ((), ())), preferred_element_type=F32
        )
        surface_ref[k : k + 1] = product[0:1] + product[1:2] + product[2:3]


def load_body(
    seeds_ref, flags_ref, gust_ref, reaction_ref, states_ref, mask_ref, table_ref, _,
    profile_out, flags_out, gust_out, reaction_out, stored_out, receptor_out, mask, table, padded, semaphores
):
    samples, rows, width, levels = flags_out.shape
    pairs = [(table_ref, table), (mask_ref, mask), (gust_ref, gust_out), (reaction_ref, reaction_out)]
    pairs += [(flags_ref.at[k], flags_out.at[k]) for k in range(samples)]
    pairs += [(states_ref.at[step], stored_out.at[step]) for step in range(STEPS)]
    copies = [
        pltpu.make_async_copy(source, target, semaphores.at[i]) for i, (source, target) in enumerate(pairs)
    ]
    for copy in copies:
        copy.start()
    copies[0].wait()
    for k in range(samples):
        for d in range(3):
            profile_out[k, d : d + 1] = table[d, pl.ds(seeds_ref[k], 1)]
    copies[1].wait()
    padded[...] = jnp.zeros_like(padded)
    padded[:, :width] = mask[...].astype(F32)
    for pair in range(rows // 2):
        receptor_out[:, 2 * width * pair : 2 * width * (pair + 1)] = (
            padded[2 * pair : 2 * pair + 1] + pltpu.roll(padded[2 * pair + 1 : 2 * pair + 2], width, 1)
        )
    for copy in copies[2:]:
        copy.wait()


def moments_body(count, *refs):
    parts, receptor_ref = refs[:count], refs[count]
    risk_ref, sens_ref, low_ref, high_ref = refs[count + 2 :]
    samples, cells = sens_ref.shape
    width = low_ref.shape[1]
    total = samples * count
    fold = lambda values: sum(jnp.sum(value, axis=0, keepdims=True) for value in values) / total
    every = [part[...] for part in parts]
    average = fold(every)
    spread = [value - average for value in every]
    cubed = [value * value * value for value in spread]
    third_moment = fold(cubed)
    fourth_moment = fold([cube * value for cube, value in zip(cubed, spread)])
    receptor = receptor_ref[...]
    risk_ref[...] = receptor * (average + KURTOSIS_WEIGHT * fourth_moment)
    sens = receptor * (1.0 / total + 4.0 * KURTOSIS_WEIGHT / total * (cubed[0] - third_moment))
    sens_ref[...] = sens
    low_ref[...] = sens[:, :width]
    high_ref[...] = pltpu.roll(sens[:, cells - 2 * width :], width, 1)[:, :width]


def outer_rows(row, kernel_rows):
    first, second, third = three_parts(row)
    left = stack_rows((first, first, first, second, second, third), row.shape[1])
    return lax.dot_general(
        left, kernel_rows, (((0,), (0,)), ((), ())), preferred_element_type=F32
    )


def kernel_rows_of(kernel_ref):
    first, second, third = three_parts(kernel_ref[...])
    return stack_rows((first, second, third, first, second, first), kernel_ref.shape[1])


def final_body(sens_ref, beside_ref, kernel_ref, edge_ref, inner_ref, beside_out, run_edge_ref, run_inner_ref):
    samples, inside, width, levels = inner_ref.shape
    rows = inside + 2
    right = kernel_rows_of(kernel_ref)
    total = [jnp.zeros((width, levels), F32)] * rows
    lanes = lax.broadcasted_iota(jnp.int32, (rows, rows * width), 1)
    starts = lax.broadcasted_iota(jnp.int32, (rows, rows * width), 0) * width
    wanted = lanes == starts + jnp.where(lax.axis_index("gy") == 1, width - 1, 0)
    for k in range(samples):
        block = outer_rows(sens_ref[k : k + 1], right)
        for x in range(rows):
            piece = block[x * width : (x + 1) * width]
            if x in (0, rows - 1):
                edge_ref[k, x // (rows - 1)] = piece
            else:
                inner_ref[k, x - 1] = piece
            total[x] = total[x] + piece
        column = jnp.sum(jnp.where(wanted, beside_ref[k : k + 1], 0.0), axis=1, keepdims=True)
        beside_out[k] = column * kernel_ref[...]
    run_edge_ref[0] = total[0]
    run_edge_ref[1] = total[rows - 1]
    for x in range(1, rows - 1):
        run_inner_ref[x - 1] = total[x]


def halo_body(low_ref, high_ref, kernel_ref, _, low_out, high_out):
    right = kernel_rows_of(kernel_ref)
    for source, target in ((low_ref, low_out), (high_ref, high_out)):
        for k in range(target.shape[0]):
            target[k] = outer_rows(source[k : k + 1], right)


class Plan:
    def __init__(self, levels):
        lane = lax.broadcasted_iota(jnp.int32, (8, levels), 1)
        row = lax.broadcasted_iota(jnp.int32, (8, levels), 0)
        self.below_top = lane < levels - 1
        self.above_base = lane > 0
        self.top_row = row == 7
        self.base_row = row == 0
        self.loss = 1.0 - (
            jnp.where(self.below_top, DIFFUSION, 0.0) + jnp.where(self.above_base, DIFFUSION, 0.0)
        )


def step_row(plan, centre, west, east, low_row, high_row, bits, gust, twice, stored, speeds):
    width, levels = centre.shape
    tiles = width // 8
    first, second, third, whole = speeds
    piece = lambda value, t: value[8 * t : 8 * t + 8]
    parts = [piece(centre, t) for t in range(tiles)]
    up = [pltpu.roll(part, 7, 0) for part in parts] + [jnp.broadcast_to(high_row, (8, levels))]
    down = [jnp.broadcast_to(low_row, (8, levels))] + [pltpu.roll(part, 1, 0) for part in parts]
    result = []
    for t in range(tiles):
        here = parts[t]
        north = jnp.where(plan.top_row, up[t + 1], up[t])
        south = jnp.where(plan.base_row, down[t], down[t + 1])
        above = jnp.where(plan.below_top, pltpu.roll(here, levels - 1, 1), 0.0)
        below = jnp.where(plan.above_base, pltpu.roll(here, 1, 1), 0.0)
        flag = piece(bits, t)
        moved = (
            first * jnp.where((flag & 1) != 0, piece(east, t), piece(west, t))
            + second * jnp.where((flag & 2) != 0, north, south)
            + third * jnp.where((flag & 4) != 0, above, below)
            - whole * here
        )
        result.append(
            here * (plan.loss - piece(twice, t) * piece(stored, t))
            + piece(gust, t) * moved
            + DIFFUSION * (above + below)
        )
    return result


def speeds_of(profile_ref, k, levels):
    rows = [profile_ref[k, d : d + 1] for d in range(3)]
    rows.append(rows[0] + rows[1] + rows[2])
    return [jnp.broadcast_to(row, (8, levels)) for row in rows]


def side_flags(levels):
    side = lax.axis_index("gy")
    ones = jnp.full((1, levels), 1.0, F32)
    return jnp.where(side == 1, ones, 0.0), jnp.where(side == 0, ones, 0.0), side == 1


def inner_body(
    step, last, edge_ref, inner_ref, beside_ref, run_ref, profile_ref, flags_ref, gust_ref, reaction_ref,
    stored_ref, *outs
):
    samples, inside, width, levels = inner_ref.shape
    plan = Plan(levels)
    if last:
        risk_ref, buffer, risk_out = outs
        for x in range(inside + 2):
            pair = risk_ref[:, 2 * width * (x // 2) : 2 * width * (x // 2 + 1)]
            pair = pair if x % 2 == 0 else pltpu.roll(pair, width, 1)
            risk_out[x : x + 1] = pair[:, :width]
    else:
        buffer, rim_out, run_out = outs
    low_side, high_side, upper = side_flags(levels)

    def at(k, x):
        return edge_ref[k, x // (inside + 1)] if x in (0, inside + 1) else inner_ref[k, x - 1]

    for x in range(1, inside + 1):
        gust = gust_ref[x]
        twice = 2.0 * reaction_ref[x]
        total = None if last else [run_ref[x - 1, 8 * t : 8 * t + 8] for t in range(width // 8)]
        for k in range(samples):
            halo = beside_ref[k, x : x + 1]
            tiles = step_row(
                plan, at(k, x), at(k, x - 1), at(k, x + 1), halo * low_side, halo * high_side,
                flags_ref[k, x], gust, twice, stored_ref[step, k, x].astype(F32),
                speeds_of(profile_ref, k, levels),
            )
            for t, tile in enumerate(tiles):
                buffer[k, x - 1, 8 * t : 8 * t + 8] = tile
                if not last:
                    total[t] = total[t] + tile
            if not last:
                rim_out[k, x : x + 1] = jnp.where(upper, tiles[0][0:1], tiles[-1][7:8])
        if not last:
            for t, tile in enumerate(total):
                run_out[x - 1, 8 * t : 8 * t + 8] = tile


def edge_body(
    step, last, shards, edge_ref, inner_ref, low_ref, high_ref, beside_ref, run_ref, profile_ref, flags_ref,
    gust_ref, reaction_ref, stored_ref, *outs
):
    samples, inside, width, levels = inner_ref.shape
    plan = Plan(levels)
    copies = []
    if last:
        pieces, (now_ref, target, source_out, buffer, source, semaphores) = outs[:shards], outs[shards:]
        for k in range(samples):
            copies.append(
                pltpu.make_async_copy(
                    now_ref.at[k], target.at[k, 1 : inside + 1], semaphores.at[2 * samples + 1 + k]
                )
            )
            copies[-1].start()
        source[...] = sum(piece[...] for piece in pieces)
        copies.append(pltpu.make_async_copy(source, source_out, semaphores.at[2 * samples]))
        copies[-1].start()
    else:
        rim_ref, buffer, low_out, high_out, rim_out, run_out = outs
        rim_out[...] = rim_ref[...]
    low_side, high_side, upper = side_flags(levels)
    for side, x in enumerate((0, inside + 1)):
        gust = gust_ref[x]
        twice = 2.0 * reaction_ref[x]
        total = None if last else [run_ref[side, 8 * t : 8 * t + 8] for t in range(width // 8)]
        for k in range(samples):
            halo = beside_ref[k, x : x + 1]
            if side == 0:
                west, east = low_ref[k].astype(F32), inner_ref[k, 0]
            else:
                west, east = inner_ref[k, inside - 1], high_ref[k].astype(F32)
            tiles = step_row(
                plan, edge_ref[k, side], west, east, halo * low_side, halo * high_side,
                flags_ref[k, x], gust, twice, stored_ref[step, k, x].astype(F32),
                speeds_of(profile_ref, k, levels),
            )
            for t, tile in enumerate(tiles):
                buffer[k, side, 8 * t : 8 * t + 8] = tile
                if not last:
                    total[t] = total[t] + tile
            if not last:
                whole = jnp.concatenate(tiles, axis=0).astype(BF16)
                (low_out if side == 0 else high_out)[k] = whole
                rim_out[k, x : x + 1] = jnp.where(upper, tiles[0][0:1], tiles[-1][7:8])
            if last:
                copies.append(
                    pltpu.make_async_copy(
                        buffer.at[k, side], target.at[k, x], semaphores.at[side * samples + k]
                    )
                )
                copies[-1].start()
        if not last:
            for t, tile in enumerate(total):
                run_out[side, 8 * t : 8 * t + 8] = tile
    for copy in copies:
        copy.wait()


def share_body(shards, edge_ref, inner_ref, _, *outs):
    pieces, full = outs[:shards], outs[shards]
    rows = full.shape[0]
    full[0] = edge_ref[0]
    full[1 : rows - 1] = inner_ref[...]
    full[rows - 1] = edge_ref[1]
    me = lax.axis_index("samples")
    share = rows // shards
    for hop in range(shards):
        owner = lax.rem(me + hop, shards)
        pieces[hop][...] = full[pl.ds(owner * share, share)]


def exchange_x(to_low, to_high):
    count = lax.axis_size("gx")
    forward = [(i, (i + 1) % count) for i in range(count)]
    backward = [(target, source) for source, target in forward]
    return lax.ppermute(to_high, "gx", forward), lax.ppermute(to_low, "gx", backward)


def swap_y(block):
    return lax.ppermute(block, "gy", [(0, 1), (1, 0)])


def rotate(block, axis, hop):
    count = lax.axis_size(axis)
    return lax.ppermute(block, axis, [(i, (i + hop) % count) for i in range(count)])


def on_device(seeds, wind_profiles, gust, reaction, flags, mask, kernel, states):
    local_count, rows, width, levels = flags.shape
    shards = lax.axis_size("samples")
    inside = rows - 2
    slab = shape(local_count, width, levels)
    rim = shape(local_count, rows, levels)
    flat = shape(local_count, rows * width)
    hold = lambda value: pltpu.with_memory_space_constraint(value, pltpu.HBM)
    states = hold(states)

    surface, kernel_row = call(
        surface_body,
        (flat, shape(1, levels)),
        (states, hold(kernel[None, :])),
        "surface",
        in_specs=[HBM] * 2,
        scratch=[
            pltpu.VMEM((local_count, rows, width, levels), BF16),
            pltpu.SemaphoreType.DMA((local_count + 1,)),
        ],
    )
    table = jnp.swapaxes(wind_profiles, 0, 1)
    *fixed, receptor = call(
        load_body,
        (
            shape(local_count, 3, levels),
            shape(*flags.shape, dtype=flags.dtype),
            shape(*gust.shape),
            shape(*reaction.shape),
            shape(STEPS, *flags.shape, dtype=states.dtype),
            shape(1, rows * width),
        ),
        (seeds, hold(flags), hold(gust), hold(reaction), states, hold(mask), hold(table), kernel_row),
        "load",
        in_specs=[pl.BlockSpec(memory_space=pltpu.SMEM)] + [HBM] * 6 + [VMEM],
        scratch=[
            pltpu.VMEM(mask.shape, mask.dtype),
            pltpu.VMEM(table.shape, F32),
            pltpu.VMEM((rows, 2 * width), F32),
            pltpu.SemaphoreType.DMA((local_count + STEPS + 4,)),
        ],
    )
    others = [rotate(surface, "samples", hop) for hop in range(1, shards)]
    risk, sensitivity, low_sens, high_sens = call(
        functools.partial(moments_body, shards),
        (shape(1, rows * width), flat) + (shape(local_count, width),) * 2,
        (surface, *others, receptor, fixed[0]),
        "moments",
        micros=0.1,
    )
    low, high = exchange_x(low_sens, high_sens)
    edge, inner, beside, run_edge, run_inner = call(
        final_body,
        (
            shape(local_count, 2, width, levels),
            shape(local_count, inside, width, levels),
            rim,
            shape(2, width, levels),
            shape(inside, width, levels),
        ),
        (sensitivity, swap_y(sensitivity), kernel_row),
        "final",
        micros=INNER_COST,
    )
    for step in range(STEPS - 1, 0, -1):
        inner_now, rim_inner, run_inner = call(
            functools.partial(inner_body, step, False),
            (shape(local_count, inside, width, levels), rim, shape(inside, width, levels)),
            (edge, inner, beside, run_inner, *fixed),
            f"inner{step}",
            micros=INNER_COST,
        )
        if step == STEPS - 1:
            low, high = call(
                halo_body, (slab,) * 2, (low, high, kernel_row, rim_inner), "halo", micros=0.1
            )
        edge, to_low, to_high, rim_all, run_edge = call(
            functools.partial(edge_body, step, False, 0),
            (
                shape(local_count, 2, width, levels),
                shape(local_count, width, levels, dtype=BF16),
                shape(local_count, width, levels, dtype=BF16),
                rim,
                shape(2, width, levels),
            ),
            (edge, inner, low, high, beside, run_edge, *fixed, rim_inner),
            f"edge{step}",
            micros=0.4,
        )
        inner = inner_now
        beside = swap_y(rim_all)
        low, high = exchange_x(to_low, to_high)

    share = shape(rows // shards, width, levels)
    pieces = call(
        functools.partial(share_body, shards),
        (share,) * shards,
        (run_edge, run_inner, rim_all),
        "share",
        scratch=[pltpu.VMEM((rows, width, levels), F32)],
        micros=0.1,
    )
    pieces = [pieces[0]] + [rotate(pieces[hop], "samples", hop) for hop in range(1, shards)]
    inner_now, risk_map = call(
        functools.partial(inner_body, 0, True),
        (shape(local_count, inside, width, levels), shape(rows, width)),
        (edge, inner, beside, run_inner, *fixed, risk),
        "inner0",
        micros=INNER_COST,
    )
    initial_adjoint, source_gradient = call(
        functools.partial(edge_body, 0, True, shards),
        (shape(*flags.shape), share),
        (edge, inner, low, high, beside, run_edge, *fixed, *pieces, inner_now),
        "edge0",
        out_specs=(HBM, HBM),
        scratch=[
            pltpu.VMEM((local_count, 2, width, levels), F32),
            pltpu.VMEM(share.shape, F32),
            pltpu.SemaphoreType.DMA((3 * local_count + 1,)),
        ],
        micros=0.4,
    )
    return risk_map, source_gradient, initial_adjoint


def solution(mesh):
    return jax.shard_map(
        on_device,
        mesh=mesh,
        in_specs=(
            P(("groups", "samples")),
            P(),
            P("gx", "gy", None),
            P("gx", "gy", None),
            P(("groups", "samples"), "gx", "gy", None),
            P("gx", "gy"),
            P(),
            P(None, ("groups", "samples"), "gx", "gy", None),
        ),
        out_specs=(
            P(("groups", "gx"), "gy"),
            P(("groups", "gx", "samples"), "gy", None),
            P(("groups", "samples"), "gx", "gy", None),
        ),
        check_vma=False,
    )
```

time: 40.6 us -> 36.5 us (0.90)
  starting transfers between devices: 21.4 us -> 19.5 us
  waiting for transfers between devices: 6.24 us -> 4.68 us
  Pallas kernels: 12.1 us -> 11.4 us
    ppermute x4, starting transfers between devices: 12.5 us -> 10.3 us  [exchange_x(): lax.ppermute(to_low, 'gx', backward)]
    ppermute x4, starting transfers between devices: 3.2 us -> 5.17 us  [exchange_x(): lax.ppermute(to_high, 'gx', forward)]
    ppermute x2, waiting for transfers between devices: 1.72 us -> 0.01 us  [rotate(): lax.ppermute(block, axis, [(i, (i + hop) % count) for i in range(count)])]
    ppermute x7 -> x4, starting transfers between devices: 1.09 us -> 0.02 us  [swap_y(): return lax.ppermute(block, 'gy', [(0, 1), (1, 0)])]
    ppermute x7 -> x4, waiting for transfers between devices: 2.77 us -> 3.55 us  [swap_y(): return lax.ppermute(block, 'gy', [(0, 1), (1, 0)])]
    pallas_call x14, Pallas kernels: 12.1 us -> 11.4 us  [call(): pl.pallas_call(body, name=name, out_shape=outs, in_specs=in_specs or [VME...]
    ppermute x4, waiting for transfers between devices: 1.74 us -> 1.12 us  [exchange_x(): lax.ppermute(to_high, 'gx', forward)]
    ppermute x2, starting transfers between devices: 4.56 us -> 3.99 us  [rotate(): lax.ppermute(block, axis, [(i, (i + hop) % count) for i in range(count)])]
  transfers between devices with their start and end apart: 17 -> 14, of which waited for: 6 -> 6; matrix products, arithmetic and copies ran while one was open for 0% -> 0% of each run, Pallas kernels for 18% -> 20%
where the time goes in v3:
time: 36.5 us; the launch traced here: 36.4 us
  starting transfers between devices  19.5 us (53%)
  Pallas kernels  11.4 us (31%)
  waiting for transfers between devices  4.68 us (13%)
  between operations  0.72 us (2%)
    pallas_call x14, Pallas kernels, call(): pl.pallas_call(body, name=name, out_shape=outs, in_specs=in_specs or [VME...  11.4 us
    ppermute x4, starting transfers between devices, exchange_x(): lax.ppermute(to_low, 'gx', backward)  10.3 us
    ppermute x4, starting transfers between devices, exchange_x(): lax.ppermute(to_high, 'gx', forward)  5.17 us
    ppermute x2, starting transfers between devices, rotate(): lax.ppermute(block, axis, [(i, (i + hop) % count) for i in range(count)])  3.99 us
    ppermute x4, waiting for transfers between devices, swap_y(): return lax.ppermute(block, 'gy', [(0, 1), (1, 0)])  3.55 us
    ppermute x4, waiting for transfers between devices, exchange_x(): lax.ppermute(to_high, 'gx', forward)  1.12 us
  transfers between devices with their start and end apart: 14, of which 6 were waited for; matrix products, arithmetic and copies ran while one was open for 0% of the time, Pallas kernels for 20%

profile of v3, /device:TPU:0, one launch (start us, length us, event | category | flops | bytes accessed | tf_op | source)
XLA Modules:
  0.0 36.4 jit_solution(12055497224189296772)
XLA Ops:
  0.6 1.6 %surface.1 = (f32[4,512]{1,0:T(4,128)S(1)}, f32[1,128]{1,0:T(1,128)S(1)}) custom-call(bf16[5,4,8,64,128]{4,3,2,1,0:T(8,128)(2,1)} %states_ref.3, f32[1,128]{1,0:T(1,128)} %bitcast.3), custom_call_target="tpu_custom_call" | custom-call | flops 1000000 | bytes 3000000 | tf_op jit(solution)/shard_map/surface/pallas_call | solution.py:23
  2.2 3.0 %collective-permute-start = (f32[4,512]{1,0:T(4,128)S(1)}, f32[4,512]{1,0:T(4,128)S(1)}, u32[]{:S(2)}, u32[]{:S(2)}) collective-permute-start(f32[4,512]{1,0:T(4,128)S(1)} %get-tuple-element.52.refs_0_), channel_id=1, source_target_pairs={{0,2},{2,0},{1,3},{3,1},{4,6},{6,4},{5,7},{7,5},{8,10},{10,8},{9,1... | collective-permute-start | bytes 24584 | tf_op jit(solution)/shard_map/ppermute | solution.py:353
  5.3 2.7 %load.1 = (f32[4,3,128]{2,1,0:T(4,128)S(1)}, s32[4,8,64,128]{3,2,1,0:T(8,128)S(1)}, f32[8,64,128]{2,1,0:T(8,128)S(1)}, f32[8,64,128]{2,1,0:T(8,128)S(1)}, bf16[4...) custom-call(s32[4]{0:T(128)S(1)} %copy-done, s32[4,8,64,128]{3,2,1,0:T(8,128)} %flags_ref.1, ...), custom_call_target="tpu_custom_call" | custom-call | flops 1000000 | bytes 3000000 | tf_op jit(solution)/shard_map/load/pallas_call | solution.py:23
  8.0 0.0 collective-permute-done.refs_1_
  8.0 0.1 moments.1
  8.1 0.0 collective-permute-start.1
  8.1 1.6 %collective-permute-start.2 = (f32[4,64]{1,0:T(4,128)S(1)}, f32[4,64]{1,0:T(4,128)S(1)}, u32[]{:S(2)}, u32[]{:S(2)}) collective-permute-start(f32[4,64]{1,0:T(4,128)S(1)} %get-tuple-element.59), channel_id=1, source_target_pairs={{0,4},{4,8},{8,12},{12,0},{1,5},{5,9},{9,13},{13,1},{2,6},{6,10},{... | collective-permute-start | bytes 3080 | tf_op jit(solution)/shard_map/ppermute | solution.py:344
  9.7 2.2 %collective-permute-start.3 = (f32[4,64]{1,0:T(4,128)S(1)}, f32[4,64]{1,0:T(4,128)S(1)}, u32[]{:S(2)}, u32[]{:S(2)}) collective-permute-start(f32[4,64]{1,0:T(4,128)S(1)} %get-tuple-element.60), channel_id=1, source_target_pairs={{4,0},{8,4},{12,8},{0,12},{5,1},{9,5},{13,9},{1,13},{6,2},{10,6},{... | collective-permute-start | bytes 3080 | tf_op jit(solution)/shard_map/ppermute | solution.py:344
  12.0 0.4 final.1
  12.3 0.9 %inner3.1 = (f32[4,6,64,128]{3,2,1,0:T(8,128)S(1)}, f32[4,8,128]{2,1,0:T(8,128)S(1)}, f32[6,64,128]{2,1,0:T(8,128)S(1)}) custom-call(f32[4,2,64,128]{3,2,1,0:T(8,128)S(1)} %get-tuple-element.57.edge_ref, f32[4,6,64,128]{3,2,1,0:T(8,128)S(1)} %get-tuple-element.58.inner_ref, f32[4,8,128]{2,1,0:T(8,128)S(1)} %get-tuple-element.61.beside_ref, ...), custom_call_target="tpu_custom_call" | custom-call | flops 1000000 | bytes 3000000 | tf_op jit(solution)/shard_map/inner3/pallas_call | solution.py:23
  13.3 0.3 collective-permute-done.2.low_ref
  13.5 0.0 collective-permute-done.3.high_ref
  13.6 0.2 halo.1
  13.8 0.3 edge3.1
  14.1 1.4 %collective-permute-start.4 = (bf16[4,64,128]{2,1,0:T(8,128)(2,1)S(1)}, bf16[4,64,128]{2,1,0:T(8,128)(2,1)S(1)}, u32[]{:S(2)}, u32[]{:S(2)}) collective-permute-start(bf16[4,64,128]{2,1,0:T(8,128)(2,1)S(1)} %get-tuple-element.73), channel_id=1, source_target_pairs={{0,4},{4,8},{8,12},{12,0},{1,5},{5,9},{9,13},{13,1},{2,6},{6,10},{... | collective-permute-start | bytes 196616 | tf_op jit(solution)/shard_map/ppermute | solution.py:344
  15.5 2.5 %collective-permute-start.5 = (bf16[4,64,128]{2,1,0:T(8,128)(2,1)S(1)}, bf16[4,64,128]{2,1,0:T(8,128)(2,1)S(1)}, u32[]{:S(2)}, u32[]{:S(2)}) collective-permute-start(bf16[4,64,128]{2,1,0:T(8,128)(2,1)S(1)} %get-tuple-element.74), channel_id=1, source_target_pairs={{4,0},{8,4},{12,8},{0,12},{5,1},{9,5},{13,9},{1,13},{6,2},{10,6},{... | collective-permute-start | bytes 196616 | tf_op jit(solution)/shard_map/ppermute | solution.py:344
  18.0 1.2 %collective-permute-done.6.beside_ref = f32[4,8,128]{2,1,0:T(8,128)S(1)} collective-permute-done((f32[4,8,128]{2,1,0:T(8,128)S(1)}, f32[4,8,128]{2,1,0:T(8,128)S(1)}, u32[]{:S(2)}, u32[]{:S(2)}) %collective-permute-start.6) | collective-permute-done | bytes 16416 | tf_op jit(solution)/shard_map/ppermute | solution.py:348
  19.2 1.0 %inner2.1 = (f32[4,6,64,128]{3,2,1,0:T(8,128)S(1)}, f32[4,8,128]{2,1,0:T(8,128)S(1)}, f32[6,64,128]{2,1,0:T(8,128)S(1)}) custom-call(f32[4,2,64,128]{3,2,1,0:T(8,128)S(1)} %get-tuple-element.71.edge_ref, f32[4,6,64,128]{3,2,1,0:T(8,128)S(1)} %get-tuple-element.72.inner_ref, f32[4,8,128]{2,1,0:T(8,128)S(1)} %collective-permute-done.6.beside_ref, ...), custom_call_target="tpu_custom_call" | custom-call | flops 1000000 | bytes 3000000 | tf_op jit(solution)/shard_map/inner2/pallas_call | solution.py:23
  20.2 0.7 %collective-permute-done.4.low_ref = bf16[4,64,128]{2,1,0:T(8,128)(2,1)S(1)} collective-permute-done((bf16[4,64,128]{2,1,0:T(8,128)(2,1)S(1)}, bf16[4,64,128]{2,1,0:T(8,128)(2,1)S(1)}, u32[]{:S(2)}, u32[]{:S(2)}) %collective-permute-start.4) | collective-permute-done | bytes 65568 | tf_op jit(solution)/shard_map/ppermute | solution.py:344
  20.9 0.3 edge2.1
  21.2 0.9 %collective-permute-start.7 = (bf16[4,64,128]{2,1,0:T(8,128)(2,1)S(1)}, bf16[4,64,128]{2,1,0:T(8,128)(2,1)S(1)}, u32[]{:S(2)}, u32[]{:S(2)}) collective-permute-start(bf16[4,64,128]{2,1,0:T(8,128)(2,1)S(1)} %get-tuple-element.81), channel_id=1, source_target_pairs={{0,4},{4,8},{8,12},{12,0},{1,5},{5,9},{9,13},{13,1},{2,6},{6,10},{... | collective-permute-start | bytes 196616 | tf_op jit(solution)/shard_map/ppermute | solution.py:344
  22.2 2.9 %collective-permute-start.8 = (bf16[4,64,128]{2,1,0:T(8,128)(2,1)S(1)}, bf16[4,64,128]{2,1,0:T(8,128)(2,1)S(1)}, u32[]{:S(2)}, u32[]{:S(2)}) collective-permute-start(bf16[4,64,128]{2,1,0:T(8,128)(2,1)S(1)} %get-tuple-element.82), channel_id=1, source_target_pairs={{4,0},{8,4},{12,8},{0,12},{5,1},{9,5},{13,9},{1,13},{6,2},{10,6},{... | collective-permute-start | bytes 196616 | tf_op jit(solution)/shard_map/ppermute | solution.py:344
  25.1 1.2 %collective-permute-done.9.beside_ref = f32[4,8,128]{2,1,0:T(8,128)S(1)} collective-permute-done((f32[4,8,128]{2,1,0:T(8,128)S(1)}, f32[4,8,128]{2,1,0:T(8,128)S(1)}, u32[]{:S(2)}, u32[]{:S(2)}) %collective-permute-start.9) | collective-permute-done | bytes 16416 | tf_op jit(solution)/shard_map/ppermute | solution.py:348
  26.3 0.9 %inner1.1 = (f32[4,6,64,128]{3,2,1,0:T(8,128)S(1)}, f32[4,8,128]{2,1,0:T(8,128)S(1)}, f32[6,64,128]{2,1,0:T(8,128)S(1)}) custom-call(f32[4,2,64,128]{3,2,1,0:T(8,128)S(1)} %get-tuple-element.79.edge_ref, f32[4,6,64,128]{3,2,1,0:T(8,128)S(1)} %get-tuple-element.80.inner_ref, f32[4,8,128]{2,1,0:T(8,128)S(1)} %collective-permute-done.9.beside_ref, ...), custom_call_target="tpu_custom_call" | custom-call | flops 1000000 | bytes 3000000 | tf_op jit(solution)/shard_map/inner1/pallas_call | solution.py:23
  27.2 0.2 collective-permute-done.7.low_ref
  27.4 0.3 edge1.1
  27.8 1.0 %collective-permute-start.13 = (f32[4,64,128]{2,1,0:T(8,128)S(1)}, f32[4,64,128]{2,1,0:T(8,128)S(1)}, u32[]{:S(2)}, u32[]{:S(2)}) collective-permute-start(f32[4,64,128]{2,1,0:T(8,128)S(1)} %get-tuple-element.97), channel_id=1, source_target_pairs={{0,2},{2,0},{1,3},{3,1},{4,6},{6,4},{5,7},{7,5},{8,10},{10,8},{9,1... | collective-permute-start | bytes 393224 | tf_op jit(solution)/shard_map/ppermute | solution.py:353
  28.8 1.2 %collective-permute-start.11 = (bf16[4,64,128]{2,1,0:T(8,128)(2,1)S(1)}, bf16[4,64,128]{2,1,0:T(8,128)(2,1)S(1)}, u32[]{:S(2)}, u32[]{:S(2)}) collective-permute-start(bf16[4,64,128]{2,1,0:T(8,128)(2,1)S(1)} %get-tuple-element.93), channel_id=1, source_target_pairs={{0,4},{4,8},{8,12},{12,0},{1,5},{5,9},{9,13},{13,1},{2,6},{6,10},{... | collective-permute-start | bytes 196616 | tf_op jit(solution)/shard_map/ppermute | solution.py:344
  30.0 2.6 %collective-permute-start.12 = (bf16[4,64,128]{2,1,0:T(8,128)(2,1)S(1)}, bf16[4,64,128]{2,1,0:T(8,128)(2,1)S(1)}, u32[]{:S(2)}, u32[]{:S(2)}) collective-permute-start(bf16[4,64,128]{2,1,0:T(8,128)(2,1)S(1)} %get-tuple-element.94), channel_id=1, source_target_pairs={{4,0},{8,4},{12,8},{0,12},{5,1},{9,5},{13,9},{1,13},{6,2},{10,6},{... | collective-permute-start | bytes 196616 | tf_op jit(solution)/shard_map/ppermute | solution.py:344
  32.6 1.2 %collective-permute-done.10.beside_ref = f32[4,8,128]{2,1,0:T(8,128)S(1)} collective-permute-done((f32[4,8,128]{2,1,0:T(8,128)S(1)}, f32[4,8,128]{2,1,0:T(8,128)S(1)}, u32[]{:S(2)}, u32[]{:S(2)}) %collective-permute-start.10) | collective-permute-done | bytes 16416 | tf_op jit(solution)/shard_map/ppermute | solution.py:348
  33.8 1.4 %inner0.1 = (f32[4,6,64,128]{3,2,1,0:T(8,128)S(1)}, f32[8,64]{1,0:T(8,128)}) custom-call(f32[4,2,64,128]{3,2,1,0:T(8,128)S(1)} %get-tuple-element.87.edge_ref, f32[4,6,64,128]{3,2,1,0:T(8,128)S(1)} %get-tuple-element.88.inner_ref, f32[4,8,128]{2,1,0:T(8,128)S(1)} %collective-permute-done.10.beside_ref, ...), custom_call_target="tpu_custom_call" | custom-call | flops 1000000 | bytes 3000000 | tf_op jit(solution)/shard_map/inner0/pallas_call | solution.py:23
  35.2 1.1 %edge0.1 = (f32[4,8,64,128]{3,2,1,0:T(8,128)}, f32[4,64,128]{2,1,0:T(8,128)}) custom-call(f32[4,2,64,128]{3,2,1,0:T(8,128)S(1)} %get-tuple-element.87.edge_ref, f32[4,6,64,128]{3,2,1,0:T(8,128)S(1)} %get-tuple-element.88.inner_ref, bf16[4,64,128]{2,1,0:T(8,128)(2,1)S(1)} %collective-permute-done.11.low_ref, ...), custom_call_target="tpu_custom_call" | custom-call | flops 400000 | bytes 1200000 | tf_op jit(solution)/shard_map/edge0/pallas_call | solution.py:23
  (12 shorter events, 0.1 us)
Async XLA Ops:
  0.6 4.6 %copy-start = (s32[4]{0:T(128)S(1)}, s32[4]{0:T(128)}, u32[]{:S(2)}) copy-start(s32[4]{0:T(128)} %seeds_ref.1) | copy-start | bytes 52
  2.2 5.7 %collective-permute-start = (f32[4,512]{1,0:T(4,128)S(1)}, f32[4,512]{1,0:T(4,128)S(1)}, u32[]{:S(2)}, u32[]{:S(2)}) collective-permute-start(f32[4,512]{1,0:T(4,128)S(1)} %get-tuple-element.52.refs_0_), channel_id=1, source_target_pairs={{0,2},{2,0},{1,3},{3,1},{4,6},{6,4},{5,7},{7,5},{8,10},{10,8},{9,1... | collective-permute-start | bytes 24584 | tf_op jit(solution)/shard_map/ppermute | solution.py:353
  8.1 3.9 %collective-permute-start.1 = (f32[4,512]{1,0:T(4,128)S(1)}, f32[4,512]{1,0:T(4,128)S(1)}, u32[]{:S(2)}, u32[]{:S(2)}) collective-permute-start(f32[4,512]{1,0:T(4,128)S(1)} %get-tuple-element.56.sens_ref), channel_id=1, source_target_pairs={{0,1},{1,0},{2,3},{3,2},{4,5},{5,4},{6,7},{7,6},{8,9},{9,8},{10,11... | collective-permute-start | bytes 24584 | tf_op jit(solution)/shard_map/ppermute | solution.py:348
  8.1 5.4 %collective-permute-start.2 = (f32[4,64]{1,0:T(4,128)S(1)}, f32[4,64]{1,0:T(4,128)S(1)}, u32[]{:S(2)}, u32[]{:S(2)}) collective-permute-start(f32[4,64]{1,0:T(4,128)S(1)} %get-tuple-element.59), channel_id=1, source_target_pairs={{0,4},{4,8},{8,12},{12,0},{1,5},{5,9},{9,13},{13,1},{2,6},{6,10},{... | collective-permute-start | bytes 3080 | tf_op jit(solution)/shard_map/ppermute | solution.py:344
  9.7 3.8 %collective-permute-start.3 = (f32[4,64]{1,0:T(4,128)S(1)}, f32[4,64]{1,0:T(4,128)S(1)}, u32[]{:S(2)}, u32[]{:S(2)}) collective-permute-start(f32[4,64]{1,0:T(4,128)S(1)} %get-tuple-element.60), channel_id=1, source_target_pairs={{4,0},{8,4},{12,8},{0,12},{5,1},{9,5},{13,9},{1,13},{6,2},{10,6},{... | collective-permute-start | bytes 3080 | tf_op jit(solution)/shard_map/ppermute | solution.py:344
  14.1 6.8 %collective-permute-start.4 = (bf16[4,64,128]{2,1,0:T(8,128)(2,1)S(1)}, bf16[4,64,128]{2,1,0:T(8,128)(2,1)S(1)}, u32[]{:S(2)}, u32[]{:S(2)}) collective-permute-start(bf16[4,64,128]{2,1,0:T(8,128)(2,1)S(1)} %get-tuple-element.73), channel_id=1, source_target_pairs={{0,4},{4,8},{8,12},{12,0},{1,5},{5,9},{9,13},{13,1},{2,6},{6,10},{... | collective-permute-start | bytes 196616 | tf_op jit(solution)/shard_map/ppermute | solution.py:344
  15.5 5.4 %collective-permute-start.5 = (bf16[4,64,128]{2,1,0:T(8,128)(2,1)S(1)}, bf16[4,64,128]{2,1,0:T(8,128)(2,1)S(1)}, u32[]{:S(2)}, u32[]{:S(2)}) collective-permute-start(bf16[4,64,128]{2,1,0:T(8,128)(2,1)S(1)} %get-tuple-element.74), channel_id=1, source_target_pairs={{4,0},{8,4},{12,8},{0,12},{5,1},{9,5},{13,9},{1,13},{6,2},{10,6},{... | collective-permute-start | bytes 196616 | tf_op jit(solution)/shard_map/ppermute | solution.py:344
  18.0 1.2 %collective-permute-start.6 = (f32[4,8,128]{2,1,0:T(8,128)S(1)}, f32[4,8,128]{2,1,0:T(8,128)S(1)}, u32[]{:S(2)}, u32[]{:S(2)}) collective-permute-start(f32[4,8,128]{2,1,0:T(8,128)S(1)} %get-tuple-element.75), channel_id=1, source_target_pairs={{0,1},{1,0},{2,3},{3,2},{4,5},{5,4},{6,7},{7,6},{8,9},{9,8},{10,11... | collective-permute-start | bytes 49160 | tf_op jit(solution)/shard_map/ppermute | solution.py:348
  21.2 6.2 %collective-permute-start.7 = (bf16[4,64,128]{2,1,0:T(8,128)(2,1)S(1)}, bf16[4,64,128]{2,1,0:T(8,128)(2,1)S(1)}, u32[]{:S(2)}, u32[]{:S(2)}) collective-permute-start(bf16[4,64,128]{2,1,0:T(8,128)(2,1)S(1)} %get-tuple-element.81), channel_id=1, source_target_pairs={{0,4},{4,8},{8,12},{12,0},{1,5},{5,9},{9,13},{13,1},{2,6},{6,10},{... | collective-permute-start | bytes 196616 | tf_op jit(solution)/shard_map/ppermute | solution.py:344
  22.2 5.2 %collective-permute-start.8 = (bf16[4,64,128]{2,1,0:T(8,128)(2,1)S(1)}, bf16[4,64,128]{2,1,0:T(8,128)(2,1)S(1)}, u32[]{:S(2)}, u32[]{:S(2)}) collective-permute-start(bf16[4,64,128]{2,1,0:T(8,128)(2,1)S(1)} %get-tuple-element.82), channel_id=1, source_target_pairs={{4,0},{8,4},{12,8},{0,12},{5,1},{9,5},{13,9},{1,13},{6,2},{10,6},{... | collective-permute-start | bytes 196616 | tf_op jit(solution)/shard_map/ppermute | solution.py:344
  25.1 1.2 %collective-permute-start.9 = (f32[4,8,128]{2,1,0:T(8,128)S(1)}, f32[4,8,128]{2,1,0:T(8,128)S(1)}, u32[]{:S(2)}, u32[]{:S(2)}) collective-permute-start(f32[4,8,128]{2,1,0:T(8,128)S(1)} %get-tuple-element.83), channel_id=1, source_target_pairs={{0,1},{1,0},{2,3},{3,2},{4,5},{5,4},{6,7},{7,6},{8,9},{9,8},{10,11... | collective-permute-start | bytes 49160 | tf_op jit(solution)/shard_map/ppermute | solution.py:348
  27.8 7.4 %collective-permute-start.13 = (f32[4,64,128]{2,1,0:T(8,128)S(1)}, f32[4,64,128]{2,1,0:T(8,128)S(1)}, u32[]{:S(2)}, u32[]{:S(2)}) collective-permute-start(f32[4,64,128]{2,1,0:T(8,128)S(1)} %get-tuple-element.97), channel_id=1, source_target_pairs={{0,2},{2,0},{1,3},{3,1},{4,6},{6,4},{5,7},{7,5},{8,10},{10,8},{9,1... | collective-permute-start | bytes 393224 | tf_op jit(solution)/shard_map/ppermute | solution.py:353
  28.8 6.4 %collective-permute-start.11 = (bf16[4,64,128]{2,1,0:T(8,128)(2,1)S(1)}, bf16[4,64,128]{2,1,0:T(8,128)(2,1)S(1)}, u32[]{:S(2)}, u32[]{:S(2)}) collective-permute-start(bf16[4,64,128]{2,1,0:T(8,128)(2,1)S(1)} %get-tuple-element.93), channel_id=1, source_target_pairs={{0,4},{4,8},{8,12},{12,0},{1,5},{5,9},{9,13},{13,1},{2,6},{6,10},{... | collective-permute-start | bytes 196616 | tf_op jit(solution)/shard_map/ppermute | solution.py:344
  30.0 5.2 %collective-permute-start.12 = (bf16[4,64,128]{2,1,0:T(8,128)(2,1)S(1)}, bf16[4,64,128]{2,1,0:T(8,128)(2,1)S(1)}, u32[]{:S(2)}, u32[]{:S(2)}) collective-permute-start(bf16[4,64,128]{2,1,0:T(8,128)(2,1)S(1)} %get-tuple-element.94), channel_id=1, source_target_pairs={{4,0},{8,4},{12,8},{0,12},{5,1},{9,5},{13,9},{1,13},{6,2},{10,6},{... | collective-permute-start | bytes 196616 | tf_op jit(solution)/shard_map/ppermute | solution.py:344
  32.6 1.2 %collective-permute-start.10 = (f32[4,8,128]{2,1,0:T(8,128)S(1)}, f32[4,8,128]{2,1,0:T(8,128)S(1)}, u32[]{:S(2)}, u32[]{:S(2)}) collective-permute-start(f32[4,8,128]{2,1,0:T(8,128)S(1)} %get-tuple-element.89._), channel_id=1, source_target_pairs={{0,1},{1,0},{2,3},{3,2},{4,5},{5,4},{6,7},{7,6},{8,9},{9,8},{10,11... | collective-permute-start | bytes 49160 | tf_op jit(solution)/shard_map/ppermute | solution.py:348

commit v4 on v3

--- a/solution.py
+++ b/solution.py
@@ -10,7 +10,6 @@
 STEPS = 4
 DIFFUSION = 0.05
 KURTOSIS_WEIGHT = 1.0
-INNER_COST = 1.0
 
 F32 = jnp.float32
 BF16 = jnp.bfloat16
@@ -54,16 +53,23 @@
     return block.astype(BF16)
 
 
-def surface_body(states_ref, kernel_ref, surface_ref, kernel_out, buffer, semaphores):
+def surface_body(
+    states_ref, kernel_ref, flags_ref, gust_ref, reaction_ref,
+    surface_ref, kernel_out, flags_out, gust_out, reaction_out, buffer, semaphores
+):
     samples, rows, width, levels = buffer.shape
     copies = [
         pltpu.make_async_copy(states_ref.at[STEPS, k], buffer.at[k], semaphores.at[k])
         for k in range(samples)
     ]
-    copies.append(pltpu.make_async_copy(kernel_ref, kernel_out, semaphores.at[samples]))
+    others = ((kernel_ref, kernel_out), (flags_ref, flags_out), (gust_ref, gust_out), (reaction_ref, reaction_out))
+    copies += [
+        pltpu.make_async_copy(source, target, semaphores.at[samples + i])
+        for i, (source, target) in enumerate(others)
+    ]
     for copy in copies:
         copy.start()
-    copies[-1].wait()
+    copies[samples].wait()
     parts = stack_rows(three_parts(kernel_out[...]), levels)
     for k in range(samples):
         copies[k].wait()
@@ -72,15 +78,16 @@
             parts, flat, (((1,), (1,)), ((), ())), preferred_element_type=F32
         )
         surface_ref[k : k + 1] = product[0:1] + product[1:2] + product[2:3]
+    for copy in copies[samples + 1 :]:
+        copy.wait()
 
 
 def load_body(
-    seeds_ref, flags_ref, gust_ref, reaction_ref, states_ref, mask_ref, table_ref, _,
-    profile_out, flags_out, gust_out, reaction_out, stored_out, receptor_out, mask, table, padded, semaphores
+    seeds_ref, states_ref, mask_ref, table_ref, _,
+    profile_out, stored_out, receptor_out, mask, table, padded, semaphores
 ):
-    samples, rows, width, levels = flags_out.shape
-    pairs = [(table_ref, table), (mask_ref, mask), (gust_ref, gust_out), (reaction_ref, reaction_out)]
-    pairs += [(flags_ref.at[k], flags_out.at[k]) for k in range(samples)]
+    _, samples, rows, width, levels = stored_out.shape
+    pairs = [(table_ref, table), (mask_ref, mask)]
     pairs += [(states_ref.at[step], stored_out.at[step]) for step in range(STEPS)]
     copies = [
         pltpu.make_async_copy(source, target, semaphores.at[i]) for i, (source, target) in enumerate(pairs)
@@ -161,13 +168,6 @@
         run_inner_ref[x - 1] = total[x]
 
 
-def halo_body(low_ref, high_ref, kernel_ref, _, low_out, high_out):
-    right = kernel_rows_of(kernel_ref)
-    for source, target in ((low_ref, low_out), (high_ref, high_out)):
-        for k in range(target.shape[0]):
-            target[k] = outer_rows(source[k : k + 1], right)
-
-
 class Plan:
     def __init__(self, levels):
         lane = lax.broadcasted_iota(jnp.int32, (8, levels), 1)
@@ -230,11 +230,7 @@
     samples, inside, width, levels = inner_ref.shape
     plan = Plan(levels)
     if last:
-        risk_ref, buffer, risk_out = outs
-        for x in range(inside + 2):
-            pair = risk_ref[:, 2 * width * (x // 2) : 2 * width * (x // 2 + 1)]
-            pair = pair if x % 2 == 0 else pltpu.roll(pair, width, 1)
-            risk_out[x : x + 1] = pair[:, :width]
+        (buffer,) = outs
     else:
         buffer, rim_out, run_out = outs
     low_side, high_side, upper = side_flags(levels)
@@ -272,7 +268,9 @@
     plan = Plan(levels)
     copies = []
     if last:
-        pieces, (now_ref, target, source_out, buffer, source, semaphores) = outs[:shards], outs[shards:]
+        pieces, (now_ref, risk_ref, target, source_out, risk_out, buffer, source, risk, semaphores) = (
+            outs[:shards], outs[shards:]
+        )
         for k in range(samples):
             copies.append(
                 pltpu.make_async_copy(
@@ -281,12 +279,22 @@
             )
             copies[-1].start()
         source[...] = sum(piece[...] for piece in pieces)
+        for x in range(inside + 2):
+            pair = risk_ref[:, 2 * width * (x // 2) : 2 * width * (x // 2 + 1)]
+            pair = pair if x % 2 == 0 else pltpu.roll(pair, width, 1)
+            risk[x : x + 1] = pair[:, :width]
         copies.append(pltpu.make_async_copy(source, source_out, semaphores.at[2 * samples]))
+        copies.append(pltpu.make_async_copy(risk, risk_out, semaphores.at[3 * samples + 1]))
+        copies[-2].start()
         copies[-1].start()
     else:
-        rim_ref, buffer, low_out, high_out, rim_out, run_out = outs
+        rim_ref, (buffer, low_out, high_out, rim_out, run_out) = outs[0], outs[-5:]
         rim_out[...] = rim_ref[...]
     low_side, high_side, upper = side_flags(levels)
+    right = kernel_rows_of(outs[1]) if low_ref.ndim == 2 else None
+    outer = lambda ref, k: (
+        ref[k].astype(F32) if right is None else outer_rows(ref[k : k + 1], right)
+    )
     for side, x in enumerate((0, inside + 1)):
         gust = gust_ref[x]
         twice = 2.0 * reaction_ref[x]
@@ -294,9 +302,9 @@
         for k in range(samples):
             halo = beside_ref[k, x : x + 1]
             if side == 0:
-                west, east = low_ref[k].astype(F32), inner_ref[k, 0]
+                west, east = outer(low_ref, k), inner_ref[k, 0]
             else:
-                west, east = inner_ref[k, inside - 1], high_ref[k].astype(F32)
+                west, east = inner_ref[k, inside - 1], outer(high_ref, k)
             tiles = step_row(
                 plan, edge_ref[k, side], west, east, halo * low_side, halo * high_side,
                 flags_ref[k, x], gust, twice, stored_ref[step, k, x].astype(F32),
@@ -357,49 +365,52 @@
     local_count, rows, width, levels = flags.shape
     shards = lax.axis_size("samples")
     inside = rows - 2
-    slab = shape(local_count, width, levels)
     rim = shape(local_count, rows, levels)
     flat = shape(local_count, rows * width)
     hold = lambda value: pltpu.with_memory_space_constraint(value, pltpu.HBM)
     states = hold(states)
 
-    surface, kernel_row = call(
+    surface, kernel_row, *fixed = call(
         surface_body,
-        (flat, shape(1, levels)),
-        (states, hold(kernel[None, :])),
+        (
+            flat,
+            shape(1, levels),
+            shape(*flags.shape, dtype=flags.dtype),
+            shape(*gust.shape),
+            shape(*reaction.shape),
+        ),
+        (states, hold(kernel[None, :]), hold(flags), hold(gust), hold(reaction)),
         "surface",
-        in_specs=[HBM] * 2,
+        in_specs=[HBM] * 5,
         scratch=[
             pltpu.VMEM((local_count, rows, width, levels), BF16),
-            pltpu.SemaphoreType.DMA((local_count + 1,)),
+            pltpu.SemaphoreType.DMA((local_count + 4,)),
         ],
     )
     table = jnp.swapaxes(wind_profiles, 0, 1)
-    *fixed, receptor = call(
+    profile, stored, receptor = call(
         load_body,
         (
             shape(local_count, 3, levels),
-            shape(*flags.shape, dtype=flags.dtype),
-            shape(*gust.shape),
-            shape(*reaction.shape),
             shape(STEPS, *flags.shape, dtype=states.dtype),
             shape(1, rows * width),
         ),
-        (seeds, hold(flags), hold(gust), hold(reaction), states, hold(mask), hold(table), kernel_row),
+        (seeds, states, hold(mask), hold(table), kernel_row),
         "load",
-        in_specs=[pl.BlockSpec(memory_space=pltpu.SMEM)] + [HBM] * 6 + [VMEM],
+        in_specs=[pl.BlockSpec(memory_space=pltpu.SMEM)] + [HBM] * 3 + [VMEM],
         scratch=[
             pltpu.VMEM(mask.shape, mask.dtype),
             pltpu.VMEM(table.shape, F32),
             pltpu.VMEM((rows, 2 * width), F32),
-            pltpu.SemaphoreType.DMA((local_count + STEPS + 4,)),
+            pltpu.SemaphoreType.DMA((STEPS + 2,)),
         ],
     )
+    fixed = (profile, *fixed, stored)
     others = [rotate(surface, "samples", hop) for hop in range(1, shards)]
     risk, sensitivity, low_sens, high_sens = call(
         functools.partial(moments_body, shards),
         (shape(1, rows * width), flat) + (shape(local_count, width),) * 2,
-        (surface, *others, receptor, fixed[0]),
+        (surface, *others, receptor, profile),
         "moments",
         micros=0.1,
     )
@@ -415,7 +426,7 @@
         ),
         (sensitivity, swap_y(sensitivity), kernel_row),
         "final",
-        micros=INNER_COST,
+        micros=1.0,
     )
     for step in range(STEPS - 1, 0, -1):
         inner_now, rim_inner, run_inner = call(
@@ -423,12 +434,8 @@
             (shape(local_count, inside, width, levels), rim, shape(inside, width, levels)),
             (edge, inner, beside, run_inner, *fixed),
             f"inner{step}",
-            micros=INNER_COST,
-        )
-        if step == STEPS - 1:
-            low, high = call(
-                halo_body, (slab,) * 2, (low, high, kernel_row, rim_inner), "halo", micros=0.1
-            )
+            micros=1.0,
+        )
         edge, to_low, to_high, rim_all, run_edge = call(
             functools.partial(edge_body, step, False, 0),
             (
@@ -438,7 +445,8 @@
                 rim,
                 shape(2, width, levels),
             ),
-            (edge, inner, low, high, beside, run_edge, *fixed, rim_inner),
+            (edge, inner, low, high, beside, run_edge, *fixed, rim_inner)
+            + ((kernel_row,) if step == STEPS - 1 else ()),
             f"edge{step}",
             micros=0.4,
         )
@@ -456,23 +464,24 @@
         micros=0.1,
     )
     pieces = [pieces[0]] + [rotate(pieces[hop], "samples", hop) for hop in range(1, shards)]
-    inner_now, risk_map = call(
+    inner_now = call(
         functools.partial(inner_body, 0, True),
-        (shape(local_count, inside, width, levels), shape(rows, width)),
-        (edge, inner, beside, run_inner, *fixed, risk),
+        shape(local_count, inside, width, levels),
+        (edge, inner, beside, run_inner, *fixed),
         "inner0",
-        micros=INNER_COST,
-    )
-    initial_adjoint, source_gradient = call(
+        micros=1.0,
+    )
+    initial_adjoint, source_gradient, risk_map = call(
         functools.partial(edge_body, 0, True, shards),
-        (shape(*flags.shape), share),
-        (edge, inner, low, high, beside, run_edge, *fixed, *pieces, inner_now),
+        (shape(*flags.shape), share, shape(rows, width)),
+        (edge, inner, low, high, beside, run_edge, *fixed, *pieces, inner_now, risk),
         "edge0",
-        out_specs=(HBM, HBM),
+        out_specs=(HBM,) * 3,
         scratch=[
             pltpu.VMEM((local_count, 2, width, levels), F32),
             pltpu.VMEM(share.shape, F32),
-            pltpu.SemaphoreType.DMA((3 * local_count + 1,)),
+            pltpu.VMEM((rows, width), F32),
+            pltpu.SemaphoreType.DMA((3 * local_count + 2,)),
         ],
         micros=0.4,
     )

time: 36.5 us -> 36.3 us (level)
  Pallas kernels: 11.4 us -> 10.5 us
  starting transfers between devices: 19.5 us -> 20 us
    pallas_call x14 -> x13, Pallas kernels: 11.4 us -> 10.5 us  [call(): pl.pallas_call(body, name=name, out_shape=outs, in_specs=in_specs or [VME...]
    ppermute x2, starting transfers between devices: 3.99 us -> 4.52 us  [rotate(): lax.ppermute(block, axis, [(i, (i + hop) % count) for i in range(count)])]
  transfers between devices with their start and end apart: 14 -> 14, of which waited for: 6 -> 7; matrix products, arithmetic and copies ran while one was open for 0% -> 0% of each run, Pallas kernels for 20% -> 18%
where the time goes in v4:
time: 36.3 us; the launch traced here: 36.1 us
  starting transfers between devices  20 us (55%)
  Pallas kernels  10.5 us (29%)
  waiting for transfers between devices  4.92 us (14%)
  between operations  0.72 us (2%)
    pallas_call x13, Pallas kernels, call(): pl.pallas_call(body, name=name, out_shape=outs, in_specs=in_specs or [VME...  10.5 us
    ppermute x4, starting transfers between devices, exchange_x(): lax.ppermute(to_low, 'gx', backward)  10.2 us
    ppermute x4, starting transfers between devices, exchange_x(): lax.ppermute(to_high, 'gx', forward)  5.27 us
    ppermute x2, starting transfers between devices, rotate(): lax.ppermute(block, axis, [(i, (i + hop) % count) for i in range(count)])  4.52 us
    ppermute x4, waiting for transfers between devices, swap_y(): return lax.ppermute(block, 'gy', [(0, 1), (1, 0)])  3.55 us
    ppermute x4, waiting for transfers between devices, exchange_x(): lax.ppermute(to_high, 'gx', forward)  1.36 us
  transfers between devices with their start and end apart: 14, of which 7 were waited for; matrix products, arithmetic and copies ran while one was open for 0% of the time, Pallas kernels for 18%

profile of v4, /device:TPU:0, one launch (start us, length us, event | category | flops | bytes accessed | tf_op | source)
XLA Modules:
  0.0 36.1 jit_solution(3268253359842873336)
XLA Ops:
  0.6 1.7 %surface.1 = (f32[4,512]{1,0:T(4,128)S(1)}, f32[1,128]{1,0:T(1,128)S(1)}, s32[4,8,64,128]{3,2,1,0:T(8,128)S(1)}, f32[8,64,128]{2,1,0:T(8,128)S(1)}, f32[8,64,128]{2,1,0:T(8,128)S(1)}) custom-call(bf16[5,4,8,64,128]{4,3,2,1,0:T(8,128)(2,1)} %states_ref.3, f32[1,128]{1,0:T(1,128)} %bitcast.3, s32[4,8,64,128]{3,2,1,0:T(8,128)} %flags_ref.1, ...), custom_call_target="tpu_custom_call" | custom-call | flops 1000000 | bytes 3000000 | tf_op jit(solution)/shard_map/surface/pallas_call | solution.py:22
  2.3 3.0 %collective-permute-start = (f32[4,512]{1,0:T(4,128)S(1)}, f32[4,512]{1,0:T(4,128)S(1)}, u32[]{:S(2)}, u32[]{:S(2)}) collective-permute-start(f32[4,512]{1,0:T(4,128)S(1)} %get-tuple-element.49.refs_0_), channel_id=1, source_target_pairs={{0,2},{2,0},{1,3},{3,1},{4,6},{6,4},{5,7},{7,5},{8,10},{10,8},{9,1... | collective-permute-start | bytes 24584 | tf_op jit(solution)/shard_map/ppermute | solution.py:361
  5.4 2.2 %load.1 = (f32[4,3,128]{2,1,0:T(4,128)S(1)}, bf16[4,4,8,64,128]{4,3,2,1,0:T(8,128)(2,1)S(1)}, f32[1,512]{1,0:T(1,128)S(1)}) custom-call(s32[4]{0:T(128)S(1)} %copy-done, bf16[5,4,8,64,128]{4,3,2,1,0:T(8,128)(2,1)} %states_ref.3, s32[8,64]{1,0:T(8,128)} %mask_ref.1, f32[3,64,128]{2,1,0:T(8,128)} %bitcast.2, f32[1,128]{1,0:T(1,128)S(1)} %get-tuple-element.50._.kernel_ref.outs_1_), custom_call_target="tpu_custom_call" | custom-call | flops 1000000 | bytes 3000000 | tf_op jit(solution)/shard_map/load/pallas_call | solution.py:22
  7.5 0.0 collective-permute-done.refs_1_
  7.6 0.1 moments.1
  7.7 0.0 collective-permute-start.1
  7.7 1.6 %collective-permute-start.2 = (f32[4,64]{1,0:T(4,128)S(1)}, f32[4,64]{1,0:T(4,128)S(1)}, u32[]{:S(2)}, u32[]{:S(2)}) collective-permute-start(f32[4,64]{1,0:T(4,128)S(1)} %get-tuple-element.56), channel_id=1, source_target_pairs={{0,4},{4,8},{8,12},{12,0},{1,5},{5,9},{9,13},{13,1},{2,6},{6,10},{... | collective-permute-start | bytes 3080 | tf_op jit(solution)/shard_map/ppermute | solution.py:352
  9.3 2.2 %collective-permute-start.3 = (f32[4,64]{1,0:T(4,128)S(1)}, f32[4,64]{1,0:T(4,128)S(1)}, u32[]{:S(2)}, u32[]{:S(2)}) collective-permute-start(f32[4,64]{1,0:T(4,128)S(1)} %get-tuple-element.57), channel_id=1, source_target_pairs={{4,0},{8,4},{12,8},{0,12},{5,1},{9,5},{13,9},{1,13},{6,2},{10,6},{... | collective-permute-start | bytes 3080 | tf_op jit(solution)/shard_map/ppermute | solution.py:352
  11.6 0.0 collective-permute-done.1.beside_ref
  11.6 0.4 final.1
  11.9 1.0 %inner3.1 = (f32[4,6,64,128]{3,2,1,0:T(8,128)S(1)}, f32[4,8,128]{2,1,0:T(8,128)S(1)}, f32[6,64,128]{2,1,0:T(8,128)S(1)}) custom-call(f32[4,2,64,128]{3,2,1,0:T(8,128)S(1)} %get-tuple-element.54.edge_ref, f32[4,6,64,128]{3,2,1,0:T(8,128)S(1)} %get-tuple-element.55.inner_ref, f32[4,8,128]{2,1,0:T(8,128)S(1)} %get-tuple-element.58.beside_ref, ...), custom_call_target="tpu_custom_call" | custom-call | flops 1000000 | bytes 3000000 | tf_op jit(solution)/shard_map/inner3/pallas_call | solution.py:22
  12.9 0.2 collective-permute-done.2.low_ref
  13.1 0.5 %edge3.1 = (f32[4,2,64,128]{3,2,1,0:T(8,128)S(1)}, bf16[4,64,128]{2,1,0:T(8,128)(2,1)S(1)}, bf16[4,64,128]{2,1,0:T(8,128)(2,1)S(1)}, f32[4,8,128]{2,1,0:T(8,128)S(1)}, f32[2,64,128]{2,1,0:T(8,128)S(1)}) custom-call(f32[4,2,64,128]{3,2,1,0:T(8,128)S(1)} %get-tuple-element.54.edge_ref, f32[4,6,64,128]{3,2,1,0:T(8,128)S(1)} %get-tuple-element.55.inner_ref, ...), custom_call_target="tpu_custom_call" | custom-call | flops 400000 | bytes 1200000 | tf_op jit(solution)/shard_map/edge3/pallas_call | solution.py:22
  13.6 1.4 %collective-permute-start.4 = (bf16[4,64,128]{2,1,0:T(8,128)(2,1)S(1)}, bf16[4,64,128]{2,1,0:T(8,128)(2,1)S(1)}, u32[]{:S(2)}, u32[]{:S(2)}) collective-permute-start(bf16[4,64,128]{2,1,0:T(8,128)(2,1)S(1)} %get-tuple-element.68), channel_id=1, source_target_pairs={{0,4},{4,8},{8,12},{12,0},{1,5},{5,9},{9,13},{13,1},{2,6},{6,10},{... | collective-permute-start | bytes 196616 | tf_op jit(solution)/shard_map/ppermute | solution.py:352
  15.0 2.5 %collective-permute-start.5 = (bf16[4,64,128]{2,1,0:T(8,128)(2,1)S(1)}, bf16[4,64,128]{2,1,0:T(8,128)(2,1)S(1)}, u32[]{:S(2)}, u32[]{:S(2)}) collective-permute-start(bf16[4,64,128]{2,1,0:T(8,128)(2,1)S(1)} %get-tuple-element.69), channel_id=1, source_target_pairs={{4,0},{8,4},{12,8},{0,12},{5,1},{9,5},{13,9},{1,13},{6,2},{10,6},{... | collective-permute-start | bytes 196616 | tf_op jit(solution)/shard_map/ppermute | solution.py:352
  17.5 1.2 %collective-permute-done.6.beside_ref = f32[4,8,128]{2,1,0:T(8,128)S(1)} collective-permute-done((f32[4,8,128]{2,1,0:T(8,128)S(1)}, f32[4,8,128]{2,1,0:T(8,128)S(1)}, u32[]{:S(2)}, u32[]{:S(2)}) %collective-permute-start.6) | collective-permute-done | bytes 16416 | tf_op jit(solution)/shard_map/ppermute | solution.py:356
  18.7 1.0 %inner2.1 = (f32[4,6,64,128]{3,2,1,0:T(8,128)S(1)}, f32[4,8,128]{2,1,0:T(8,128)S(1)}, f32[6,64,128]{2,1,0:T(8,128)S(1)}) custom-call(f32[4,2,64,128]{3,2,1,0:T(8,128)S(1)} %get-tuple-element.66.edge_ref, f32[4,6,64,128]{3,2,1,0:T(8,128)S(1)} %get-tuple-element.67.inner_ref, f32[4,8,128]{2,1,0:T(8,128)S(1)} %collective-permute-done.6.beside_ref, ...), custom_call_target="tpu_custom_call" | custom-call | flops 1000000 | bytes 3000000 | tf_op jit(solution)/shard_map/inner2/pallas_call | solution.py:22
  19.7 0.6 %collective-permute-done.4.low_ref = bf16[4,64,128]{2,1,0:T(8,128)(2,1)S(1)} collective-permute-done((bf16[4,64,128]{2,1,0:T(8,128)(2,1)S(1)}, bf16[4,64,128]{2,1,0:T(8,128)(2,1)S(1)}, u32[]{:S(2)}, u32[]{:S(2)}) %collective-permute-start.4) | collective-permute-done | bytes 65568 | tf_op jit(solution)/shard_map/ppermute | solution.py:352
  20.3 0.3 edge2.1
  20.6 1.0 %collective-permute-start.7 = (bf16[4,64,128]{2,1,0:T(8,128)(2,1)S(1)}, bf16[4,64,128]{2,1,0:T(8,128)(2,1)S(1)}, u32[]{:S(2)}, u32[]{:S(2)}) collective-permute-start(bf16[4,64,128]{2,1,0:T(8,128)(2,1)S(1)} %get-tuple-element.76), channel_id=1, source_target_pairs={{0,4},{4,8},{8,12},{12,0},{1,5},{5,9},{9,13},{13,1},{2,6},{6,10},{... | collective-permute-start | bytes 196616 | tf_op jit(solution)/shard_map/ppermute | solution.py:352
  21.7 2.8 %collective-permute-start.8 = (bf16[4,64,128]{2,1,0:T(8,128)(2,1)S(1)}, bf16[4,64,128]{2,1,0:T(8,128)(2,1)S(1)}, u32[]{:S(2)}, u32[]{:S(2)}) collective-permute-start(bf16[4,64,128]{2,1,0:T(8,128)(2,1)S(1)} %get-tuple-element.77), channel_id=1, source_target_pairs={{4,0},{8,4},{12,8},{0,12},{5,1},{9,5},{13,9},{1,13},{6,2},{10,6},{... | collective-permute-start | bytes 196616 | tf_op jit(solution)/shard_map/ppermute | solution.py:352
  24.5 1.2 %collective-permute-done.9.beside_ref = f32[4,8,128]{2,1,0:T(8,128)S(1)} collective-permute-done((f32[4,8,128]{2,1,0:T(8,128)S(1)}, f32[4,8,128]{2,1,0:T(8,128)S(1)}, u32[]{:S(2)}, u32[]{:S(2)}) %collective-permute-start.9) | collective-permute-done | bytes 16416 | tf_op jit(solution)/shard_map/ppermute | solution.py:356
  25.7 1.0 %inner1.1 = (f32[4,6,64,128]{3,2,1,0:T(8,128)S(1)}, f32[4,8,128]{2,1,0:T(8,128)S(1)}, f32[6,64,128]{2,1,0:T(8,128)S(1)}) custom-call(f32[4,2,64,128]{3,2,1,0:T(8,128)S(1)} %get-tuple-element.74.edge_ref, f32[4,6,64,128]{3,2,1,0:T(8,128)S(1)} %get-tuple-element.75.inner_ref, f32[4,8,128]{2,1,0:T(8,128)S(1)} %collective-permute-done.9.beside_ref, ...), custom_call_target="tpu_custom_call" | custom-call | flops 1000000 | bytes 3000000 | tf_op jit(solution)/shard_map/inner1/pallas_call | solution.py:22
  26.7 0.2 collective-permute-done.7.low_ref
  26.8 0.3 edge1.1
  27.2 1.5 %collective-permute-start.13 = (f32[4,64,128]{2,1,0:T(8,128)S(1)}, f32[4,64,128]{2,1,0:T(8,128)S(1)}, u32[]{:S(2)}, u32[]{:S(2)}) collective-permute-start(f32[4,64,128]{2,1,0:T(8,128)S(1)} %get-tuple-element.90), channel_id=1, source_target_pairs={{0,2},{2,0},{1,3},{3,1},{4,6},{6,4},{5,7},{7,5},{8,10},{10,8},{9,1... | collective-permute-start | bytes 393224 | tf_op jit(solution)/shard_map/ppermute | solution.py:361
  28.7 1.2 %collective-permute-start.10 = (bf16[4,64,128]{2,1,0:T(8,128)(2,1)S(1)}, bf16[4,64,128]{2,1,0:T(8,128)(2,1)S(1)}, u32[]{:S(2)}, u32[]{:S(2)}) collective-permute-start(bf16[4,64,128]{2,1,0:T(8,128)(2,1)S(1)} %get-tuple-element.84), channel_id=1, source_target_pairs={{0,4},{4,8},{8,12},{12,0},{1,5},{5,9},{9,13},{13,1},{2,6},{6,10},{... | collective-permute-start | bytes 196616 | tf_op jit(solution)/shard_map/ppermute | solution.py:352
  29.9 2.6 %collective-permute-start.11 = (bf16[4,64,128]{2,1,0:T(8,128)(2,1)S(1)}, bf16[4,64,128]{2,1,0:T(8,128)(2,1)S(1)}, u32[]{:S(2)}, u32[]{:S(2)}) collective-permute-start(bf16[4,64,128]{2,1,0:T(8,128)(2,1)S(1)} %get-tuple-element.85), channel_id=1, source_target_pairs={{4,0},{8,4},{12,8},{0,12},{5,1},{9,5},{13,9},{1,13},{6,2},{10,6},{... | collective-permute-start | bytes 196616 | tf_op jit(solution)/shard_map/ppermute | solution.py:352
  32.5 1.2 %collective-permute-done.12.beside_ref = f32[4,8,128]{2,1,0:T(8,128)S(1)} collective-permute-done((f32[4,8,128]{2,1,0:T(8,128)S(1)}, f32[4,8,128]{2,1,0:T(8,128)S(1)}, u32[]{:S(2)}, u32[]{:S(2)}) %collective-permute-start.12) | collective-permute-done | bytes 16416 | tf_op jit(solution)/shard_map/ppermute | solution.py:356
  33.7 0.9 %inner0.1.outs_2_ = f32[4,6,64,128]{3,2,1,0:T(8,128)S(1)} custom-call(f32[4,2,64,128]{3,2,1,0:T(8,128)S(1)} %get-tuple-element.82.edge_ref, f32[4,6,64,128]{3,2,1,0:T(8,128)S(1)} %get-tuple-element.83.inner_ref, f32[4,8,128]{2,1,0:T(8,128)S(1)} %collective-permute-done.12.beside_ref, f32[6,64,128]{2,1,0:T(8,128)S(1)} %get-tuple-element.88.inner_ref.run_ref, ...), custom_call_target="tpu_custom_call" | custom-call | flops 1000000 | bytes 3000000 | tf_op jit(solution)/shard_map/inner0/pallas_call | solution.py:22
  34.6 0.4 collective-permute-done.10.low_ref
  35.0 1.1 %edge0.1 = (f32[4,8,64,128]{3,2,1,0:T(8,128)}, f32[4,64,128]{2,1,0:T(8,128)}, f32[8,64]{1,0:T(8,128)}) custom-call(f32[4,2,64,128]{3,2,1,0:T(8,128)S(1)} %get-tuple-element.82.edge_ref, f32[4,6,64,128]{3,2,1,0:T(8,128)S(1)} %get-tuple-element.83.inner_ref, bf16[4,64,128]{2,1,0:T(8,128)(2,1)S(1)} %collective-permute-done.10.low_ref, ...), custom_call_target="tpu_custom_call" | custom-call | flops 400000 | bytes 1200000 | tf_op jit(solution)/shard_map/edge0/pallas_call | solution.py:22
  (11 shorter events, 0.1 us)
Async XLA Ops:
  0.6 4.7 %copy-start = (s32[4]{0:T(128)S(1)}, s32[4]{0:T(128)}, u32[]{:S(2)}) copy-start(s32[4]{0:T(128)} %seeds_ref.1) | copy-start | bytes 52
  2.3 5.2 %collective-permute-start = (f32[4,512]{1,0:T(4,128)S(1)}, f32[4,512]{1,0:T(4,128)S(1)}, u32[]{:S(2)}, u32[]{:S(2)}) collective-permute-start(f32[4,512]{1,0:T(4,128)S(1)} %get-tuple-element.49.refs_0_), channel_id=1, source_target_pairs={{0,2},{2,0},{1,3},{3,1},{4,6},{6,4},{5,7},{7,5},{8,10},{10,8},{9,1... | collective-permute-start | bytes 24584 | tf_op jit(solution)/shard_map/ppermute | solution.py:361
  7.7 3.9 %collective-permute-start.1 = (f32[4,512]{1,0:T(4,128)S(1)}, f32[4,512]{1,0:T(4,128)S(1)}, u32[]{:S(2)}, u32[]{:S(2)}) collective-permute-start(f32[4,512]{1,0:T(4,128)S(1)} %get-tuple-element.53.sens_ref), channel_id=1, source_target_pairs={{0,1},{1,0},{2,3},{3,2},{4,5},{5,4},{6,7},{7,6},{8,9},{9,8},{10,11... | collective-permute-start | bytes 24584 | tf_op jit(solution)/shard_map/ppermute | solution.py:356
  7.7 5.4 %collective-permute-start.2 = (f32[4,64]{1,0:T(4,128)S(1)}, f32[4,64]{1,0:T(4,128)S(1)}, u32[]{:S(2)}, u32[]{:S(2)}) collective-permute-start(f32[4,64]{1,0:T(4,128)S(1)} %get-tuple-element.56), channel_id=1, source_target_pairs={{0,4},{4,8},{8,12},{12,0},{1,5},{5,9},{9,13},{13,1},{2,6},{6,10},{... | collective-permute-start | bytes 3080 | tf_op jit(solution)/shard_map/ppermute | solution.py:352
  9.3 3.8 %collective-permute-start.3 = (f32[4,64]{1,0:T(4,128)S(1)}, f32[4,64]{1,0:T(4,128)S(1)}, u32[]{:S(2)}, u32[]{:S(2)}) collective-permute-start(f32[4,64]{1,0:T(4,128)S(1)} %get-tuple-element.57), channel_id=1, source_target_pairs={{4,0},{8,4},{12,8},{0,12},{5,1},{9,5},{13,9},{1,13},{6,2},{10,6},{... | collective-permute-start | bytes 3080 | tf_op jit(solution)/shard_map/ppermute | solution.py:352
  13.6 6.7 %collective-permute-start.4 = (bf16[4,64,128]{2,1,0:T(8,128)(2,1)S(1)}, bf16[4,64,128]{2,1,0:T(8,128)(2,1)S(1)}, u32[]{:S(2)}, u32[]{:S(2)}) collective-permute-start(bf16[4,64,128]{2,1,0:T(8,128)(2,1)S(1)} %get-tuple-element.68), channel_id=1, source_target_pairs={{0,4},{4,8},{8,12},{12,0},{1,5},{5,9},{9,13},{13,1},{2,6},{6,10},{... | collective-permute-start | bytes 196616 | tf_op jit(solution)/shard_map/ppermute | solution.py:352
  15.0 5.3 %collective-permute-start.5 = (bf16[4,64,128]{2,1,0:T(8,128)(2,1)S(1)}, bf16[4,64,128]{2,1,0:T(8,128)(2,1)S(1)}, u32[]{:S(2)}, u32[]{:S(2)}) collective-permute-start(bf16[4,64,128]{2,1,0:T(8,128)(2,1)S(1)} %get-tuple-element.69), channel_id=1, source_target_pairs={{4,0},{8,4},{12,8},{0,12},{5,1},{9,5},{13,9},{1,13},{6,2},{10,6},{... | collective-permute-start | bytes 196616 | tf_op jit(solution)/shard_map/ppermute | solution.py:352
  17.5 1.2 %collective-permute-start.6 = (f32[4,8,128]{2,1,0:T(8,128)S(1)}, f32[4,8,128]{2,1,0:T(8,128)S(1)}, u32[]{:S(2)}, u32[]{:S(2)}) collective-permute-start(f32[4,8,128]{2,1,0:T(8,128)S(1)} %get-tuple-element.70), channel_id=1, source_target_pairs={{0,1},{1,0},{2,3},{3,2},{4,5},{5,4},{6,7},{7,6},{8,9},{9,8},{10,11... | collective-permute-start | bytes 49160 | tf_op jit(solution)/shard_map/ppermute | solution.py:356
  20.6 6.2 %collective-permute-start.7 = (bf16[4,64,128]{2,1,0:T(8,128)(2,1)S(1)}, bf16[4,64,128]{2,1,0:T(8,128)(2,1)S(1)}, u32[]{:S(2)}, u32[]{:S(2)}) collective-permute-start(bf16[4,64,128]{2,1,0:T(8,128)(2,1)S(1)} %get-tuple-element.76), channel_id=1, source_target_pairs={{0,4},{4,8},{8,12},{12,0},{1,5},{5,9},{9,13},{13,1},{2,6},{6,10},{... | collective-permute-start | bytes 196616 | tf_op jit(solution)/shard_map/ppermute | solution.py:352
  21.7 5.2 %collective-permute-start.8 = (bf16[4,64,128]{2,1,0:T(8,128)(2,1)S(1)}, bf16[4,64,128]{2,1,0:T(8,128)(2,1)S(1)}, u32[]{:S(2)}, u32[]{:S(2)}) collective-permute-start(bf16[4,64,128]{2,1,0:T(8,128)(2,1)S(1)} %get-tuple-element.77), channel_id=1, source_target_pairs={{4,0},{8,4},{12,8},{0,12},{5,1},{9,5},{13,9},{1,13},{6,2},{10,6},{... | collective-permute-start | bytes 196616 | tf_op jit(solution)/shard_map/ppermute | solution.py:352
  24.5 1.2 %collective-permute-start.9 = (f32[4,8,128]{2,1,0:T(8,128)S(1)}, f32[4,8,128]{2,1,0:T(8,128)S(1)}, u32[]{:S(2)}, u32[]{:S(2)}) collective-permute-start(f32[4,8,128]{2,1,0:T(8,128)S(1)} %get-tuple-element.78), channel_id=1, source_target_pairs={{0,1},{1,0},{2,3},{3,2},{4,5},{5,4},{6,7},{7,6},{8,9},{9,8},{10,11... | collective-permute-start | bytes 49160 | tf_op jit(solution)/shard_map/ppermute | solution.py:356
  27.2 7.8 %collective-permute-start.13 = (f32[4,64,128]{2,1,0:T(8,128)S(1)}, f32[4,64,128]{2,1,0:T(8,128)S(1)}, u32[]{:S(2)}, u32[]{:S(2)}) collective-permute-start(f32[4,64,128]{2,1,0:T(8,128)S(1)} %get-tuple-element.90), channel_id=1, source_target_pairs={{0,2},{2,0},{1,3},{3,1},{4,6},{6,4},{5,7},{7,5},{8,10},{10,8},{9,1... | collective-permute-start | bytes 393224 | tf_op jit(solution)/shard_map/ppermute | solution.py:361
  28.7 6.3 %collective-permute-start.10 = (bf16[4,64,128]{2,1,0:T(8,128)(2,1)S(1)}, bf16[4,64,128]{2,1,0:T(8,128)(2,1)S(1)}, u32[]{:S(2)}, u32[]{:S(2)}) collective-permute-start(bf16[4,64,128]{2,1,0:T(8,128)(2,1)S(1)} %get-tuple-element.84), channel_id=1, source_target_pairs={{0,4},{4,8},{8,12},{12,0},{1,5},{5,9},{9,13},{13,1},{2,6},{6,10},{... | collective-permute-start | bytes 196616 | tf_op jit(solution)/shard_map/ppermute | solution.py:352
  29.9 5.1 %collective-permute-start.11 = (bf16[4,64,128]{2,1,0:T(8,128)(2,1)S(1)}, bf16[4,64,128]{2,1,0:T(8,128)(2,1)S(1)}, u32[]{:S(2)}, u32[]{:S(2)}) collective-permute-start(bf16[4,64,128]{2,1,0:T(8,128)(2,1)S(1)} %get-tuple-element.85), channel_id=1, source_target_pairs={{4,0},{8,4},{12,8},{0,12},{5,1},{9,5},{13,9},{1,13},{6,2},{10,6},{... | collective-permute-start | bytes 196616 | tf_op jit(solution)/shard_map/ppermute | solution.py:352
  32.5 1.2 %collective-permute-start.12 = (f32[4,8,128]{2,1,0:T(8,128)S(1)}, f32[4,8,128]{2,1,0:T(8,128)S(1)}, u32[]{:S(2)}, u32[]{:S(2)}) collective-permute-start(f32[4,8,128]{2,1,0:T(8,128)S(1)} %get-tuple-element.86._), channel_id=1, source_target_pairs={{0,1},{1,0},{2,3},{3,2},{4,5},{5,4},{6,7},{7,6},{8,9},{9,8},{10,11... | collective-permute-start | bytes 49160 | tf_op jit(solution)/shard_map/ppermute | solution.py:356

commit v5 on v4

--- a/solution.py
+++ b/solution.py
@@ -260,12 +260,32 @@
                 run_out[x - 1, 8 * t : 8 * t + 8] = tile
 
 
-def edge_body(
-    step, last, shards, edge_ref, inner_ref, low_ref, high_ref, beside_ref, run_ref, profile_ref, flags_ref,
-    gust_ref, reaction_ref, stored_ref, *outs
+def part_body(
+    step, edge_ref, inner_ref, beside_ref, profile_ref, flags_ref, gust_ref, reaction_ref, stored_ref, part_ref
 ):
     samples, inside, width, levels = inner_ref.shape
     plan = Plan(levels)
+    low_side, high_side, _ = side_flags(levels)
+    empty = jnp.zeros((width, levels), F32)
+    for side, x in enumerate((0, inside + 1)):
+        gust = gust_ref[x]
+        twice = 2.0 * reaction_ref[x]
+        for k in range(samples):
+            halo = beside_ref[k, x : x + 1]
+            west, east = (empty, inner_ref[k, 0]) if side == 0 else (inner_ref[k, inside - 1], empty)
+            tiles = step_row(
+                plan, edge_ref[k, side], west, east, halo * low_side, halo * high_side,
+                flags_ref[k, x], gust, twice, stored_ref[step, k, x].astype(F32),
+                speeds_of(profile_ref, k, levels),
+            )
+            for t, tile in enumerate(tiles):
+                part_ref[k, side, 8 * t : 8 * t + 8] = tile
+
+
+def edge_body(
+    last, shards, inside, part_ref, low_ref, high_ref, run_ref, profile_ref, flags_ref, gust_ref, *outs
+):
+    samples, _, width, levels = part_ref.shape
     copies = []
     if last:
         pieces, (now_ref, risk_ref, target, source_out, risk_out, buffer, source, risk, semaphores) = (
@@ -290,34 +310,20 @@
     else:
         rim_ref, (buffer, low_out, high_out, rim_out, run_out) = outs[0], outs[-5:]
         rim_out[...] = rim_ref[...]
-    low_side, high_side, upper = side_flags(levels)
+    upper = side_flags(levels)[2]
     right = kernel_rows_of(outs[1]) if low_ref.ndim == 2 else None
     outer = lambda ref, k: (
         ref[k].astype(F32) if right is None else outer_rows(ref[k : k + 1], right)
     )
     for side, x in enumerate((0, inside + 1)):
-        gust = gust_ref[x]
-        twice = 2.0 * reaction_ref[x]
-        total = None if last else [run_ref[side, 8 * t : 8 * t + 8] for t in range(width // 8)]
+        total = None if last else run_ref[side]
+        halo_ref = (low_ref, high_ref)[side]
         for k in range(samples):
-            halo = beside_ref[k, x : x + 1]
-            if side == 0:
-                west, east = outer(low_ref, k), inner_ref[k, 0]
-            else:
-                west, east = inner_ref[k, inside - 1], outer(high_ref, k)
-            tiles = step_row(
-                plan, edge_ref[k, side], west, east, halo * low_side, halo * high_side,
-                flags_ref[k, x], gust, twice, stored_ref[step, k, x].astype(F32),
-                speeds_of(profile_ref, k, levels),
-            )
-            for t, tile in enumerate(tiles):
-                buffer[k, side, 8 * t : 8 * t + 8] = tile
-                if not last:
-                    total[t] = total[t] + tile
-            if not last:
-                whole = jnp.concatenate(tiles, axis=0).astype(BF16)
-                (low_out if side == 0 else high_out)[k] = whole
-                rim_out[k, x : x + 1] = jnp.where(upper, tiles[0][0:1], tiles[-1][7:8])
+            toward = (flags_ref[k, x] & 1) != 0
+            rate = gust_ref[x] * profile_ref[k, 0:1]
+            rate = jnp.where(toward, 0.0, rate) if side == 0 else jnp.where(toward, rate, 0.0)
+            now = part_ref[k, side] + rate * outer(halo_ref, k)
+            buffer[k, side] = now
             if last:
                 copies.append(
                     pltpu.make_async_copy(
@@ -325,9 +331,12 @@
                     )
                 )
                 copies[-1].start()
+            else:
+                total = total + now
+                (low_out if side == 0 else high_out)[k] = now.astype(BF16)
+                rim_out[k, x : x + 1] = jnp.where(upper, now[0:1], now[width - 1 : width])
         if not last:
-            for t, tile in enumerate(total):
-                run_out[side, 8 * t : 8 * t + 8] = tile
+            run_out[side] = total
     for copy in copies:
         copy.wait()
 
@@ -436,8 +445,15 @@
             f"inner{step}",
             micros=1.0,
         )
+        part = call(
+            functools.partial(part_body, step),
+            shape(local_count, 2, width, levels),
+            (edge, inner, beside, *fixed),
+            f"part{step}",
+            micros=0.4,
+        )
         edge, to_low, to_high, rim_all, run_edge = call(
-            functools.partial(edge_body, step, False, 0),
+            functools.partial(edge_body, False, 0, inside),
             (
                 shape(local_count, 2, width, levels),
                 shape(local_count, width, levels, dtype=BF16),
@@ -445,7 +461,7 @@
                 rim,
                 shape(2, width, levels),
             ),
-            (edge, inner, low, high, beside, run_edge, *fixed, rim_inner)
+            (part, low, high, run_edge, *fixed[:3], rim_inner)
             + ((kernel_row,) if step == STEPS - 1 else ()),
             f"edge{step}",
             micros=0.4,
@@ -471,10 +487,17 @@
         "inner0",
         micros=1.0,
     )
+    part = call(
+        functools.partial(part_body, 0),
+        shape(local_count, 2, width, levels),
+        (edge, inner, beside, *fixed),
+        "part0",
+        micros=0.4,
+    )
     initial_adjoint, source_gradient, risk_map = call(
-        functools.partial(edge_body, 0, True, shards),
+        functools.partial(edge_body, True, shards, inside),
         (shape(*flags.shape), share, shape(rows, width)),
-        (edge, inner, low, high, beside, run_edge, *fixed, *pieces, inner_now, risk),
+        (part, low, high, run_edge, *fixed[:3], *pieces, inner_now, risk),
         "edge0",
         out_specs=(HBM,) * 3,
         scratch=[

time: 36.3 us -> 35.9 us (0.989)
  waiting for transfers between devices: 4.92 us -> 4.13 us
  Pallas kernels: 10.5 us -> 10.9 us
    ppermute x4, waiting for transfers between devices: 1.36 us -> 0.57 us  [exchange_x(): lax.ppermute(to_high, 'gx', forward)]
    pallas_call x13 -> x17, Pallas kernels: 10.5 us -> 10.9 us  [call(): pl.pallas_call(body, name=name, out_shape=outs, in_specs=in_specs or [VME...]
  transfers between devices with their start and end apart: 14 -> 14, of which waited for: 7 -> 5; matrix products, arithmetic and copies ran while one was open for 0% -> 0% of each run, Pallas kernels for 18% -> 21%
where the time goes in v5:
time: 35.9 us; the launch traced here: 35.8 us
  starting transfers between devices  20 us (56%)
  Pallas kernels  10.9 us (30%)
  waiting for transfers between devices  4.13 us (12%)
  between operations  0.74 us (2%)
    pallas_call x17, Pallas kernels, call(): pl.pallas_call(body, name=name, out_shape=outs, in_specs=in_specs or [VME...  10.9 us
    ppermute x4, starting transfers between devices, exchange_x(): lax.ppermute(to_low, 'gx', backward)  10.5 us
    ppermute x4, starting transfers between devices, exchange_x(): lax.ppermute(to_high, 'gx', forward)  4.94 us
    ppermute x2, starting transfers between devices, rotate(): lax.ppermute(block, axis, [(i, (i + hop) % count) for i in range(count)])  4.52 us
    ppermute x4, waiting for transfers between devices, swap_y(): return lax.ppermute(block, 'gy', [(0, 1), (1, 0)])  3.55 us
  transfers between devices with their start and end apart: 14, of which 5 were waited for; matrix products, arithmetic and copies ran while one was open for 0% of the time, Pallas kernels for 21%

profile of v5, /device:TPU:0, one launch (start us, length us, event | category | flops | bytes accessed | tf_op | source)
XLA Modules:
  0.0 35.8 jit_solution(10669944778929638082)
XLA Ops:
  0.6 1.7 %surface.1 = (f32[4,512]{1,0:T(4,128)S(1)}, f32[1,128]{1,0:T(1,128)S(1)}, s32[4,8,64,128]{3,2,1,0:T(8,128)S(1)}, f32[8,64,128]{2,1,0:T(8,128)S(1)}, f32[8,64,128]{2,1,0:T(8,128)S(1)}) custom-call(bf16[5,4,8,64,128]{4,3,2,1,0:T(8,128)(2,1)} %states_ref.3, f32[1,128]{1,0:T(1,128)} %bitcast.3, s32[4,8,64,128]{3,2,1,0:T(8,128)} %flags_ref.1, ...), custom_call_target="tpu_custom_call" | custom-call | flops 1000000 | bytes 3000000 | tf_op jit(solution)/shard_map/surface/pallas_call | solution.py:22
  2.3 3.0 %collective-permute-start = (f32[4,512]{1,0:T(4,128)S(1)}, f32[4,512]{1,0:T(4,128)S(1)}, u32[]{:S(2)}, u32[]{:S(2)}) collective-permute-start(f32[4,512]{1,0:T(4,128)S(1)} %get-tuple-element.49.refs_0_), channel_id=1, source_target_pairs={{0,2},{2,0},{1,3},{3,1},{4,6},{6,4},{5,7},{7,5},{8,10},{10,8},{9,1... | collective-permute-start | bytes 24584 | tf_op jit(solution)/shard_map/ppermute | solution.py:370
  5.4 2.2 %load.1 = (f32[4,3,128]{2,1,0:T(4,128)S(1)}, bf16[4,4,8,64,128]{4,3,2,1,0:T(8,128)(2,1)S(1)}, f32[1,512]{1,0:T(1,128)S(1)}) custom-call(s32[4]{0:T(128)S(1)} %copy-done, bf16[5,4,8,64,128]{4,3,2,1,0:T(8,128)(2,1)} %states_ref.3, s32[8,64]{1,0:T(8,128)} %mask_ref.1, f32[3,64,128]{2,1,0:T(8,128)} %bitcast.2, f32[1,128]{1,0:T(1,128)S(1)} %get-tuple-element.50._.kernel_ref.outs_1_), custom_call_target="tpu_custom_call" | custom-call | flops 1000000 | bytes 3000000 | tf_op jit(solution)/shard_map/load/pallas_call | solution.py:22
  7.6 0.1 moments.1
  7.7 1.6 %collective-permute-start.2 = (f32[4,64]{1,0:T(4,128)S(1)}, f32[4,64]{1,0:T(4,128)S(1)}, u32[]{:S(2)}, u32[]{:S(2)}) collective-permute-start(f32[4,64]{1,0:T(4,128)S(1)} %get-tuple-element.61), channel_id=1, source_target_pairs={{0,4},{4,8},{8,12},{12,0},{1,5},{5,9},{9,13},{13,1},{2,6},{6,10},{... | collective-permute-start | bytes 3080 | tf_op jit(solution)/shard_map/ppermute | solution.py:361
  9.3 2.2 %collective-permute-start.3 = (f32[4,64]{1,0:T(4,128)S(1)}, f32[4,64]{1,0:T(4,128)S(1)}, u32[]{:S(2)}, u32[]{:S(2)}) collective-permute-start(f32[4,64]{1,0:T(4,128)S(1)} %get-tuple-element.62), channel_id=1, source_target_pairs={{4,0},{8,4},{12,8},{0,12},{5,1},{9,5},{13,9},{1,13},{6,2},{10,6},{... | collective-permute-start | bytes 3080 | tf_op jit(solution)/shard_map/ppermute | solution.py:361
  11.6 0.4 final.1
  11.9 0.3 part3.1.part_ref
  12.2 0.9 %inner3.1 = (f32[4,6,64,128]{3,2,1,0:T(8,128)S(1)}, f32[4,8,128]{2,1,0:T(8,128)S(1)}, f32[6,64,128]{2,1,0:T(8,128)S(1)}) custom-call(f32[4,2,64,128]{3,2,1,0:T(8,128)S(1)} %get-tuple-element.54.edge_ref, f32[4,6,64,128]{3,2,1,0:T(8,128)S(1)} %get-tuple-element.55.inner_ref, f32[4,8,128]{2,1,0:T(8,128)S(1)} %get-tuple-element.56.beside_ref, ...), custom_call_target="tpu_custom_call" | custom-call | flops 1000000 | bytes 3000000 | tf_op jit(solution)/shard_map/inner3/pallas_call | solution.py:22
  13.2 0.2 edge3.1
  13.5 1.3 %collective-permute-start.5 = (bf16[4,64,128]{2,1,0:T(8,128)(2,1)S(1)}, bf16[4,64,128]{2,1,0:T(8,128)(2,1)S(1)}, u32[]{:S(2)}, u32[]{:S(2)}) collective-permute-start(bf16[4,64,128]{2,1,0:T(8,128)(2,1)S(1)} %get-tuple-element.69), channel_id=1, source_target_pairs={{0,4},{4,8},{8,12},{12,0},{1,5},{5,9},{9,13},{13,1},{2,6},{6,10},{... | collective-permute-start | bytes 196616 | tf_op jit(solution)/shard_map/ppermute | solution.py:361
  14.8 2.6 %collective-permute-start.6 = (bf16[4,64,128]{2,1,0:T(8,128)(2,1)S(1)}, bf16[4,64,128]{2,1,0:T(8,128)(2,1)S(1)}, u32[]{:S(2)}, u32[]{:S(2)}) collective-permute-start(bf16[4,64,128]{2,1,0:T(8,128)(2,1)S(1)} %get-tuple-element.70), channel_id=1, source_target_pairs={{4,0},{8,4},{12,8},{0,12},{5,1},{9,5},{13,9},{1,13},{6,2},{10,6},{... | collective-permute-start | bytes 196616 | tf_op jit(solution)/shard_map/ppermute | solution.py:361
  17.3 1.2 %collective-permute-done.4.beside_ref = f32[4,8,128]{2,1,0:T(8,128)S(1)} collective-permute-done((f32[4,8,128]{2,1,0:T(8,128)S(1)}, f32[4,8,128]{2,1,0:T(8,128)S(1)}, u32[]{:S(2)}, u32[]{:S(2)}) %collective-permute-start.4) | collective-permute-done | bytes 16416 | tf_op jit(solution)/shard_map/ppermute | solution.py:365
  18.5 0.3 part2.1.part_ref
  18.8 1.0 %inner2.1 = (f32[4,6,64,128]{3,2,1,0:T(8,128)S(1)}, f32[4,8,128]{2,1,0:T(8,128)S(1)}, f32[6,64,128]{2,1,0:T(8,128)S(1)}) custom-call(f32[4,2,64,128]{3,2,1,0:T(8,128)S(1)} %get-tuple-element.66.edge_ref, f32[4,6,64,128]{3,2,1,0:T(8,128)S(1)} %get-tuple-element.67.inner_ref, f32[4,8,128]{2,1,0:T(8,128)S(1)} %collective-permute-done.4.beside_ref, ...), custom_call_target="tpu_custom_call" | custom-call | flops 1000000 | bytes 3000000 | tf_op jit(solution)/shard_map/inner2/pallas_call | solution.py:22
  19.8 0.3 collective-permute-done.5.low_ref
  20.1 0.1 edge2.1
  20.2 1.1 %collective-permute-start.8 = (bf16[4,64,128]{2,1,0:T(8,128)(2,1)S(1)}, bf16[4,64,128]{2,1,0:T(8,128)(2,1)S(1)}, u32[]{:S(2)}, u32[]{:S(2)}) collective-permute-start(bf16[4,64,128]{2,1,0:T(8,128)(2,1)S(1)} %get-tuple-element.77), channel_id=1, source_target_pairs={{0,4},{4,8},{8,12},{12,0},{1,5},{5,9},{9,13},{13,1},{2,6},{6,10},{... | collective-permute-start | bytes 196616 | tf_op jit(solution)/shard_map/ppermute | solution.py:361
  21.2 2.8 %collective-permute-start.9 = (bf16[4,64,128]{2,1,0:T(8,128)(2,1)S(1)}, bf16[4,64,128]{2,1,0:T(8,128)(2,1)S(1)}, u32[]{:S(2)}, u32[]{:S(2)}) collective-permute-start(bf16[4,64,128]{2,1,0:T(8,128)(2,1)S(1)} %get-tuple-element.78), channel_id=1, source_target_pairs={{4,0},{8,4},{12,8},{0,12},{5,1},{9,5},{13,9},{1,13},{6,2},{10,6},{... | collective-permute-start | bytes 196616 | tf_op jit(solution)/shard_map/ppermute | solution.py:361
  24.0 1.2 %collective-permute-done.7.beside_ref = f32[4,8,128]{2,1,0:T(8,128)S(1)} collective-permute-done((f32[4,8,128]{2,1,0:T(8,128)S(1)}, f32[4,8,128]{2,1,0:T(8,128)S(1)}, u32[]{:S(2)}, u32[]{:S(2)}) %collective-permute-start.7) | collective-permute-done | bytes 16416 | tf_op jit(solution)/shard_map/ppermute | solution.py:365
  25.2 0.3 part1.1.part_ref
  25.5 0.9 %inner1.1 = (f32[4,6,64,128]{3,2,1,0:T(8,128)S(1)}, f32[4,8,128]{2,1,0:T(8,128)S(1)}, f32[6,64,128]{2,1,0:T(8,128)S(1)}) custom-call(f32[4,2,64,128]{3,2,1,0:T(8,128)S(1)} %get-tuple-element.74.edge_ref, f32[4,6,64,128]{3,2,1,0:T(8,128)S(1)} %get-tuple-element.75.inner_ref, f32[4,8,128]{2,1,0:T(8,128)S(1)} %collective-permute-done.7.beside_ref, ...), custom_call_target="tpu_custom_call" | custom-call | flops 1000000 | bytes 3000000 | tf_op jit(solution)/shard_map/inner1/pallas_call | solution.py:22
  26.5 0.2 collective-permute-done.8.low_ref
  26.7 0.1 edge1.1
  26.9 1.5 %collective-permute-start.13 = (f32[4,64,128]{2,1,0:T(8,128)S(1)}, f32[4,64,128]{2,1,0:T(8,128)S(1)}, u32[]{:S(2)}, u32[]{:S(2)}) collective-permute-start(f32[4,64,128]{2,1,0:T(8,128)S(1)} %get-tuple-element.90), channel_id=1, source_target_pairs={{0,2},{2,0},{1,3},{3,1},{4,6},{6,4},{5,7},{7,5},{8,10},{10,8},{9,1... | collective-permute-start | bytes 393224 | tf_op jit(solution)/shard_map/ppermute | solution.py:370
  28.4 0.9 %collective-permute-start.11 = (bf16[4,64,128]{2,1,0:T(8,128)(2,1)S(1)}, bf16[4,64,128]{2,1,0:T(8,128)(2,1)S(1)}, u32[]{:S(2)}, u32[]{:S(2)}) collective-permute-start(bf16[4,64,128]{2,1,0:T(8,128)(2,1)S(1)} %get-tuple-element.85), channel_id=1, source_target_pairs={{0,4},{4,8},{8,12},{12,0},{1,5},{5,9},{9,13},{13,1},{2,6},{6,10},{... | collective-permute-start | bytes 196616 | tf_op jit(solution)/shard_map/ppermute | solution.py:361
  29.3 2.9 %collective-permute-start.12 = (bf16[4,64,128]{2,1,0:T(8,128)(2,1)S(1)}, bf16[4,64,128]{2,1,0:T(8,128)(2,1)S(1)}, u32[]{:S(2)}, u32[]{:S(2)}) collective-permute-start(bf16[4,64,128]{2,1,0:T(8,128)(2,1)S(1)} %get-tuple-element.86), channel_id=1, source_target_pairs={{4,0},{8,4},{12,8},{0,12},{5,1},{9,5},{13,9},{1,13},{6,2},{10,6},{... | collective-permute-start | bytes 196616 | tf_op jit(solution)/shard_map/ppermute | solution.py:361
  32.2 1.2 %collective-permute-done.10.beside_ref = f32[4,8,128]{2,1,0:T(8,128)S(1)} collective-permute-done((f32[4,8,128]{2,1,0:T(8,128)S(1)}, f32[4,8,128]{2,1,0:T(8,128)S(1)}, u32[]{:S(2)}, u32[]{:S(2)}) %collective-permute-start.10) | collective-permute-done | bytes 16416 | tf_op jit(solution)/shard_map/ppermute | solution.py:365
  33.4 0.3 part0.1.part_ref
  33.7 0.9 %inner0.1.outs_2_ = f32[4,6,64,128]{3,2,1,0:T(8,128)S(1)} custom-call(f32[4,2,64,128]{3,2,1,0:T(8,128)S(1)} %get-tuple-element.82.edge_ref, f32[4,6,64,128]{3,2,1,0:T(8,128)S(1)} %get-tuple-element.83.inner_ref, f32[4,8,128]{2,1,0:T(8,128)S(1)} %collective-permute-done.10.beside_ref, f32[6,64,128]{2,1,0:T(8,128)S(1)} %get-tuple-element.88.inner_ref.run_ref, ...), custom_call_target="tpu_custom_call" | custom-call | flops 1000000 | bytes 3000000 | tf_op jit(solution)/shard_map/inner0/pallas_call | solution.py:22
  34.6 0.0 collective-permute-done.11.low_ref
  34.6 1.1 %edge0.1 = (f32[4,8,64,128]{3,2,1,0:T(8,128)}, f32[4,64,128]{2,1,0:T(8,128)}, f32[8,64]{1,0:T(8,128)}) custom-call(f32[4,2,64,128]{3,2,1,0:T(8,128)S(1)} %part0.1.part_ref, bf16[4,64,128]{2,1,0:T(8,128)(2,1)S(1)} %collective-permute-done.11.low_ref, bf16[4,64,128]{2,1,0:T(8,128)(2,1)S(1)} %collective-permute-done.12.high_ref, ...), custom_call_target="tpu_custom_call" | custom-call | flops 400000 | bytes 1200000 | tf_op jit(solution)/shard_map/edge0/pallas_call | solution.py:22
  (15 shorter events, 0.1 us)
Async XLA Ops:
  0.6 4.7 %copy-start = (s32[4]{0:T(128)S(1)}, s32[4]{0:T(128)}, u32[]{:S(2)}) copy-start(s32[4]{0:T(128)} %seeds_ref.1) | copy-start | bytes 52
  2.3 5.2 %collective-permute-start = (f32[4,512]{1,0:T(4,128)S(1)}, f32[4,512]{1,0:T(4,128)S(1)}, u32[]{:S(2)}, u32[]{:S(2)}) collective-permute-start(f32[4,512]{1,0:T(4,128)S(1)} %get-tuple-element.49.refs_0_), channel_id=1, source_target_pairs={{0,2},{2,0},{1,3},{3,1},{4,6},{6,4},{5,7},{7,5},{8,10},{10,8},{9,1... | collective-permute-start | bytes 24584 | tf_op jit(solution)/shard_map/ppermute | solution.py:370
  7.7 3.9 %collective-permute-start.1 = (f32[4,512]{1,0:T(4,128)S(1)}, f32[4,512]{1,0:T(4,128)S(1)}, u32[]{:S(2)}, u32[]{:S(2)}) collective-permute-start(f32[4,512]{1,0:T(4,128)S(1)} %get-tuple-element.53.sens_ref), channel_id=1, source_target_pairs={{0,1},{1,0},{2,3},{3,2},{4,5},{5,4},{6,7},{7,6},{8,9},{9,8},{10,11... | collective-permute-start | bytes 24584 | tf_op jit(solution)/shard_map/ppermute | solution.py:365
  7.7 5.5 %collective-permute-start.2 = (f32[4,64]{1,0:T(4,128)S(1)}, f32[4,64]{1,0:T(4,128)S(1)}, u32[]{:S(2)}, u32[]{:S(2)}) collective-permute-start(f32[4,64]{1,0:T(4,128)S(1)} %get-tuple-element.61), channel_id=1, source_target_pairs={{0,4},{4,8},{8,12},{12,0},{1,5},{5,9},{9,13},{13,1},{2,6},{6,10},{... | collective-permute-start | bytes 3080 | tf_op jit(solution)/shard_map/ppermute | solution.py:361
  9.3 3.9 %collective-permute-start.3 = (f32[4,64]{1,0:T(4,128)S(1)}, f32[4,64]{1,0:T(4,128)S(1)}, u32[]{:S(2)}, u32[]{:S(2)}) collective-permute-start(f32[4,64]{1,0:T(4,128)S(1)} %get-tuple-element.62), channel_id=1, source_target_pairs={{4,0},{8,4},{12,8},{0,12},{5,1},{9,5},{13,9},{1,13},{6,2},{10,6},{... | collective-permute-start | bytes 3080 | tf_op jit(solution)/shard_map/ppermute | solution.py:361
  13.5 6.6 %collective-permute-start.5 = (bf16[4,64,128]{2,1,0:T(8,128)(2,1)S(1)}, bf16[4,64,128]{2,1,0:T(8,128)(2,1)S(1)}, u32[]{:S(2)}, u32[]{:S(2)}) collective-permute-start(bf16[4,64,128]{2,1,0:T(8,128)(2,1)S(1)} %get-tuple-element.69), channel_id=1, source_target_pairs={{0,4},{4,8},{8,12},{12,0},{1,5},{5,9},{9,13},{13,1},{2,6},{6,10},{... | collective-permute-start | bytes 196616 | tf_op jit(solution)/shard_map/ppermute | solution.py:361
  14.8 5.3 %collective-permute-start.6 = (bf16[4,64,128]{2,1,0:T(8,128)(2,1)S(1)}, bf16[4,64,128]{2,1,0:T(8,128)(2,1)S(1)}, u32[]{:S(2)}, u32[]{:S(2)}) collective-permute-start(bf16[4,64,128]{2,1,0:T(8,128)(2,1)S(1)} %get-tuple-element.70), channel_id=1, source_target_pairs={{4,0},{8,4},{12,8},{0,12},{5,1},{9,5},{13,9},{1,13},{6,2},{10,6},{... | collective-permute-start | bytes 196616 | tf_op jit(solution)/shard_map/ppermute | solution.py:361
  17.3 1.2 %collective-permute-start.4 = (f32[4,8,128]{2,1,0:T(8,128)S(1)}, f32[4,8,128]{2,1,0:T(8,128)S(1)}, u32[]{:S(2)}, u32[]{:S(2)}) collective-permute-start(f32[4,8,128]{2,1,0:T(8,128)S(1)} %get-tuple-element.68), channel_id=1, source_target_pairs={{0,1},{1,0},{2,3},{3,2},{4,5},{5,4},{6,7},{7,6},{8,9},{9,8},{10,11... | collective-permute-start | bytes 49160 | tf_op jit(solution)/shard_map/ppermute | solution.py:365
  20.2 6.6 %collective-permute-start.8 = (bf16[4,64,128]{2,1,0:T(8,128)(2,1)S(1)}, bf16[4,64,128]{2,1,0:T(8,128)(2,1)S(1)}, u32[]{:S(2)}, u32[]{:S(2)}) collective-permute-start(bf16[4,64,128]{2,1,0:T(8,128)(2,1)S(1)} %get-tuple-element.77), channel_id=1, source_target_pairs={{0,4},{4,8},{8,12},{12,0},{1,5},{5,9},{9,13},{13,1},{2,6},{6,10},{... | collective-permute-start | bytes 196616 | tf_op jit(solution)/shard_map/ppermute | solution.py:361
  21.2 5.5 %collective-permute-start.9 = (bf16[4,64,128]{2,1,0:T(8,128)(2,1)S(1)}, bf16[4,64,128]{2,1,0:T(8,128)(2,1)S(1)}, u32[]{:S(2)}, u32[]{:S(2)}) collective-permute-start(bf16[4,64,128]{2,1,0:T(8,128)(2,1)S(1)} %get-tuple-element.78), channel_id=1, source_target_pairs={{4,0},{8,4},{12,8},{0,12},{5,1},{9,5},{13,9},{1,13},{6,2},{10,6},{... | collective-permute-start | bytes 196616 | tf_op jit(solution)/shard_map/ppermute | solution.py:361
  24.0 1.2 %collective-permute-start.7 = (f32[4,8,128]{2,1,0:T(8,128)S(1)}, f32[4,8,128]{2,1,0:T(8,128)S(1)}, u32[]{:S(2)}, u32[]{:S(2)}) collective-permute-start(f32[4,8,128]{2,1,0:T(8,128)S(1)} %get-tuple-element.76), channel_id=1, source_target_pairs={{0,1},{1,0},{2,3},{3,2},{4,5},{5,4},{6,7},{7,6},{8,9},{9,8},{10,11... | collective-permute-start | bytes 49160 | tf_op jit(solution)/shard_map/ppermute | solution.py:365
  26.9 7.8 %collective-permute-start.13 = (f32[4,64,128]{2,1,0:T(8,128)S(1)}, f32[4,64,128]{2,1,0:T(8,128)S(1)}, u32[]{:S(2)}, u32[]{:S(2)}) collective-permute-start(f32[4,64,128]{2,1,0:T(8,128)S(1)} %get-tuple-element.90), channel_id=1, source_target_pairs={{0,2},{2,0},{1,3},{3,1},{4,6},{6,4},{5,7},{7,5},{8,10},{10,8},{9,1... | collective-permute-start | bytes 393224 | tf_op jit(solution)/shard_map/ppermute | solution.py:370
  28.4 6.3 %collective-permute-start.11 = (bf16[4,64,128]{2,1,0:T(8,128)(2,1)S(1)}, bf16[4,64,128]{2,1,0:T(8,128)(2,1)S(1)}, u32[]{:S(2)}, u32[]{:S(2)}) collective-permute-start(bf16[4,64,128]{2,1,0:T(8,128)(2,1)S(1)} %get-tuple-element.85), channel_id=1, source_target_pairs={{0,4},{4,8},{8,12},{12,0},{1,5},{5,9},{9,13},{13,1},{2,6},{6,10},{... | collective-permute-start | bytes 196616 | tf_op jit(solution)/shard_map/ppermute | solution.py:361
  29.3 5.3 %collective-permute-start.12 = (bf16[4,64,128]{2,1,0:T(8,128)(2,1)S(1)}, bf16[4,64,128]{2,1,0:T(8,128)(2,1)S(1)}, u32[]{:S(2)}, u32[]{:S(2)}) collective-permute-start(bf16[4,64,128]{2,1,0:T(8,128)(2,1)S(1)} %get-tuple-element.86), channel_id=1, source_target_pairs={{4,0},{8,4},{12,8},{0,12},{5,1},{9,5},{13,9},{1,13},{6,2},{10,6},{... | collective-permute-start | bytes 196616 | tf_op jit(solution)/shard_map/ppermute | solution.py:361
  32.2 1.2 %collective-permute-start.10 = (f32[4,8,128]{2,1,0:T(8,128)S(1)}, f32[4,8,128]{2,1,0:T(8,128)S(1)}, u32[]{:S(2)}, u32[]{:S(2)}) collective-permute-start(f32[4,8,128]{2,1,0:T(8,128)S(1)} %get-tuple-element.84._), channel_id=1, source_target_pairs={{0,1},{1,0},{2,3},{3,2},{4,5},{5,4},{6,7},{7,6},{8,9},{9,8},{10,11... | collective-permute-start | bytes 49160 | tf_op jit(solution)/shard_map/ppermute | solution.py:365
